TPU v7x, 256 devices: a whole 4x4x8 slice. The times are simulated.
256 devices in a mesh: mem: 64 (over x, z, core), reg: 4 (over y).
Axes of the slice: x: 4, y: 4, z: 8, core: 2. Of those that a mesh axis runs over, the one named last changes fastest.
Arguments:
- background: bfloat16 [256, 4, 512, 128], P('mem', 'reg'), may hold values from -6 to 6
- obs_value: float32 [128, 8, 512], P('mem', 'reg'), may hold values from -6 to 6
- obs_error: float32 [128, 8, 512], P('mem', 'reg'), may hold values from 1 to 4
- obs_patch: int32 [128, 8, 512], P('mem', 'reg'), may hold values from 0 to 7
- obs_variable: int32 [128, 8, 512], P('mem', 'reg'), may hold values from 0 to 127
- obs_count: int32 [128, 8], P('mem', 'reg'), may hold values from 1 to 512
- patch_corners: int32 [4, 512, 4], P('reg', 'mem'), may hold values from 0 to 8, as said below
- interp_weights: float32 [4, 512, 4], P('reg', 'mem'), may hold values from 0 to 1, as said below
Outputs:
- analysis: bfloat16 [256, 4, 512, 128], P('mem', 'reg')
Inputs may be any that keep to these rules, and one draw needn't show every extreme that they name: `patch_corners`: each patch's four numbers are base, base + 3, base + 1, base + 4 with base = i * 3 + e, i below 2 and e below 2; in the last region e is below 1. `interp_weights`: the four weights of a patch are non-negative and sum to one.
All inputs are finite; a program needn't handle non-finite values.
Results may differ from a plain program's by a relative error of at most 0.006.
Values may be sent and summed in bfloat16 or wider, within the bound.
No kernel may reach another device: no remote copies, remote signals or barrier semaphores. Data moves between devices by JAX's collectives and lax.ppermute only.
A program may use at most 64 MiB of HBM per device.

v0:
```python
import jax
import jax.numpy as jnp
from jax import lax
from jax.sharding import PartitionSpec as P

NS_ITERS = 4


def passed_along(block, axis, distance):
    devices = range(lax.axis_size(axis))
    route = [((i - distance) % len(devices), i) for i in devices]
    return lax.ppermute(block, axis, route)


def passed_along_2(value, axis, steps):
    count = lax.axis_size(axis)
    leading, last = (max(0, -steps), min(count, count - steps))
    return lax.ppermute(value, axis, [(source, source + steps) for source in range(leading, last)])


def analysis_weights(gram, obs_pert, obs_weight, innovation, members):
    identity = jnp.eye(members, dtype=jnp.float32)
    system = (members - 1.0) * identity + gram
    scaling = jnp.trace(system, axis1=1, axis2=2) / members
    iterate = system / scaling[:, None, None]
    inverse = jnp.broadcast_to(identity, system.shape)
    for iteration in range(NS_ITERS):
        factor = 1.5 * identity - 0.5 * jnp.einsum(
            "nij,njk->nik", inverse, iterate, precision=lax.Precision.HIGHEST
        )
        new_iterate = jnp.einsum("nij,njk->nik", iterate, factor, precision=lax.Precision.HIGHEST)
        inverse = jnp.einsum("nij,njk->nik", factor, inverse, precision=lax.Precision.HIGHEST)
        iterate = new_iterate
    projected = jnp.einsum(
        "kns,ns->nk", obs_pert, obs_weight * innovation, precision=lax.Precision.HIGHEST
    )
    once = jnp.einsum("nij,nj->ni", inverse, projected, precision=lax.Precision.HIGHEST)
    mean_weight = (
        jnp.einsum("nij,nj->ni", inverse, once, precision=lax.Precision.HIGHEST) / scaling[:, None]
    )
    spread = jnp.sqrt((members - 1.0) / scaling)[:, None, None] * inverse
    return (spread + mean_weight[:, :, None]).astype(jnp.bfloat16)


def per_device(
    background,
    obs_value,
    obs_error,
    obs_patch,
    obs_variable,
    obs_count,
    patch_corners,
    interp_weights,
):
    regrouped = lax.all_to_all(background, "mem", split_axis=2, concat_axis=0, tiled=True)
    ensemble = regrouped[:, 0]
    members, patches, fields = ensemble.shape
    rows_ca, cols_cb, slot_count = obs_value.shape
    points = rows_ca * cols_cb
    centre = jnp.mean(ensemble.astype(jnp.float32), axis=0)
    perturb = (ensemble.astype(jnp.float32) - centre).astype(jnp.bfloat16)
    columns = ensemble.reshape(members, patches * fields)
    position = (obs_patch * fields + obs_variable).reshape(-1)
    observed = (
        jnp.take(columns, position, axis=1).astype(jnp.float32).reshape(members, points, slot_count)
    )
    obs_mean = jnp.mean(observed, axis=0)
    obs_pert = observed - obs_mean
    innovation = obs_value.reshape(points, slot_count) - obs_mean
    counts = obs_count.reshape(points)
    slot_index = jnp.arange(slot_count)
    obs_weight = jnp.where(
        slot_index[None, :] < counts[:, None], 1.0 / obs_error.reshape(points, slot_count), 0.0
    )
    weighted = obs_pert * obs_weight[None]
    gram = jnp.einsum("kns,jns->nkj", weighted, obs_pert, precision=lax.Precision.HIGHEST)
    weights = analysis_weights(gram, obs_pert, obs_weight, innovation, members)
    weights = weights.reshape(rows_ca, cols_cb, members, members)
    below = passed_along(weights[0:1], "mem", -1)
    with_rows = jnp.concatenate([weights, below], axis=0)
    beside = passed_along_2(with_rows[:, 0:1], "reg", -1)
    extended = jnp.concatenate([with_rows, beside], axis=1)
    weight_points = extended.reshape(-1, members, members)
    group = max(1, patches // 8)
    turns = patches // group
    corner_blocks = patch_corners[0].reshape(turns, group, 4)
    coeff_blocks = interp_weights[0].reshape(turns, group, 4)
    pert_blocks = jnp.transpose(perturb.reshape(members, turns, group, fields), (1, 0, 2, 3))

    def update_block(packed):
        corner_part, coeff_part, pert_part = packed
        chosen = weight_points[corner_part]
        product = jnp.einsum(
            "gcjk,jgv->gckv", chosen, pert_part, preferred_element_type=jnp.float32
        )
        return jnp.einsum("gc,gckv->kgv", coeff_part, product, precision=lax.Precision.HIGHEST)

    increment_blocks = lax.map(update_block, (corner_blocks, coeff_blocks, pert_blocks))
    increment = jnp.transpose(increment_blocks, (1, 0, 2, 3)).reshape(members, patches, fields)
    analysis = (centre[None] + increment).astype(jnp.bfloat16)
    return lax.all_to_all(analysis[:, None], "mem", split_axis=0, concat_axis=2, tiled=True)


def solution(mesh):
    placed = (
        P("mem", "reg", None, None),
        P("mem", "reg", None),
        P("mem", "reg", None),
        P("mem", "reg", None),
        P("mem", "reg", None),
        P("mem", "reg"),
        P("reg", "mem", None),
        P("reg", "mem", None),
    )
    return jax.shard_map(
        per_device,
        mesh=mesh,
        in_specs=placed,
        out_specs=P("mem", "reg", None, None),
        check_vma=False,
    )
```

profile of v0, /device:TPU:1, one launch (start us, length us, event | category | flops | bytes accessed | tf_op | source)
XLA Modules:
  0.0 148.5 jit_solution(2711029778452874093)
XLA Ops:
  0.0 2.3 %copy.55 = bf16[4,1,512,128]{3,0,1,2:T(4,128)(2,1)} copy(bf16[4,1,512,128]{3,2,1,0:T(8,128)(2,1)} %param.10) | data formatting | bytes 1048576 | tf_op args[0]
  2.3 13.0 %all-to-all-start = ((bf16[4,1,512,128]{3,0,1,2:T(4,128)(2,1)}), bf16[4,1,512,128]{3,0,1,2:T(4,128)(2,1)S(1)}, u32[]{:S(2)}, u32[]{:S(2)}) async-start(bf16[4,1,512,128]{3,0,1,2:T(4,128)(2,1)} %copy.55), calls=%async_computation | async-start | bytes 1048576 | tf_op jit(solution)/shard_map/all_to_all | solution.py:55
  15.3 0.7 fusion.29
  16.3 0.7 fusion.31
  17.1 15.5 %all-to-all-done = bf16[4,1,512,128]{3,0,1,2:T(4,128)(2,1)S(1)} async-done(((bf16[4,1,512,128]{3,0,1,2:T(4,128)(2,1)}), bf16[4,1,512,128]{3,0,1,2:T(4,128)(2,1)S(1)}, u32[]{:S(2)}, u32[]{:S(2)}) %all-to-all-start) | async-done | bytes 524320 | tf_op jit(solution)/shard_map/all_to_all | solution.py:55
  33.1 7.5 %gather_fusion.1 = bf16[2048,256]{1,0:T(8,128)(2,1)S(1)} fusion(bf16[256,1024]{0,1:T(8,128)(2,1)S(1)} %copy.58, s32[2048]{0:T(1024)S(1)} %broadcast_clamp_fusion), kind=kCustom, calls=%fused_computation.1 | custom fusion | bytes 2105344 | tf_op jit(solution)/shard_map/jit(_take)/gather | solution.py:65
  40.6 0.7 convert_reduce_fusion
  41.4 1.3 copy.59
  42.8 4.2 %select_reduce_fusion = (f32[4]{0:T(128)S(1)}, f32[4,256,256]{2,1,0:T(8,128)S(1)}) fusion(pred[256,256]{1,0:T(8,128)(4,1)S(1)} %iota_compare_fusion, f32[4,512]{1,0:T(4,128)S(1)} %div.57, bf16[256,4,512]{2,0,1:T(8,128)(2,1)} %copy.59, pred[4,512]{1,0:T(4,128)(4,1)S(1)} %compare_and_fusion.1, f32[4,512]{1,0:T(4,128)S(1)} %get-tuple-element.87, ...), kind=kOutput, calls=%fused_computation.35 | convolution fusion | flops 1615069184 | bytes 2443280 | tf_op jit(solution)/shard_map/kns,jns->nkj/dot_general | solution.py:76
  47.1 1.2 fusion.18
  48.3 1.2 fusion.32
  49.5 1.1 fusion.24
  50.6 1.2 fusion.17
  51.8 1.1 fusion.44
  52.9 1.1 fusion.43
  54.1 1.2 fusion.16
  55.3 1.4 fusion.45
  56.6 1.1 fusion.46
  57.9 2.0 %fusion.11 = f32[4,1,256]{2,1,0:T(1,128)S(1)} fusion(f32[4,512]{1,0:T(4,128)S(1)} %div.57, bf16[256,4,512]{2,0,1:T(8,128)(2,1)S(1)} %copy-done.2, pred[4,512]{1,0:T(4,128)(4,1)S(1)} %compare_and_fusion.1, f32[4,512,1]{1,0,2:T(4,128)S(1)} %get-tuple-element.86), kind=kOutput, calls=%fused_computation.19 | convolution fusion | flops 7864320 | bytes 1071104 | tf_op jit(solution)/shard_map/kns,ns->nk/dot_general | solution.py:34
  59.9 1.2 fusion.15
  61.1 1.1 fusion.47
  62.3 1.0 fusion.37
  63.3 1.0 fusion.35
  64.3 0.2 add_convert_fusion
  64.6 0.3 collective-permute-start
  65.2 0.3 convert_reduce_fusion.1
  65.5 5.0 %collective-permute-done = bf16[1,2,256,256]{3,2,1,0:T(8,128)(2,1)S(1)} collective-permute-done((bf16[1,2,256,256]{3,2,1,0:T(8,128)(2,1)S(1)}, bf16[1,2,256,256]{3,2,1,0:T(8,128)(2,1)S(1)}, u32[]{:S(2)}, u32[]{:S(2)}) %collective-permute-start) | collective-permute-done | bytes 262176 | tf_op jit(solution)/shard_map/ppermute | solution.py:12
  70.5 1.3 collective-permute-start.1
  72.0 10.9 %collective-permute-done.1 = bf16[3,1,256,256]{3,2,1,0:T(8,128)(2,1)S(1)} collective-permute-done((bf16[3,1,256,256]{3,2,1,0:T(8,128)(2,1)S(1)}, bf16[3,1,256,256]{3,2,1,0:T(8,128)(2,1)S(1)}, u32[]{:S(2)}, u32[]{:S(2)}) %collective-permute-start.1) | collective-permute-done | bytes 393248 | tf_op jit(solution)/shard_map/ppermute | solution.py:18
  83.0 41.1 %while.10 = (s32[]{:T(128)}, f32[8,256,1,128]{3,0,1,2:T(8,128)S(1)}, s32[8,1,4]{2,1,0:T(1,128)S(1)}, bf16[9,256,256]{2,1,0:T(8,128)(2,1)S(1)}, bf16[8,256,1,128]...) while((s32[]{:T(128)}, f32[8,256,1,128]{3,0,1,2:T(8,128)S(1)}, ...), condition=%wide.region_4.5_spmd, body=%wide.region_3.4_spmd.sunk | while | flops 68682768 | bytes 3084973 | solution.py:98
  83.1 0.6 gather_fusion
  83.7 0.3 fusion.80
  84.0 1.3 convolution_bitcast_fusion.2
  85.3 2.8 %dynamic_update_slice.5 = f32[8,256,1,128]{3,0,1,2:T(8,128)S(1)} dynamic-update-slice(f32[8,256,1,128]{3,0,1,2:T(8,128)S(1)} %get-tuple-element.140, f32[1,256,1,128]{3,0,1,2:T(1,128)S(1)} %convolution_bitcast_fusion.2, s32[]{:T(128)S(6)} %copy.109, s32[]{:T(128)} %constant.31.clone.1..sunk, s32[]{:T(128)} %constant.31.clone.1..sunk, s32[]{:T(128)} %constant.31.clone.1..sunk) | dynamic-update-slice | bytes 262148 | tf_op jit(solution)/shard_map/while/body/jit(dynamic_update_index_in_dim)/dynamic_update_slice | solution.py:98
  88.2 0.6 gather_fusion
  88.8 0.3 fusion.80
  89.1 1.3 convolution_bitcast_fusion.2
  90.5 2.8 %dynamic_update_slice.5 = f32[8,256,1,128]{3,0,1,2:T(8,128)S(1)} dynamic-update-slice(f32[8,256,1,128]{3,0,1,2:T(8,128)S(1)} %get-tuple-element.140, f32[1,256,1,128]{3,0,1,2:T(1,128)S(1)} %convolution_bitcast_fusion.2, s32[]{:T(128)S(6)} %copy.109, s32[]{:T(128)} %constant.31.clone.1..sunk, s32[]{:T(128)} %constant.31.clone.1..sunk, s32[]{:T(128)} %constant.31.clone.1..sunk) | dynamic-update-slice | bytes 262148 | tf_op jit(solution)/shard_map/while/body/jit(dynamic_update_index_in_dim)/dynamic_update_slice | solution.py:98
  93.3 0.6 gather_fusion
  93.9 0.3 fusion.80
  94.3 1.3 convolution_bitcast_fusion.2
  95.6 2.8 %dynamic_update_slice.5 = f32[8,256,1,128]{3,0,1,2:T(8,128)S(1)} dynamic-update-slice(f32[8,256,1,128]{3,0,1,2:T(8,128)S(1)} %get-tuple-element.140, f32[1,256,1,128]{3,0,1,2:T(1,128)S(1)} %convolution_bitcast_fusion.2, s32[]{:T(128)S(6)} %copy.109, s32[]{:T(128)} %constant.31.clone.1..sunk, s32[]{:T(128)} %constant.31.clone.1..sunk, s32[]{:T(128)} %constant.31.clone.1..sunk) | dynamic-update-slice | bytes 262148 | tf_op jit(solution)/shard_map/while/body/jit(dynamic_update_index_in_dim)/dynamic_update_slice | solution.py:98
  98.5 0.6 gather_fusion
  99.1 0.3 fusion.80
  99.4 1.3 convolution_bitcast_fusion.2
  100.8 2.8 %dynamic_update_slice.5 = f32[8,256,1,128]{3,0,1,2:T(8,128)S(1)} dynamic-update-slice(f32[8,256,1,128]{3,0,1,2:T(8,128)S(1)} %get-tuple-element.140, f32[1,256,1,128]{3,0,1,2:T(1,128)S(1)} %convolution_bitcast_fusion.2, s32[]{:T(128)S(6)} %copy.109, s32[]{:T(128)} %constant.31.clone.1..sunk, s32[]{:T(128)} %constant.31.clone.1..sunk, s32[]{:T(128)} %constant.31.clone.1..sunk) | dynamic-update-slice | bytes 262148 | tf_op jit(solution)/shard_map/while/body/jit(dynamic_update_index_in_dim)/dynamic_update_slice | solution.py:98
  103.6 0.6 gather_fusion
  104.2 0.3 fusion.80
  104.6 1.3 convolution_bitcast_fusion.2
  105.9 2.8 %dynamic_update_slice.5 = f32[8,256,1,128]{3,0,1,2:T(8,128)S(1)} dynamic-update-slice(f32[8,256,1,128]{3,0,1,2:T(8,128)S(1)} %get-tuple-element.140, f32[1,256,1,128]{3,0,1,2:T(1,128)S(1)} %convolution_bitcast_fusion.2, s32[]{:T(128)S(6)} %copy.109, s32[]{:T(128)} %constant.31.clone.1..sunk, s32[]{:T(128)} %constant.31.clone.1..sunk, s32[]{:T(128)} %constant.31.clone.1..sunk) | dynamic-update-slice | bytes 262148 | tf_op jit(solution)/shard_map/while/body/jit(dynamic_update_index_in_dim)/dynamic_update_slice | solution.py:98
  108.8 0.6 gather_fusion
  109.4 0.3 fusion.80
  109.7 1.3 convolution_bitcast_fusion.2
  111.0 2.8 %dynamic_update_slice.5 = f32[8,256,1,128]{3,0,1,2:T(8,128)S(1)} dynamic-update-slice(f32[8,256,1,128]{3,0,1,2:T(8,128)S(1)} %get-tuple-element.140, f32[1,256,1,128]{3,0,1,2:T(1,128)S(1)} %convolution_bitcast_fusion.2, s32[]{:T(128)S(6)} %copy.109, s32[]{:T(128)} %constant.31.clone.1..sunk, s32[]{:T(128)} %constant.31.clone.1..sunk, s32[]{:T(128)} %constant.31.clone.1..sunk) | dynamic-update-slice | bytes 262148 | tf_op jit(solution)/shard_map/while/body/jit(dynamic_update_index_in_dim)/dynamic_update_slice | solution.py:98
  113.9 0.6 gather_fusion
  114.5 0.3 fusion.80
  114.9 1.3 convolution_bitcast_fusion.2
  116.2 2.8 %dynamic_update_slice.5 = f32[8,256,1,128]{3,0,1,2:T(8,128)S(1)} dynamic-update-slice(f32[8,256,1,128]{3,0,1,2:T(8,128)S(1)} %get-tuple-element.140, f32[1,256,1,128]{3,0,1,2:T(1,128)S(1)} %convolution_bitcast_fusion.2, s32[]{:T(128)S(6)} %copy.109, s32[]{:T(128)} %constant.31.clone.1..sunk, s32[]{:T(128)} %constant.31.clone.1..sunk, s32[]{:T(128)} %constant.31.clone.1..sunk) | dynamic-update-slice | bytes 262148 | tf_op jit(solution)/shard_map/while/body/jit(dynamic_update_index_in_dim)/dynamic_update_slice | solution.py:98
  119.1 0.6 gather_fusion
  119.6 0.3 fusion.80
  120.0 1.3 convolution_bitcast_fusion.2
  121.3 2.8 %dynamic_update_slice.5 = f32[8,256,1,128]{3,0,1,2:T(8,128)S(1)} dynamic-update-slice(f32[8,256,1,128]{3,0,1,2:T(8,128)S(1)} %get-tuple-element.140, f32[1,256,1,128]{3,0,1,2:T(1,128)S(1)} %convolution_bitcast_fusion.2, s32[]{:T(128)S(6)} %copy.109, s32[]{:T(128)} %constant.31.clone.1..sunk, s32[]{:T(128)} %constant.31.clone.1..sunk, s32[]{:T(128)} %constant.31.clone.1..sunk) | dynamic-update-slice | bytes 262148 | tf_op jit(solution)/shard_map/while/body/jit(dynamic_update_index_in_dim)/dynamic_update_slice | solution.py:98
  124.2 23.4 %all_to_all.33 = bf16[256,1,8,128]{3,2,1,0:T(8,128)(2,1)S(1)} all-to-all(bf16[256,1,8,128]{3,2,1,0:T(8,128)(2,1)S(1)} %fusion.19), channel_id=1, replica_groups=mesh['mem'=64,'reg'=4] {'mem'}, dimensions={0} | all-to-all | bytes 1048576 | tf_op jit(solution)/shard_map/all_to_all | solution.py:101
  147.6 0.9 copy.101
  (74 shorter events, 1.9 us)
Async XLA Ops:
  0.0 16.1 %copy-start.4 = (s32[2,2,512]{2,1,0:T(2,128)S(1)}, s32[2,2,512]{2,1,0:T(2,128)}, u32[]{:S(2)}) copy-start(s32[2,2,512]{2,1,0:T(2,128)} %param.14) | copy-start | bytes 24580
  0.0 16.1 %copy-start.5 = (s32[2,2,512]{2,1,0:T(2,128)S(1)}, s32[2,2,512]{2,1,0:T(2,128)}, u32[]{:S(2)}) copy-start(s32[2,2,512]{2,1,0:T(2,128)} %param.13) | copy-start | bytes 24580
  0.0 16.1 %copy-start.6 = (f32[2,2,512]{2,1,0:T(2,128)S(1)}, f32[2,2,512]{2,1,0:T(2,128)}, u32[]{:S(2)}) copy-start(f32[2,2,512]{2,1,0:T(2,128)} %param.12) | copy-start | bytes 24580
  0.0 16.2 %copy-start.10 = (s32[2,2]{1,0:T(2,128)S(1)}, s32[2,2]{1,0:T(2,128)}, u32[]{:S(2)}) copy-start(s32[2,2]{1,0:T(2,128)} %param.15) | copy-start | bytes 52
  0.0 16.3 %copy-start.7 = (f32[2,2,512]{2,1,0:T(2,128)S(1)}, f32[2,2,512]{2,1,0:T(2,128)}, u32[]{:S(2)}) copy-start(f32[2,2,512]{2,1,0:T(2,128)} %param.11) | copy-start | bytes 24580
  2.3 30.3 %all-to-all-start = ((bf16[4,1,512,128]{3,0,1,2:T(4,128)(2,1)}), bf16[4,1,512,128]{3,0,1,2:T(4,128)(2,1)S(1)}, u32[]{:S(2)}, u32[]{:S(2)}) async-start(bf16[4,1,512,128]{3,0,1,2:T(4,128)(2,1)} %copy.55), calls=%async_computation | async-start | bytes 1048576 | tf_op jit(solution)/shard_map/all_to_all | solution.py:55
  41.4 1.4 copy-start.3
  42.8 4.3 %copy-start = (f32[256,256]{1,0:T(8,128)S(1)}, f32[256,256]{1,0:T(8,128)}, u32[]{:S(2)}) copy-start(f32[256,256]{1,0:T(8,128)} %fusion.29) | copy-start | bytes 786436
  56.6 1.2 copy-start.2
  64.2 0.7 copy-start.8
  64.3 0.8 copy-start.9
  64.6 5.9 %collective-permute-start = (bf16[1,2,256,256]{3,2,1,0:T(8,128)(2,1)S(1)}, bf16[1,2,256,256]{3,2,1,0:T(8,128)(2,1)S(1)}, u32[]{:S(2)}, u32[]{:S(2)}) collective-permute-start(bf16[1,2,256,256]{3,2,1,0:T(8,128)(2,1)S(1)} %slice_bitcast_fusion), channel_id=1, source_target_pairs={{4,0},{8,4},{12,8},{16,12},{20,16},{24,20},{28,24},{32,28},{36,32}... | collective-permute-start | bytes 786440 | tf_op jit(solution)/shard_map/ppermute | solution.py:12
  70.5 12.4 %collective-permute-start.1 = (bf16[3,1,256,256]{3,2,1,0:T(8,128)(2,1)S(1)}, bf16[3,1,256,256]{3,2,1,0:T(8,128)(2,1)S(1)}, u32[]{:S(2)}, u32[]{:S(2)}) collective-permute-start(bf16[3,1,256,256]{3,2,1,0:T(8,128)(2,1)S(1)} %pad_maximum_fusion.1), channel_id=1, source_target_pairs={{1,0},{2,1},{3,2},{5,4},{6,5},{7,6},{9,8},{10,9},{11,10},{13,12},{... | collective-permute-start | bytes 1179656 | tf_op jit(solution)/shard_map/ppermute | solution.py:18
  72.0 11.0 %copy-start.1 = (f32[8,256,1,128]{3,0,1,2:T(8,128)S(1)}, f32[8,256,1,128]{3,0,1,2:T(8,128)}, u32[]{:S(2)}) copy-start(f32[8,256,1,128]{3,0,1,2:T(8,128)} %custom-call.4) | copy-start | bytes 3145732
where the time goes:
time: 149 us; the launch traced here: 148 us
  local copies, waits for them, and re-layouts  40.3 us (27%)
  matrix products  34.5 us (23%)
  waiting for transfers between devices  31.4 us (21%)
  blocking collectives  23.4 us (16%)
  starting transfers between devices  14.6 us (10%)
  other arithmetic  3.49 us (2%)
    all_to_all x1, blocking collectives, per_device(): lax.all_to_all(analysis[:, None], 'mem', split_axis=0, concat_axis=2, til...  23.4 us
    dynamic_update_slice x8, local copies, waits for them, and re-layouts, per_device(): lax.map(update_block, (corner_blocks, coeff_blocks, pert_blocks))  22.6 us
    all_to_all x1, waiting for transfers between devices, per_device(): lax.all_to_all(background, 'mem', split_axis=2, concat_axis=0, tiled=True)  15.5 us
    all_to_all x1, starting transfers between devices, per_device(): lax.all_to_all(background, 'mem', split_axis=2, concat_axis=0, tiled=True)  13 us
    ppermute x1, waiting for transfers between devices, passed_along_2(): lax.ppermute(value, axis, [(source, source + steps) for source in range(l...  10.9 us
    dot_general x8, matrix products, update_block(): jnp.einsum('gc,gckv->kgv', coeff_part, product, precision=lax.Precision.H...  10.5 us
    gather x2, local copies, waits for them, and re-layouts, per_device(): jnp.take(columns, position, axis=1).astype(jnp.float32)  8.81 us
    ppermute x1, waiting for transfers between devices, passed_along(): return lax.ppermute(block, axis, route)  4.96 us
  transfers between devices with their start and end apart: 3, of which 3 were waited for; matrix products, arithmetic and copies ran while one was open for 2% of the time, Pallas kernels for 0%

commit v1 on v0

v1 whole, which is shorter than its diff:
```python
import jax
import jax.numpy as jnp
from jax import lax
from jax.experimental import pallas as pl
from jax.experimental.pallas import tpu as pltpu
from jax.sharding import PartitionSpec as P

NS_ITERS = 4
F32 = jnp.float32
BF16 = jnp.bfloat16
VMEM = pl.BlockSpec(memory_space=pltpu.VMEM)
SMEM = pl.BlockSpec(memory_space=pltpu.SMEM)
NN = (((1,), (0,)), ((), ()))
NT = (((1,), (1,)), ((), ()))


def dot(a, b, dims=NN):
    return lax.dot_general(a, b, dims, preferred_element_type=F32)


def split(x):
    high = x.astype(BF16)
    return high, (x - high.astype(F32)).astype(BF16)


def thirds(x):
    high = x.astype(BF16)
    rest = x - high.astype(F32)
    middle = rest.astype(BF16)
    return high, middle, (rest - middle.astype(F32)).astype(BF16)


def product(a, b):
    return dot(a[0], b[0]) + (dot(a[0], b[1]) + dot(a[1], b[0]))


def prepare_kernel(count_ref, value_ref, error_ref, patch_ref, var_ref, corner_ref, coeff_ref, dense_ref, value_out_ref, mix_ref):
    rows, cols, slots = value_ref.shape
    patches, fields = dense_ref.shape[1:]
    slot_index = lax.broadcasted_iota(jnp.int32, (1, slots), 1)
    field_index = lax.broadcasted_iota(jnp.int32, (fields, slots), 0)
    patch_index = lax.broadcasted_iota(jnp.int32, (patches, slots), 0)
    for a in range(rows):
        for b in range(cols):
            weight = jnp.where(slot_index < count_ref[a, b], 1.0 / error_ref[a, b : b + 1, :], 0.0)
            weighted = weight * value_ref[a, b : b + 1, :]
            chosen = (field_index == var_ref[a, b : b + 1, :]).astype(F32).astype(BF16)
            at_patch = patch_index == patch_ref[a, b : b + 1, :]
            left = jnp.concatenate([jnp.where(at_patch, x, 0.0) for x in (weight, weighted)], axis=0)
            high, middle, low = (dot(x, chosen, NT) for x in thirds(left))
            sums = high + (middle + low)
            dense_ref[a * cols + b] = sums[:patches]
            value_out_ref[a * cols + b] = sums[patches:]
    corners, coeffs = corner_ref[...], coeff_ref[...]
    for t in range(mix_ref.shape[0]):
        used = jnp.sum(jnp.where(corners == t, coeffs, 0.0), axis=1, keepdims=True)
        mix_ref[t] = jnp.broadcast_to(used, (patches, fields))


def weights_of(points, high_ref, low_ref, centre, dense_ref, value_ref, out_ref, left_high, left_low):
    members = high_ref.shape[0]
    patches, fields = centre.shape
    row = lax.broadcasted_iota(jnp.int32, (members, members), 0)
    col = lax.broadcasted_iota(jnp.int32, (members, members), 1)
    diagonal = row == col
    identity = diagonal.astype(F32)
    state = []
    for slot, n in enumerate(points):
        dense = dense_ref[n]
        pull = value_ref[n] - dense * centre
        for p in range(patches):
            lanes = slice(p * fields, (p + 1) * fields)
            scaled = (high_ref[:, lanes].astype(F32) + low_ref[:, lanes].astype(F32)) * dense[p : p + 1, :]
            left_high[slot, :members, lanes], left_low[slot, :members, lanes] = split(scaled)
            tail = jnp.broadcast_to(pull[p : p + 1, :], (left_high.shape[1] - members, fields))
            left_high[slot, members:, lanes], left_low[slot, members:, lanes] = split(tail)
    for slot, n in enumerate(points):
        high, low = high_ref[...], low_ref[...]
        both = dot(left_high[slot], high, NT) + (dot(left_high[slot], low, NT) + dot(left_low[slot], high, NT))
        gram, projected = both[:members], both[members : members + 1]
        system = (members - 1.0) * identity + gram
        trace = jnp.sum(jnp.sum(jnp.where(diagonal, system, 0.0), axis=0, keepdims=True), axis=1, keepdims=True)
        scaling = trace / members
        state.append((projected, scaling, system * (1.0 / scaling)))
    iterates, inverses = [], []
    for _, _, start in state:
        parts = split(start)
        iterates.append(1.5 * start - 0.5 * product(parts, parts))
        inverses.append(1.5 * identity - 0.5 * start)
    for step in range(1, NS_ITERS):
        z = [split(x) for x in inverses]
        y = [split(x) for x in iterates]
        factors = [split(1.5 * identity - 0.5 * product(zz, yy)) for zz, yy in zip(z, y)]
        if step < NS_ITERS - 1:
            iterates = [product(yy, ff) for yy, ff in zip(y, factors)]
        inverses = [product(ff, zz) for ff, zz in zip(factors, z)]
    for slot, (projected, scaling, _) in enumerate(state):
        inverse = inverses[slot]
        once = jnp.sum(inverse * projected, axis=1, keepdims=True)
        twice = jnp.sum(inverse * once, axis=0, keepdims=True) / scaling
        out_ref[slot] = (jnp.sqrt((members - 1.0) / scaling) * inverse + twice).astype(BF16)


def first_kernel(ensemble_ref, dense_ref, value_ref, out_ref, high_ref, low_ref, centre_ref, pert_ref, left_high, left_low):
    members, patches, fields = ensemble_ref.shape
    total = jnp.zeros((patches, fields), F32)
    chunk = 32
    for k in range(0, members, chunk):
        total = total + jnp.sum(ensemble_ref[k : k + chunk].astype(F32), axis=0)
    centre = total * (1.0 / members)
    centre_ref[...] = centre
    for k in range(0, members, chunk):
        part = ensemble_ref[k : k + chunk].astype(F32) - centre
        pert_ref[k * patches : (k + chunk) * patches] = part.reshape(chunk * patches, fields)
    for p in range(patches):
        lanes = slice(p * fields, (p + 1) * fields)
        high_ref[:, lanes], low_ref[:, lanes] = split(pert_ref[pl.ds(p, members, stride=patches), :])
    weights_of((0, 2), high_ref, low_ref, centre, dense_ref, value_ref, out_ref, left_high, left_low)


def second_kernel(high_ref, low_ref, centre_ref, dense_ref, value_ref, out_ref, left_high, left_low):
    weights_of((1, 3), high_ref, low_ref, centre_ref[...], dense_ref, value_ref, out_ref, left_high, left_low)


def blend(parts, high_ref, mix_ref, p):
    fields = mix_ref.shape[2]
    lanes = slice(p * fields, (p + 1) * fields)
    total = None
    for t, ref, slot in parts:
        share = mix_ref[t, p : p + 1, :]
        moved = dot(ref[slot], high_ref[:, lanes])
        moved = jnp.where(share != 0.0, share * moved, 0.0)
        total = moved if total is None else total + moved
    return total


def own_kernel(one_ref, two_ref, beside_ref, high_ref, mix_ref, out_ref):
    parts = ((0, one_ref, 0), (3, one_ref, 1), (1, two_ref, 0), (4, two_ref, 1), (2, beside_ref, 0), (5, beside_ref, 1))
    fields = mix_ref.shape[2]
    for p in range(mix_ref.shape[1]):
        out_ref[:, p * fields : (p + 1) * fields] = blend(parts, high_ref, mix_ref, p)


def last_kernel(below_ref, high_ref, mix_ref, partial_ref, centre_ref, out_ref, all_ref):
    parts = ((6, below_ref, 0), (7, below_ref, 1), (8, below_ref, 2))
    members, patches, fields = out_ref.shape
    for p in range(patches):
        lanes = slice(p * fields, (p + 1) * fields)
        total = partial_ref[:, lanes] + blend(parts, high_ref, mix_ref, p)
        all_ref[pl.ds(p, members, stride=patches), :] = total + centre_ref[p : p + 1, :]
    chunk = 32
    for k in range(0, members, chunk):
        part = all_ref[k * patches : (k + chunk) * patches, :]
        out_ref[k : k + chunk] = part.reshape(chunk, patches, fields).astype(BF16)


def call(kernel, outs, specs, scratch=()):
    return pl.pallas_call(
        kernel,
        out_shape=outs,
        in_specs=specs,
        out_specs=jax.tree.map(lambda _: VMEM, outs),
        scratch_shapes=list(scratch),
        compiler_params=pltpu.CompilerParams(vmem_limit_bytes=48 << 20),
    )


def per_device(background, obs_value, obs_error, obs_patch, obs_variable, obs_count, patch_corners, interp_weights):
    shape = jax.ShapeDtypeStruct
    devices = lax.axis_size("mem")
    regions = lax.axis_size("reg")
    own, _, all_patches, fields = background.shape
    patches = all_patches // devices
    members = own * devices
    points = obs_value.shape[0] * obs_value.shape[1]
    columns = patches * fields

    outgoing = jnp.transpose(background.reshape(own, devices, patches, fields), (1, 0, 2, 3))
    ensemble = lax.all_to_all(outgoing, "mem", split_axis=0, concat_axis=0, tiled=True).reshape(members, patches, fields)
    dense, values, mix = call(
        prepare_kernel,
        (shape((points, patches, fields), F32), shape((points, patches, fields), F32), shape((9, patches, fields), F32)),
        [SMEM] + [VMEM] * 6,
    )(obs_count, obs_value, obs_error, obs_patch, obs_variable, patch_corners[0], interp_weights[0])

    pair = shape((2, members, members), BF16)
    lefts = [pltpu.VMEM((2, members + 16, columns), BF16)] * 2
    one, high, low, centre = call(
        first_kernel,
        (pair, shape((members, columns), BF16), shape((members, columns), BF16), shape((patches, fields), F32)),
        [VMEM] * 3,
        [pltpu.VMEM((members * patches, fields), F32)] + lefts,
    )(ensemble, dense, values)
    beside = lax.ppermute(one, "reg", [(r + 1, r) for r in range(regions - 1)])
    two = call(second_kernel, pair, [VMEM] * 5, lefts)(high, low, centre, dense, values)
    top = jnp.stack([one[0], two[0], beside[0]])
    below = lax.ppermute(top, "mem", [((d + 1) % devices, d) for d in range(devices)])
    partial = call(own_kernel, shape((members, columns), F32), [VMEM] * 5)(one, two, beside, high, mix)
    analysis = call(
        last_kernel,
        shape((members, patches, fields), BF16),
        [VMEM] * 5,
        [pltpu.VMEM((members * patches, fields), F32)],
    )(below, high, mix, partial, centre)
    returned = lax.all_to_all(analysis.reshape(devices, own, patches, fields), "mem", split_axis=0, concat_axis=0, tiled=True)
    return jnp.transpose(returned, (1, 0, 2, 3)).reshape(own, 1, all_patches, fields)


def solution(mesh):
    placed = (
        P("mem", "reg", None, None),
        P("mem", "reg", None),
        P("mem", "reg", None),
        P("mem", "reg", None),
        P("mem", "reg", None),
        P("mem", "reg"),
        P("reg", "mem", None),
        P("reg", "mem", None),
    )
    return jax.shard_map(
        per_device,
        mesh=mesh,
        in_specs=placed,
        out_specs=P("mem", "reg", None, None),
        check_vma=False,
    )
```

time: 149 us -> 81.8 us (0.55)
  local copies, waits for them, and re-layouts: 40.3 us -> 5.2 us
  matrix products: 34.5 us -> 0 us
  Pallas kernels: 0 us -> 13 us
  waiting for transfers between devices: 31.4 us -> 23.1 us
  other arithmetic: 3.49 us -> 0.05 us
    dot_general x31 -> x0, matrix products: 34.5 us -> none  [the longest x8 10.5 us: update_block(): jnp.einsum('gc,gckv->kgv', coeff_part, product, precision=lax.Precision.H...]
    dynamic_update_slice x8 -> x0, local copies, waits for them, and re-layouts: 22.6 us -> none  [per_device(): lax.map(update_block, (corner_blocks, coeff_blocks, pert_blocks))]
    gather x10 -> x0, local copies, waits for them, and re-layouts: 13.5 us -> none  [the longest x2 8.81 us: per_device(): jnp.take(columns, position, axis=1).astype(jnp.float32)]
    pallas_call x0 -> x5, Pallas kernels: none -> 13 us  [the longest x1 4.74 us: per_device(): call(first_kernel, (pair, shape((members, columns), BF16), shape((members...]
    ppermute x2, waiting for transfers between devices: 15.9 us -> 7.65 us  [the longest x1 4.46 us: per_device(): lax.ppermute(top, 'mem', [((d + 1) % devices, d) for d in range(devices)])]
  transfers between devices with their start and end apart: 3 -> 3, of which waited for: 3 -> 3; matrix products, arithmetic and copies ran while one was open for 2% -> 0% of each run, Pallas kernels for 0% -> 9%
where the time goes in v1:
time: 81.8 us; the launch traced here: 81.5 us
  blocking collectives  24.3 us (30%)
  waiting for transfers between devices  23.1 us (28%)
  starting transfers between devices  15.7 us (19%)
  Pallas kernels  13 us (16%)
  local copies, waits for them, and re-layouts  5.2 us (6%)
    all_to_all x1, blocking collectives, per_device(): lax.all_to_all(analysis.reshape(devices, own, patches, fields), 'mem', sp...  24.3 us
    all_to_all x1, waiting for transfers between devices, per_device(): lax.all_to_all(outgoing, 'mem', split_axis=0, concat_axis=0, tiled=True)  15.4 us
    all_to_all x1, starting transfers between devices, per_device(): lax.all_to_all(outgoing, 'mem', split_axis=0, concat_axis=0, tiled=True)  13.1 us
    pallas_call x1, Pallas kernels, per_device(): call(first_kernel, (pair, shape((members, columns), BF16), shape((members...  4.74 us
    ppermute x1, waiting for transfers between devices, per_device(): lax.ppermute(top, 'mem', [((d + 1) % devices, d) for d in range(devices)])  4.46 us
    pallas_call x1, Pallas kernels, per_device(): call(second_kernel, pair, [VMEM] * 5, lefts)  4.33 us
    ppermute x1, waiting for transfers between devices, per_device(): beside = lax.ppermute(one, 'reg', [(r + 1, r) for r in range(regions - 1)])  3.18 us
    unnamed x20, local copies, waits for them, and re-layouts  2.36 us
  transfers between devices with their start and end apart: 3, of which 3 were waited for; matrix products, arithmetic and copies ran while one was open for 0% of the time, Pallas kernels for 9%

profile of v1, /device:TPU:1, one launch (start us, length us, event | category | flops | bytes accessed | tf_op | source)
XLA Modules:
  0.0 81.5 jit_solution(2514476053961892852)
XLA Ops:
  0.0 0.0 copy-start
  0.0 1.0 %copy-done = bf16[4,1,512,128]{3,2,1,0:T(8,128)(2,1)S(1)} copy-done((bf16[4,1,512,128]{3,2,1,0:T(8,128)(2,1)S(1)}, bf16[4,1,512,128]{3,2,1,0:T(8,128)(2,1)}, u32[]{:S(2)}) %copy-start) | copy-done | bytes 524312
  1.0 0.9 %copy_bitcast_fusion.1 = bf16[64,4,8,128]{3,2,1,0:T(8,128)(2,1)} fusion(bf16[4,1,512,128]{3,2,1,0:T(8,128)(2,1)S(1)} %copy-done), kind=kLoop, calls=%fused_computation.1 | loop fusion | bytes 1048576 | tf_op jit(solution)/shard_map/transpose | solution.py:178
  1.9 0.0 copy-start.8
  1.9 0.0 copy-start.9
  1.9 0.0 copy-start.4
  1.9 0.0 copy-start.5
  1.9 0.0 copy-start.6
  1.9 13.1 %all-to-all-start = ((bf16[64,4,8,128]{3,2,1,0:T(8,128)(2,1)}), bf16[64,4,8,128]{3,2,1,0:T(8,128)(2,1)S(1)}, u32[]{:S(2)}, u32[]{:S(2)}) async-start(bf16[64,4,8,128]{3,2,1,0:T(8,128)(2,1)} %copy_bitcast_fusion.1), calls=%async_computation | async-start | bytes 1048576 | tf_op jit(solution)/shard_map/all_to_all | solution.py:179
  15.1 0.0 copy-start.3
  15.1 0.0 copy-done.8
  15.1 0.1 copy.10.corner_ref
  15.2 0.0 copy-done.9
  15.2 0.0 copy-start.7
  15.2 0.1 copy.11.coeff_ref
  15.3 0.0 copy-done.4
  15.3 0.0 copy-done.5
  15.3 0.0 copy-done.6
  15.3 0.5 copy-done.3
  15.8 0.1 copy-done.7
  15.9 1.1 %shard_map.82 = (f32[4,8,128]{2,1,0:T(8,128)S(1)}, f32[4,8,128]{2,1,0:T(8,128)S(1)}, f32[9,8,128]{2,1,0:T(8,128)S(1)}) custom-call(s32[2,2]{1,0:T(2,128)S(1)} %copy-done.7, f32[2,2,512]{2,1,0:T(2,128)S(1)} %copy-done.3, f32[2,2,512]{2,1,0:T(2,128)S(1)} %copy-done.4, s32[2,2,512]{2,1,0:T(2,128)S(1)} %copy-done.5, s32[2,2,512]{2,1,0:T(2,128)S(1)} %copy-done.6, ...), custom_call_target="tpu_custom_call" | custom-call | tf_op jit(solution)/shard_map/pallas_call | solution.py:180
  16.9 15.4 %all-to-all-done = bf16[64,4,8,128]{3,2,1,0:T(8,128)(2,1)S(1)} async-done(((bf16[64,4,8,128]{3,2,1,0:T(8,128)(2,1)}), bf16[64,4,8,128]{3,2,1,0:T(8,128)(2,1)S(1)}, u32[]{:S(2)}, u32[]{:S(2)}) %all-to-all-start) | async-done | bytes 524320 | tf_op jit(solution)/shard_map/all_to_all | solution.py:179
  32.4 4.7 %shard_map.83 = (bf16[2,256,256]{2,1,0:T(8,128)(2,1)S(1)}, bf16[256,1024]{1,0:T(8,128)(2,1)S(1)}, bf16[256,1024]{1,0:T(8,128)(2,1)S(1)}, f32[8,128]{1,0:T(8,128)S(1)}) custom-call(bf16[256,8,128]{2,1,0:T(8,128)(2,1)S(1)} %bitcast.15, f32[4,8,128]{2,1,0:T(8,128)S(1)} %get-tuple-element.12.dense_ref, f32[4,8,128]{2,1,0:T(8,128)S(1)} %get-tuple-element.13.value_ref), custom_call_target="tpu_custom_call" | custom-call | tf_op jit(solution)/shard_map/pallas_call | solution.py:188
  37.1 1.3 %collective-permute-start = (bf16[2,256,256]{2,1,0:T(8,128)(2,1)S(1)}, bf16[2,256,256]{2,1,0:T(8,128)(2,1)S(1)}, u32[]{:S(2)}, u32[]{:S(2)}) collective-permute-start(bf16[2,256,256]{2,1,0:T(8,128)(2,1)S(1)} %get-tuple-element.14.one_ref), channel_id=1, source_target_pairs={{1,0},{2,1},{3,2},{5,4},{6,5},{7,6},{9,8},{10,9},{11,10},{13,12},{... | collective-permute-start | bytes 786440 | tf_op jit(solution)/shard_map/ppermute | solution.py:194
  38.4 4.3 %shard_map.84.two_ref = bf16[2,256,256]{2,1,0:T(8,128)(2,1)S(1)} custom-call(bf16[256,1024]{1,0:T(8,128)(2,1)S(1)} %get-tuple-element.15.high_ref, bf16[256,1024]{1,0:T(8,128)(2,1)S(1)} %get-tuple-element.16.low_ref, f32[8,128]{1,0:T(8,128)S(1)} %get-tuple-element.17.centre_ref, f32[4,8,128]{2,1,0:T(8,128)S(1)} %get-tuple-element.12.dense_ref, ...), custom_call_target="tpu_custom_call" | custom-call | tf_op jit(solution)/shard_map/pallas_call | solution.py:195
  42.8 0.0 copy-start.1
  42.8 0.7 copy-done.1
  43.5 3.2 %collective-permute-done.beside_ref = bf16[2,256,256]{2,1,0:T(8,128)(2,1)S(1)} collective-permute-done((bf16[2,256,256]{2,1,0:T(8,128)(2,1)S(1)}, bf16[2,256,256]{2,1,0:T(8,128)(2,1)S(1)}, u32[]{:S(2)}, u32[]{:S(2)}) %collective-permute-start) | collective-permute-done | bytes 262176 | tf_op jit(solution)/shard_map/ppermute | solution.py:194
  46.7 0.0 slice-start
  46.7 0.9 %slice-done = bf16[1,256,256]{2,1,0:T(8,128)(2,1)S(1)} async-done(((bf16[2,256,256]{2,1,0:T(8,128)(2,1)}), bf16[1,256,256]{2,1,0:T(8,128)(2,1)S(1)}, s32[]{:S(2)}) %slice-start) | async-done | bytes 131096 | tf_op jit(solution)/shard_map/slice | solution.py:196
  47.6 0.0 copy-start.2
  47.6 1.3 %collective-permute-start.1 = (bf16[3,256,256]{2,1,0:T(8,128)(2,1)S(1)}, bf16[3,256,256]{2,1,0:T(8,128)(2,1)S(1)}, u32[]{:S(2)}, u32[]{:S(2)}) collective-permute-start(bf16[3,256,256]{2,1,0:T(8,128)(2,1)S(1)} %pad_maximum_fusion), channel_id=1, source_target_pairs={{4,0},{8,4},{12,8},{16,12},{20,16},{24,20},{28,24},{32,28},{36,32}... | collective-permute-start | bytes 1179656 | tf_op jit(solution)/shard_map/ppermute | solution.py:197
  48.9 0.0 copy-done.2
  48.9 1.8 %shard_map.85.partial_ref = f32[256,1024]{1,0:T(8,128)S(1)} custom-call(bf16[2,256,256]{2,1,0:T(8,128)(2,1)S(1)} %get-tuple-element.14.one_ref, bf16[2,256,256]{2,1,0:T(8,128)(2,1)S(1)} %copy-done.2, bf16[2,256,256]{2,1,0:T(8,128)(2,1)S(1)} %collective-permute-done.beside_ref, bf16[256,1024]{1,0:T(8,128)(2,1)S(1)} %get-tuple-element.15.high_ref, ...), custom_call_target="tpu_custom_call" | custom-call | tf_op jit(solution)/shard_map/pallas_call | solution.py:198
  50.7 4.5 %collective-permute-done.1.below_ref = bf16[3,256,256]{2,1,0:T(8,128)(2,1)S(1)} collective-permute-done((bf16[3,256,256]{2,1,0:T(8,128)(2,1)S(1)}, bf16[3,256,256]{2,1,0:T(8,128)(2,1)S(1)}, u32[]{:S(2)}, u32[]{:S(2)}) %collective-permute-start.1) | collective-permute-done | bytes 393248 | tf_op jit(solution)/shard_map/ppermute | solution.py:197
  55.2 1.0 %shard_map.86 = bf16[256,8,128]{2,1,0:T(8,128)(2,1)S(1)} custom-call(bf16[3,256,256]{2,1,0:T(8,128)(2,1)S(1)} %collective-permute-done.1.below_ref, bf16[256,1024]{1,0:T(8,128)(2,1)S(1)} %get-tuple-element.15.high_ref, f32[9,8,128]{2,1,0:T(8,128)S(1)} %get-tuple-element.18.mix_ref, f32[256,1024]{1,0:T(8,128)S(1)} %shard_map.85.partial_ref, ...), custom_call_target="tpu_custom_call" | custom-call | tf_op jit(solution)/shard_map/pallas_call | solution.py:199
  56.2 24.3 %all_to_all.10 = bf16[64,4,8,128]{3,2,1,0:T(8,128)(2,1)S(1)} all-to-all(bf16[64,4,8,128]{3,2,1,0:T(8,128)(2,1)S(1)} %bitcast.14), channel_id=1, replica_groups=mesh['mem'=64,'reg'=4] {'mem'}, dimensions={0} | all-to-all | bytes 1048576 | tf_op jit(solution)/shard_map/all_to_all | solution.py:205
  80.6 0.9 %copy_bitcast_fusion = bf16[4,1,512,128]{3,2,1,0:T(8,128)(2,1)} fusion(bf16[64,4,8,128]{3,2,1,0:T(8,128)(2,1)S(1)} %all_to_all.10), kind=kLoop, calls=%fused_computation | loop fusion | bytes 1048576 | tf_op jit(solution)/shard_map/reshape | solution.py:206
  (3 shorter events, 0.1 us)
Async XLA Ops:
  0.0 1.0 %copy-start = (bf16[4,1,512,128]{3,2,1,0:T(8,128)(2,1)S(1)}, bf16[4,1,512,128]{3,2,1,0:T(8,128)(2,1)}, u32[]{:S(2)}) copy-start(bf16[4,1,512,128]{3,2,1,0:T(8,128)(2,1)} %param.8) | copy-start | bytes 1572868
  1.9 13.2 %copy-start.8 = (s32[1,8,4]{1,2,0:T(4,128)S(1)}, s32[1,8,4]{1,2,0:T(4,128)}, u32[]{:S(2)}) copy-start(s32[1,8,4]{1,2,0:T(4,128)} %param.14) | copy-start | bytes 388
  1.9 13.3 %copy-start.9 = (f32[1,8,4]{1,2,0:T(4,128)S(1)}, f32[1,8,4]{1,2,0:T(4,128)}, u32[]{:S(2)}) copy-start(f32[1,8,4]{1,2,0:T(4,128)} %param.15) | copy-start | bytes 388
  1.9 13.3 %copy-start.4 = (f32[2,2,512]{2,1,0:T(2,128)S(1)}, f32[2,2,512]{2,1,0:T(2,128)}, u32[]{:S(2)}) copy-start(f32[2,2,512]{2,1,0:T(2,128)} %error_ref.1) | copy-start | bytes 24580
  1.9 13.3 %copy-start.5 = (s32[2,2,512]{2,1,0:T(2,128)S(1)}, s32[2,2,512]{2,1,0:T(2,128)}, u32[]{:S(2)}) copy-start(s32[2,2,512]{2,1,0:T(2,128)} %patch_ref.1) | copy-start | bytes 24580
  1.9 13.3 %copy-start.6 = (s32[2,2,512]{2,1,0:T(2,128)S(1)}, s32[2,2,512]{2,1,0:T(2,128)}, u32[]{:S(2)}) copy-start(s32[2,2,512]{2,1,0:T(2,128)} %var_ref.1) | copy-start | bytes 24580
  1.9 30.4 %all-to-all-start = ((bf16[64,4,8,128]{3,2,1,0:T(8,128)(2,1)}), bf16[64,4,8,128]{3,2,1,0:T(8,128)(2,1)S(1)}, u32[]{:S(2)}, u32[]{:S(2)}) async-start(bf16[64,4,8,128]{3,2,1,0:T(8,128)(2,1)} %copy_bitcast_fusion.1), calls=%async_computation | async-start | bytes 1048576 | tf_op jit(solution)/shard_map/all_to_all | solution.py:179
  15.1 0.7 copy-start.3
  15.2 0.7 copy-start.7
  37.1 9.5 %collective-permute-start = (bf16[2,256,256]{2,1,0:T(8,128)(2,1)S(1)}, bf16[2,256,256]{2,1,0:T(8,128)(2,1)S(1)}, u32[]{:S(2)}, u32[]{:S(2)}) collective-permute-start(bf16[2,256,256]{2,1,0:T(8,128)(2,1)S(1)} %get-tuple-element.14.one_ref), channel_id=1, source_target_pairs={{1,0},{2,1},{3,2},{5,4},{6,5},{7,6},{9,8},{10,9},{11,10},{13,12},{... | collective-permute-start | bytes 786440 | tf_op jit(solution)/shard_map/ppermute | solution.py:194
  42.8 0.7 copy-start.1
  46.7 0.9 %slice-start = ((bf16[2,256,256]{2,1,0:T(8,128)(2,1)}), bf16[1,256,256]{2,1,0:T(8,128)(2,1)S(1)}, s32[]{:S(2)}) async-start(bf16[2,256,256]{2,1,0:T(8,128)(2,1)} %copy-done.1), calls=%async_computation.2 | async-start | bytes 262144 | tf_op jit(solution)/shard_map/slice | solution.py:196
  47.6 1.4 %copy-start.2 = (bf16[2,256,256]{2,1,0:T(8,128)(2,1)S(1)}, bf16[2,256,256]{2,1,0:T(8,128)(2,1)}, u32[]{:S(2)}) copy-start(bf16[2,256,256]{2,1,0:T(8,128)(2,1)} %copy-done.1) | copy-start | bytes 786436
  47.6 7.6 %collective-permute-start.1 = (bf16[3,256,256]{2,1,0:T(8,128)(2,1)S(1)}, bf16[3,256,256]{2,1,0:T(8,128)(2,1)S(1)}, u32[]{:S(2)}, u32[]{:S(2)}) collective-permute-start(bf16[3,256,256]{2,1,0:T(8,128)(2,1)S(1)} %pad_maximum_fusion), channel_id=1, source_target_pairs={{4,0},{8,4},{12,8},{16,12},{20,16},{24,20},{28,24},{32,28},{36,32}... | collective-permute-start | bytes 1179656 | tf_op jit(solution)/shard_map/ppermute | solution.py:197

commit v2 on v1

v2 whole, which is shorter than its diff:
```python
import jax
import jax.numpy as jnp
from jax import lax
from jax.experimental import pallas as pl
from jax.experimental.pallas import tpu as pltpu
from jax.sharding import PartitionSpec as P

F32 = jnp.float32
BF16 = jnp.bfloat16
VMEM = pl.BlockSpec(memory_space=pltpu.VMEM)
SMEM = pl.BlockSpec(memory_space=pltpu.SMEM)
HBM = pl.BlockSpec(memory_space=pltpu.HBM)
NN = (((1,), (0,)), ((), ()))
NT = (((1,), (1,)), ((), ()))


def dot(a, b, dims=NN):
    return lax.dot_general(a, b, dims, preferred_element_type=F32)


def split(x):
    high = x.astype(BF16)
    return high, (x - high.astype(F32)).astype(BF16)


def thirds(x):
    high = x.astype(BF16)
    rest = x - high.astype(F32)
    middle = rest.astype(BF16)
    return high, middle, (rest - middle.astype(F32)).astype(BF16)


def product(a, b):
    return dot(a[0], b[0]) + (dot(a[0], b[1]) + dot(a[1], b[0]))


def prepare_kernel(count_ref, value_ref, error_ref, patch_ref, var_ref, corner_ref, coeff_ref, dense_ref, value_out_ref, mix_ref):
    rows, cols, slots = value_ref.shape
    patches, fields = dense_ref.shape[1:]
    slot_index = lax.broadcasted_iota(jnp.int32, (1, slots), 1)
    field_index = lax.broadcasted_iota(jnp.int32, (fields, slots), 0)
    patch_index = lax.broadcasted_iota(jnp.int32, (patches, slots), 0)
    for a in range(rows):
        for b in range(cols):
            weight = jnp.where(slot_index < count_ref[a, b], 1.0 / error_ref[a, b : b + 1, :], 0.0)
            weighted = weight * value_ref[a, b : b + 1, :]
            chosen = (field_index == var_ref[a, b : b + 1, :]).astype(F32).astype(BF16)
            at_patch = patch_index == patch_ref[a, b : b + 1, :]
            left = jnp.concatenate([jnp.where(at_patch, x, 0.0) for x in (weight, weighted)], axis=0)
            high, middle, low = (dot(x, chosen, NT) for x in thirds(left))
            sums = high + (middle + low)
            dense_ref[a * cols + b] = sums[:patches]
            value_out_ref[a * cols + b] = sums[patches:]
    corners, coeffs = corner_ref[...], coeff_ref[...]
    for t in range(mix_ref.shape[0]):
        used = jnp.sum(jnp.where(corners == t, coeffs, 0.0), axis=1, keepdims=True)
        mix_ref[t] = jnp.broadcast_to(used, (patches, fields))


def shares(points, x_ref, centre, dense_ref, value_ref, left_high, left_low):
    members = x_ref.shape[0]
    patches, fields = centre.shape
    for slot, n in enumerate(points):
        dense = dense_ref[n]
        pull = value_ref[n] - dense * centre
        for p in range(patches):
            lanes = slice(p * fields, (p + 1) * fields)
            scaled = (x_ref[:, lanes].astype(F32) - centre[p : p + 1, :]) * dense[p : p + 1, :]
            left_high[slot, :members, lanes], left_low[slot, :members, lanes] = split(scaled)
            tail = jnp.broadcast_to(pull[p : p + 1, :], (left_high.shape[1] - members, fields))
            left_high[slot, members:, lanes], left_low[slot, members:, lanes] = split(tail)


def two_factors(x, square):
    return 0.375 * square - 0.5 * x + product(split(square), split(0.0625 * square - 0.3125 * x))


def weights_of(count, x_ref, left_high, left_low, out_ref):
    members = x_ref.shape[0]
    row = lax.broadcasted_iota(jnp.int32, (members, members), 0)
    col = lax.broadcasted_iota(jnp.int32, (members, members), 1)
    diagonal = row == col
    slots = range(count)
    state = []
    for slot in slots:
        columns = x_ref[...]
        both = dot(left_high[slot], columns, NT) + dot(left_low[slot], columns, NT)
        both = both - jnp.sum(both, axis=1, keepdims=True) * (1.0 / members)
        gram, projected = both[:members], both[members : members + 1]
        trace = jnp.sum(jnp.sum(jnp.where(diagonal, gram, 0.0), axis=0, keepdims=True), axis=1, keepdims=True)
        scaling = (members - 1.0) + trace / members
        inverse_scaling = 1.0 / scaling
        state.append((projected, scaling, gram * inverse_scaling + jnp.where(diagonal, (members - 1.0) * inverse_scaling - 1.0, 0.0)))
    r = [split(x) for _, _, x in state]
    squares = [product(x, x) for x in r]
    w = [two_factors(state[s][2], squares[s]) for s in slots]
    w_parts = [split(x) for x in w]
    v = [state[s][2] + w[s] + product(r[s], w_parts[s]) for s in slots]
    e = [v[s] + w[s] + product(split(v[s]), w_parts[s]) for s in slots]
    e_parts = [split(x) for x in e]
    squares = [product(x, x) for x in e_parts]
    h = [two_factors(e[s], squares[s]) for s in slots]
    inverses = [w[s] + h[s] + product(w_parts[s], split(h[s])) for s in slots]
    half = members // 2
    small_row, small_col = row[:half, :half], col[:half, :half]
    tail_row = lax.broadcasted_iota(jnp.int32, (16, members), 0)
    for slot in slots:
        projected, scaling, _ = state[slot]
        inverse = inverses[slot] + jnp.where(diagonal, 1.0, 0.0)
        once = jnp.sum(inverse * projected, axis=1, keepdims=True)
        twice = jnp.sum(inverse * once, axis=0, keepdims=True) / scaling
        spread = jnp.sqrt((members - 1.0) / scaling) * inverse
        out_ref[slot] = (spread + twice).astype(BF16)
        yield slot, spread, twice, half, small_row, small_col, tail_row


def pack(target, slot, spread, twice, half, small_row, small_col, tail_row):
    corner = spread[half:, half:]
    target[slot, :half, :half] = jnp.where(small_row >= small_col, spread[:half, :half], corner).astype(BF16)
    target[slot, :half, half:] = spread[:half, half:].astype(BF16)
    on_diagonal = jnp.sum(jnp.where(small_row == small_col, corner, 0.0), axis=0, keepdims=True)
    high, low = split(twice)
    rows = jnp.where(tail_row == 1, high.astype(F32), jnp.where(tail_row == 2, low.astype(F32), 0.0))
    first = jnp.concatenate([on_diagonal, jnp.zeros_like(on_diagonal)], axis=1)
    target[slot, half:, :] = jnp.where(tail_row == 0, first, rows).astype(BF16)


def unpack(source, slot, target, place):
    half = source.shape[1] - 16
    row = lax.broadcasted_iota(jnp.int32, (half, half), 0)
    col = lax.broadcasted_iota(jnp.int32, (half, half), 1)
    mixed = source[slot, :half, :half].astype(F32)
    across = source[slot, :half, half:].astype(F32)
    tail = source[slot, half:, :].astype(F32)
    mean = tail[1:2] + tail[2:3]
    left, right = mean[:, :half], mean[:, half:]
    turned = mixed.T
    target[place, :half, :half] = (jnp.where(row >= col, mixed, turned) + left).astype(BF16)
    target[place, :half, half:] = (across + right).astype(BF16)
    target[place, half:, :half] = (across.T + left).astype(BF16)
    corner = jnp.where(row < col, mixed, jnp.where(row == col, tail[0:1, :half], turned))
    target[place, half:, half:] = (corner + right).astype(BF16)


def first_kernel(ensemble_ref, dense_ref, value_ref, out_ref, pack_ref, x_ref, high_ref, centre_ref, wide_ref, left_high, left_low):
    members, patches, fields = ensemble_ref.shape
    total = jnp.zeros((patches, fields), F32)
    chunk = 32
    for k in range(0, members, chunk):
        part = ensemble_ref[k : k + chunk].astype(F32)
        total = total + jnp.sum(part, axis=0)
        wide_ref[k * patches : (k + chunk) * patches] = part.reshape(chunk * patches, fields)
    centre = total * (1.0 / members)
    centre_ref[...] = centre
    for p in range(patches):
        lanes = slice(p * fields, (p + 1) * fields)
        part = wide_ref[pl.ds(p, members, stride=patches), :]
        x_ref[:, lanes] = part.astype(BF16)
        high_ref[:, lanes] = (part - centre[p : p + 1, :]).astype(BF16)
    shares((0, 2), x_ref, centre, dense_ref, value_ref, left_high, left_low)
    for slot, *rest in weights_of(2, x_ref, left_high, left_low, out_ref):
        pack(pack_ref, slot, *rest)


def second_kernel(x_ref, centre_ref, dense_ref, value_ref, sent_ref, out_ref, pack_ref, left_high, left_low):
    shares((1, 3), x_ref, centre_ref[...], dense_ref, value_ref, left_high, left_low)
    pack_ref[0] = sent_ref[0]
    for slot, *rest in weights_of(2, x_ref, left_high, left_low, out_ref):
        if slot == 0:
            pack(pack_ref, 1, *rest)
    pack_ref[2] = jnp.zeros(pack_ref.shape[1:], BF16)


def blend(parts, high_ref, mix_ref, p):
    fields = mix_ref.shape[2]
    lanes = slice(p * fields, (p + 2) * fields)
    total = None
    for t, ref, slot in parts:
        share = jnp.concatenate([mix_ref[t, p : p + 1, :], mix_ref[t, p + 1 : p + 2, :]], axis=1)
        moved = dot(ref[slot], high_ref[:, lanes])
        moved = jnp.where(share != 0.0, share * moved, 0.0)
        total = moved if total is None else total + moved
    return total


def own_kernel(one_ref, two_ref, beside_ref, high_ref, mix_ref, out_ref, whole_ref):
    unpack(beside_ref, 0, whole_ref, 0)
    unpack(beside_ref, 1, whole_ref, 1)
    parts = ((0, one_ref, 0), (3, one_ref, 1), (1, two_ref, 0), (4, two_ref, 1), (2, whole_ref, 0), (5, whole_ref, 1))
    fields = mix_ref.shape[2]
    for p in range(0, mix_ref.shape[1], 2):
        out_ref[:, p * fields : (p + 2) * fields] = blend(parts, high_ref, mix_ref, p)


def last_kernel(below_ref, high_ref, mix_ref, partial_ref, centre_ref, out_ref, all_ref, whole_ref):
    for slot in range(3):
        unpack(below_ref, slot, whole_ref, slot)
    parts = ((6, whole_ref, 0), (7, whole_ref, 1), (8, whole_ref, 2))
    members, patches, fields = out_ref.shape
    for p in range(0, patches, 2):
        lanes = slice(p * fields, (p + 2) * fields)
        total = partial_ref[:, lanes] + blend(parts, high_ref, mix_ref, p)
        for q in range(2):
            part = total[:, q * fields : (q + 1) * fields] + centre_ref[p + q : p + q + 1, :]
            all_ref[pl.ds(p + q, members, stride=patches), :] = part
    chunk = 32
    for k in range(0, members, chunk):
        part = all_ref[k * patches : (k + chunk) * patches, :]
        out_ref[k : k + chunk] = part.reshape(chunk, patches, fields).astype(BF16)


def outgoing_kernel(source_ref, target_ref, done):
    copies = [pltpu.make_async_copy(source_ref.at[m], target_ref.at[:, m], done.at[m]) for m in range(source_ref.shape[0])]
    for copy in copies:
        copy.start()
    for copy in copies:
        copy.wait()


def returned_kernel(source_ref, target_ref, done):
    copies = [pltpu.make_async_copy(source_ref.at[:, m], target_ref.at[m], done.at[m]) for m in range(target_ref.shape[0])]
    for copy in copies:
        copy.start()
    for copy in copies:
        copy.wait()


def call(kernel, outs, specs, scratch=(), to=VMEM):
    return pl.pallas_call(
        kernel,
        out_shape=outs,
        in_specs=specs,
        out_specs=jax.tree.map(lambda _: to, outs),
        scratch_shapes=list(scratch),
        compiler_params=pltpu.CompilerParams(vmem_limit_bytes=48 << 20),
    )


def per_device(background, obs_value, obs_error, obs_patch, obs_variable, obs_count, patch_corners, interp_weights):
    shape = jax.ShapeDtypeStruct
    devices = lax.axis_size("mem")
    regions = lax.axis_size("reg")
    own, _, all_patches, fields = background.shape
    patches = all_patches // devices
    members = own * devices
    points = obs_value.shape[0] * obs_value.shape[1]
    columns = patches * fields
    copies = [pltpu.SemaphoreType.DMA((own,))]

    outgoing = call(outgoing_kernel, shape((devices, own, patches, fields), BF16), [HBM], copies, HBM)(
        pltpu.with_memory_space_constraint(background.reshape(own, devices, patches, fields), pltpu.HBM)
    )
    ensemble = lax.all_to_all(outgoing, "mem", split_axis=0, concat_axis=0, tiled=True).reshape(members, patches, fields)
    dense, values, mix = call(
        prepare_kernel,
        (shape((points, patches, fields), F32), shape((points, patches, fields), F32), shape((9, patches, fields), F32)),
        [SMEM] + [VMEM] * 6,
    )(obs_count, obs_value, obs_error, obs_patch, obs_variable, patch_corners[0], interp_weights[0])

    pair = shape((2, members, members), BF16)
    packed = (members // 2 + 16, members)
    lefts = [pltpu.VMEM((2, members + 16, columns), BF16)] * 2
    wide = pltpu.VMEM((members * patches, fields), F32)
    one, sent, x, high, centre = call(
        first_kernel,
        (pair, shape((2,) + packed, BF16), shape((members, columns), BF16), shape((members, columns), BF16), shape((patches, fields), F32)),
        [VMEM] * 3,
        [wide] + lefts,
    )(ensemble, dense, values)
    beside = lax.ppermute(sent, "reg", [(r + 1, r) for r in range(regions - 1)])
    two, top = call(second_kernel, (pair, shape((3,) + packed, BF16)), [VMEM] * 5, lefts)(x, centre, dense, values, sent)
    top = lax.dynamic_update_slice(top, beside[:1], (2, 0, 0))
    below = lax.ppermute(top, "mem", [((d + 1) % devices, d) for d in range(devices)])
    whole = pltpu.VMEM((3, members, members), BF16)
    partial = call(own_kernel, shape((members, columns), F32), [VMEM] * 5, [whole])(one, two, beside, high, mix)
    analysis = call(last_kernel, shape((members, patches, fields), BF16), [VMEM] * 5, [wide, whole])(below, high, mix, partial, centre)
    returned = lax.all_to_all(analysis.reshape(devices, own, patches, fields), "mem", split_axis=0, concat_axis=0, tiled=True)
    result = call(returned_kernel, shape((own, devices, patches, fields), BF16), [VMEM], copies, HBM)(returned)
    return result.reshape(own, 1, all_patches, fields)


def solution(mesh):
    placed = (
        P("mem", "reg", None, None),
        P("mem", "reg", None),
        P("mem", "reg", None),
        P("mem", "reg", None),
        P("mem", "reg", None),
        P("mem", "reg"),
        P("reg", "mem", None),
        P("reg", "mem", None),
    )
    return jax.shard_map(
        per_device,
        mesh=mesh,
        in_specs=placed,
        out_specs=P("mem", "reg", None, None),
        check_vma=False,
    )
```

time: 81.8 us -> 90.7 us (1.11)
  Pallas kernels: 13 us -> 29 us
  local copies, waits for them, and re-layouts: 5.2 us -> 0.79 us
  waiting for transfers between devices: 23.1 us -> 20.6 us
    pallas_call x4 -> x6, Pallas kernels: 11.9 us -> 28 us  [the longest x1 17 us: per_device(): call(outgoing_kernel, shape((devices, own, patches, fields), BF16), [HBM]...]
    unnamed x20 -> x14, local copies, waits for them, and re-layouts: 2.36 us -> 0.63 us
    ppermute x1, waiting for transfers between devices: 3.18 us -> 1.76 us  [per_device(): beside = lax.ppermute(sent, 'reg', [(r + 1, r) for r in range(regions - 1)])]
    ppermute x1, waiting for transfers between devices: 4.46 us -> 3.39 us  [per_device(): lax.ppermute(top, 'mem', [((d + 1) % devices, d) for d in range(devices)])]
    slice x4 -> x0, local copies, waits for them, and re-layouts: 0.91 us -> none  [per_device(): top = jnp.stack([one[0], two[0], beside[0]])]
  transfers between devices with their start and end apart: 3 -> 3, of which waited for: 3 -> 3; matrix products, arithmetic and copies ran while one was open for 0% -> 0% of each run, Pallas kernels for 9% -> 7%
where the time goes in v2:
time: 90.7 us; the launch traced here: 90.4 us
  Pallas kernels  29 us (32%)
  blocking collectives  24.4 us (27%)
  waiting for transfers between devices  20.6 us (23%)
  starting transfers between devices  15.5 us (17%)
    all_to_all x1, blocking collectives, per_device(): lax.all_to_all(analysis.reshape(devices, own, patches, fields), 'mem', sp...  24.4 us
    pallas_call x1, Pallas kernels, per_device(): call(outgoing_kernel, shape((devices, own, patches, fields), BF16), [HBM]...  17 us
    all_to_all x1, waiting for transfers between devices, per_device(): lax.all_to_all(outgoing, 'mem', split_axis=0, concat_axis=0, tiled=True)  15.4 us
    all_to_all x1, starting transfers between devices, per_device(): lax.all_to_all(outgoing, 'mem', split_axis=0, concat_axis=0, tiled=True)  13.1 us
    pallas_call x1, Pallas kernels, per_device(): call(first_kernel, (pair, shape((2,) + packed, BF16), shape((members, col...  4.35 us
    pallas_call x1, Pallas kernels, per_device(): call(second_kernel, (pair, shape((3,) + packed, BF16)), [VMEM] * 5, lefts)  4.01 us
    ppermute x1, waiting for transfers between devices, per_device(): lax.ppermute(top, 'mem', [((d + 1) % devices, d) for d in range(devices)])  3.39 us
  transfers between devices with their start and end apart: 3, of which 3 were waited for; matrix products, arithmetic and copies ran while one was open for 0% of the time, Pallas kernels for 7%

profile of v2, /device:TPU:1, one launch (start us, length us, event | category | flops | bytes accessed | tf_op | source)
XLA Modules:
  0.0 90.4 jit_solution(11442726397239795819)
XLA Ops:
  0.0 17.0 %shard_map.82 = bf16[64,4,8,128]{3,2,1,0:T(8,128)(2,1)} custom-call(bf16[4,64,8,128]{3,2,1,0:T(8,128)(2,1)} %bitcast.10), custom_call_target="tpu_custom_call" | custom-call | tf_op jit(solution)/shard_map/pallas_call | solution.py:250
  17.0 0.0 copy-start.5
  17.0 0.0 copy-start.6
  17.0 0.0 copy-start.1
  17.1 0.0 copy-start.2
  17.1 0.0 copy-start.3
  17.1 13.1 %all-to-all-start = ((bf16[64,4,8,128]{3,2,1,0:T(8,128)(2,1)}), bf16[64,4,8,128]{3,2,1,0:T(8,128)(2,1)S(1)}, u32[]{:S(2)}, u32[]{:S(2)}) async-start(bf16[64,4,8,128]{3,2,1,0:T(8,128)(2,1)} %shard_map.82), calls=%async_computation | async-start | bytes 1048576 | tf_op jit(solution)/shard_map/all_to_all | solution.py:253
  30.2 0.0 copy-start
  30.2 0.0 copy-done.5
  30.2 0.1 copy.9.corner_ref
  30.3 0.0 copy-done.6
  30.3 0.0 copy-start.4
  30.3 0.1 copy.10.coeff_ref
  30.4 0.0 copy-done.1
  30.4 0.0 copy-done.2
  30.4 0.0 copy-done.3
  30.4 0.5 copy-done
  30.9 0.1 copy-done.4
  31.0 1.1 %shard_map.83 = (f32[4,8,128]{2,1,0:T(8,128)S(1)}, f32[4,8,128]{2,1,0:T(8,128)S(1)}, f32[9,8,128]{2,1,0:T(8,128)S(1)}) custom-call(s32[2,2]{1,0:T(2,128)S(1)} %copy-done.4, f32[2,2,512]{2,1,0:T(2,128)S(1)} %copy-done, f32[2,2,512]{2,1,0:T(2,128)S(1)} %copy-done.1, s32[2,2,512]{2,1,0:T(2,128)S(1)} %copy-done.2, s32[2,2,512]{2,1,0:T(2,128)S(1)} %copy-done.3, ...), custom_call_target="tpu_custom_call" | custom-call | tf_op jit(solution)/shard_map/pallas_call | solution.py:254
  32.1 15.4 %all-to-all-done = bf16[64,4,8,128]{3,2,1,0:T(8,128)(2,1)S(1)} async-done(((bf16[64,4,8,128]{3,2,1,0:T(8,128)(2,1)}), bf16[64,4,8,128]{3,2,1,0:T(8,128)(2,1)S(1)}, u32[]{:S(2)}, u32[]{:S(2)}) %all-to-all-start) | async-done | bytes 524320 | tf_op jit(solution)/shard_map/all_to_all | solution.py:253
  47.5 4.3 %shard_map.84 = (bf16[2,256,256]{2,1,0:T(8,128)(2,1)S(1)}, bf16[2,144,256]{2,1,0:T(8,128)(2,1)S(1)}, bf16[256,1024]{1,0:T(8,128)(2,1)S(1)}, bf16[256,1024]{1,0:T(8,128)(2,1)S(1)}, f32[8,128]{1,0:T(8,128)S(1)}) custom-call(bf16[256,8,128]{2,1,0:T(8,128)(2,1)S(1)} %bitcast.8, f32[4,8,128]{2,1,0:T(8,128)S(1)} %get-tuple-element.15.dense_ref, ...), custom_call_target="tpu_custom_call" | custom-call | tf_op jit(solution)/shard_map/pallas_call | solution.py:264
  51.9 1.3 %collective-permute-start = (bf16[2,144,256]{2,1,0:T(8,128)(2,1)S(1)}, bf16[2,144,256]{2,1,0:T(8,128)(2,1)S(1)}, u32[]{:S(2)}, u32[]{:S(2)}) collective-permute-start(bf16[2,144,256]{2,1,0:T(8,128)(2,1)S(1)} %get-tuple-element.19.sent_ref), channel_id=1, source_target_pairs={{1,0},{2,1},{3,2},{5,4},{6,5},{7,6},{9,8},{10,9},{11,10},{13,12},{... | collective-permute-start | bytes 442376 | tf_op jit(solution)/shard_map/ppermute | solution.py:270
  53.2 4.0 %shard_map.85 = (bf16[2,256,256]{2,1,0:T(8,128)(2,1)S(1)}, bf16[3,144,256]{2,1,0:T(8,128)(2,1)S(1)}) custom-call(bf16[256,1024]{1,0:T(8,128)(2,1)S(1)} %get-tuple-element.17.x_ref, f32[8,128]{1,0:T(8,128)S(1)} %get-tuple-element.18.centre_ref, f32[4,8,128]{2,1,0:T(8,128)S(1)} %get-tuple-element.15.dense_ref, f32[4,8,128]{2,1,0:T(8,128)S(1)} %get-tuple-element.16.value_ref, ...), custom_call_target="tpu_custom_call" | custom-call | tf_op jit(solution)/shard_map/pallas_call | solution.py:271
  57.2 1.8 %collective-permute-done.beside_ref = bf16[2,144,256]{2,1,0:T(8,128)(2,1)S(1)} collective-permute-done((bf16[2,144,256]{2,1,0:T(8,128)(2,1)S(1)}, bf16[2,144,256]{2,1,0:T(8,128)(2,1)S(1)}, u32[]{:S(2)}, u32[]{:S(2)}) %collective-permute-start) | collective-permute-done | bytes 147488 | tf_op jit(solution)/shard_map/ppermute | solution.py:270
  58.9 1.1 %collective-permute-start.1 = (bf16[3,144,256]{2,1,0:T(8,128)(2,1)S(1)}, bf16[3,144,256]{2,1,0:T(8,128)(2,1)S(1)}, u32[]{:S(2)}, u32[]{:S(2)}) collective-permute-start(bf16[3,144,256]{2,1,0:T(8,128)(2,1)S(1)} %slice_dynamic-update-slice_fusion), channel_id=1, source_target_pairs={{4,0},{8,4},{12,8},{16,12},{20,16},{24,20},{28,24},{32,28},{36,32}... | collective-permute-start | bytes 663560 | tf_op jit(solution)/shard_map/ppermute | solution.py:273
  60.0 1.0 %shard_map.86.partial_ref = f32[256,1024]{1,0:T(8,128)S(1)} custom-call(bf16[2,256,256]{2,1,0:T(8,128)(2,1)S(1)} %get-tuple-element.23.one_ref, bf16[2,256,256]{2,1,0:T(8,128)(2,1)S(1)} %get-tuple-element.24.two_ref, bf16[2,144,256]{2,1,0:T(8,128)(2,1)S(1)} %collective-permute-done.beside_ref, bf16[256,1024]{1,0:T(8,128)(2,1)S(1)} %get-tuple-element.21.high_ref, ...), custom_call_target="tpu_custom_call" | custom-call | tf_op jit(solution)/shard_map/pallas_call | solution.py:275
  61.0 3.4 %collective-permute-done.1.below_ref = bf16[3,144,256]{2,1,0:T(8,128)(2,1)S(1)} collective-permute-done((bf16[3,144,256]{2,1,0:T(8,128)(2,1)S(1)}, bf16[3,144,256]{2,1,0:T(8,128)(2,1)S(1)}, u32[]{:S(2)}, u32[]{:S(2)}) %collective-permute-start.1) | collective-permute-done | bytes 221216 | tf_op jit(solution)/shard_map/ppermute | solution.py:273
  64.4 0.8 shard_map.87
  65.2 24.4 %all_to_all.10.source_ref = bf16[64,4,8,128]{3,2,1,0:T(8,128)(2,1)S(1)} all-to-all(bf16[64,4,8,128]{3,2,1,0:T(8,128)(2,1)S(1)} %bitcast.9), channel_id=1, replica_groups=mesh['mem'=64,'reg'=4] {'mem'}, dimensions={0} | all-to-all | bytes 1048576 | tf_op jit(solution)/shard_map/all_to_all | solution.py:277
  89.6 0.8 shard_map.88
  (1 shorter events, 0.0 us)
Async XLA Ops:
  17.0 13.2 %copy-start.5 = (s32[1,8,4]{1,2,0:T(4,128)S(1)}, s32[1,8,4]{1,2,0:T(4,128)}, u32[]{:S(2)}) copy-start(s32[1,8,4]{1,2,0:T(4,128)} %param.14) | copy-start | bytes 388
  17.0 13.3 %copy-start.6 = (f32[1,8,4]{1,2,0:T(4,128)S(1)}, f32[1,8,4]{1,2,0:T(4,128)}, u32[]{:S(2)}) copy-start(f32[1,8,4]{1,2,0:T(4,128)} %param.15) | copy-start | bytes 388
  17.0 13.4 %copy-start.1 = (f32[2,2,512]{2,1,0:T(2,128)S(1)}, f32[2,2,512]{2,1,0:T(2,128)}, u32[]{:S(2)}) copy-start(f32[2,2,512]{2,1,0:T(2,128)} %error_ref.1) | copy-start | bytes 24580
  17.1 13.3 %copy-start.2 = (s32[2,2,512]{2,1,0:T(2,128)S(1)}, s32[2,2,512]{2,1,0:T(2,128)}, u32[]{:S(2)}) copy-start(s32[2,2,512]{2,1,0:T(2,128)} %patch_ref.1) | copy-start | bytes 24580
  17.1 13.3 %copy-start.3 = (s32[2,2,512]{2,1,0:T(2,128)S(1)}, s32[2,2,512]{2,1,0:T(2,128)}, u32[]{:S(2)}) copy-start(s32[2,2,512]{2,1,0:T(2,128)} %var_ref.1) | copy-start | bytes 24580
  17.1 30.4 %all-to-all-start = ((bf16[64,4,8,128]{3,2,1,0:T(8,128)(2,1)}), bf16[64,4,8,128]{3,2,1,0:T(8,128)(2,1)S(1)}, u32[]{:S(2)}, u32[]{:S(2)}) async-start(bf16[64,4,8,128]{3,2,1,0:T(8,128)(2,1)} %shard_map.82), calls=%async_computation | async-start | bytes 1048576 | tf_op jit(solution)/shard_map/all_to_all | solution.py:253
  30.2 0.7 copy-start
  30.3 0.7 copy-start.4
  51.9 7.1 %collective-permute-start = (bf16[2,144,256]{2,1,0:T(8,128)(2,1)S(1)}, bf16[2,144,256]{2,1,0:T(8,128)(2,1)S(1)}, u32[]{:S(2)}, u32[]{:S(2)}) collective-permute-start(bf16[2,144,256]{2,1,0:T(8,128)(2,1)S(1)} %get-tuple-element.19.sent_ref), channel_id=1, source_target_pairs={{1,0},{2,1},{3,2},{5,4},{6,5},{7,6},{9,8},{10,9},{11,10},{13,12},{... | collective-permute-start | bytes 442376 | tf_op jit(solution)/shard_map/ppermute | solution.py:270
  58.9 5.5 %collective-permute-start.1 = (bf16[3,144,256]{2,1,0:T(8,128)(2,1)S(1)}, bf16[3,144,256]{2,1,0:T(8,128)(2,1)S(1)}, u32[]{:S(2)}, u32[]{:S(2)}) collective-permute-start(bf16[3,144,256]{2,1,0:T(8,128)(2,1)S(1)} %slice_dynamic-update-slice_fusion), channel_id=1, source_target_pairs={{4,0},{8,4},{12,8},{16,12},{20,16},{24,20},{28,24},{32,28},{36,32}... | collective-permute-start | bytes 663560 | tf_op jit(solution)/shard_map/ppermute | solution.py:273

commit v3 on v2

--- a/solution.py
+++ b/solution.py
@@ -4,6 +4,7 @@
 from jax.experimental import pallas as pl
 from jax.experimental.pallas import tpu as pltpu
 from jax.sharding import PartitionSpec as P
+
 
 F32 = jnp.float32
 BF16 = jnp.bfloat16
@@ -57,28 +58,38 @@
         mix_ref[t] = jnp.broadcast_to(used, (patches, fields))
 
 
-def shares(points, x_ref, centre, dense_ref, value_ref, left_high, left_low):
-    members = x_ref.shape[0]
+def shares(points, pert_ref, centre, dense_ref, value_ref, left_high, left_low):
+    members = pert_ref.shape[0]
     patches, fields = centre.shape
-    for slot, n in enumerate(points):
-        dense = dense_ref[n]
-        pull = value_ref[n] - dense * centre
-        for p in range(patches):
-            lanes = slice(p * fields, (p + 1) * fields)
-            scaled = (x_ref[:, lanes].astype(F32) - centre[p : p + 1, :]) * dense[p : p + 1, :]
-            left_high[slot, :members, lanes], left_low[slot, :members, lanes] = split(scaled)
-            tail = jnp.broadcast_to(pull[p : p + 1, :], (left_high.shape[1] - members, fields))
+    pulls = [value_ref[n] - dense_ref[n] * centre for n in points]
+    for p in range(patches):
+        lanes = slice(p * fields, (p + 1) * fields)
+        pert = pert_ref[:, lanes]
+        for slot, n in enumerate(points):
+            left_high[slot, :members, lanes], left_low[slot, :members, lanes] = split(pert * dense_ref[n, p : p + 1, :])
+            tail = jnp.broadcast_to(pulls[slot][p : p + 1, :], (left_high.shape[1] - members, fields))
             left_high[slot, members:, lanes], left_low[slot, members:, lanes] = split(tail)
 
 
-def two_factors(x, square):
-    return 0.375 * square - 0.5 * x + product(split(square), split(0.0625 * square - 0.3125 * x))
+def add_diagonal(x, value, diagonal):
+    half = diagonal.shape[0]
+    step = jnp.where(diagonal, value, 0.0)
+    top = jnp.concatenate([x[:half, :half] + step, x[:half, half:]], axis=1)
+    bottom = jnp.concatenate([x[half:, :half], x[half:, half:] + step], axis=1)
+    return jnp.concatenate([top, bottom], axis=0)
+
+
+def two_factors(x, parts, diagonal):
+    square = product(parts, parts)
+    inner = add_diagonal(square - 4.5 * x, 6.75, diagonal)
+    return add_diagonal(product(split(square), split(inner)) - 4.875 * x, 2.25, diagonal)
 
 
 def weights_of(count, x_ref, left_high, left_low, out_ref):
     members = x_ref.shape[0]
-    row = lax.broadcasted_iota(jnp.int32, (members, members), 0)
-    col = lax.broadcasted_iota(jnp.int32, (members, members), 1)
+    half = members // 2
+    row = lax.broadcasted_iota(jnp.int32, (half, half), 0)
+    col = lax.broadcasted_iota(jnp.int32, (half, half), 1)
     diagonal = row == col
     slots = range(count)
     state = []
@@ -87,34 +98,33 @@
         both = dot(left_high[slot], columns, NT) + dot(left_low[slot], columns, NT)
         both = both - jnp.sum(both, axis=1, keepdims=True) * (1.0 / members)
         gram, projected = both[:members], both[members : members + 1]
-        trace = jnp.sum(jnp.sum(jnp.where(diagonal, gram, 0.0), axis=0, keepdims=True), axis=1, keepdims=True)
+        on_diagonal = jnp.where(diagonal, gram[:half, :half] + gram[half:, half:], 0.0)
+        trace = jnp.sum(jnp.sum(on_diagonal, axis=0, keepdims=True), axis=1, keepdims=True)
         scaling = (members - 1.0) + trace / members
-        inverse_scaling = 1.0 / scaling
-        state.append((projected, scaling, gram * inverse_scaling + jnp.where(diagonal, (members - 1.0) * inverse_scaling - 1.0, 0.0)))
-    r = [split(x) for _, _, x in state]
-    squares = [product(x, x) for x in r]
-    w = [two_factors(state[s][2], squares[s]) for s in slots]
-    w_parts = [split(x) for x in w]
-    v = [state[s][2] + w[s] + product(r[s], w_parts[s]) for s in slots]
-    e = [v[s] + w[s] + product(split(v[s]), w_parts[s]) for s in slots]
-    e_parts = [split(x) for x in e]
-    squares = [product(x, x) for x in e_parts]
-    h = [two_factors(e[s], squares[s]) for s in slots]
-    inverses = [w[s] + h[s] + product(w_parts[s], split(h[s])) for s in slots]
-    half = members // 2
-    small_row, small_col = row[:half, :half], col[:half, :half]
-    tail_row = lax.broadcasted_iota(jnp.int32, (16, members), 0)
+        half_inverse = 0.5 / scaling
+        state.append((projected, scaling, add_diagonal(gram * half_inverse, (members - 1.0) * half_inverse, diagonal)))
+    parts = [split(x) for _, _, x in state]
+    z = [split(two_factors(state[s][2], parts[s], diagonal)) for s in slots]
+    y = [split(product(parts[s], z[s])) for s in slots]
+    c = [product(y[s], z[s]) for s in slots]
+    f = [split(two_factors(c[s], split(c[s]), diagonal)) for s in slots]
+    inverses = [product(f[s], z[s]) for s in slots]
     for slot in slots:
         projected, scaling, _ = state[slot]
-        inverse = inverses[slot] + jnp.where(diagonal, 1.0, 0.0)
+        inverse = inverses[slot]
         once = jnp.sum(inverse * projected, axis=1, keepdims=True)
         twice = jnp.sum(inverse * once, axis=0, keepdims=True) / scaling
         spread = jnp.sqrt((members - 1.0) / scaling) * inverse
         out_ref[slot] = (spread + twice).astype(BF16)
-        yield slot, spread, twice, half, small_row, small_col, tail_row
-
-
-def pack(target, slot, spread, twice, half, small_row, small_col, tail_row):
+        yield slot, spread, twice
+
+
+def pack(target, slot, spread, twice):
+    members = spread.shape[0]
+    half = members // 2
+    small_row = lax.broadcasted_iota(jnp.int32, (half, half), 0)
+    small_col = lax.broadcasted_iota(jnp.int32, (half, half), 1)
+    tail_row = lax.broadcasted_iota(jnp.int32, (16, members), 0)
     corner = spread[half:, half:]
     target[slot, :half, :half] = jnp.where(small_row >= small_col, spread[:half, :half], corner).astype(BF16)
     target[slot, :half, half:] = spread[:half, half:].astype(BF16)
@@ -142,7 +152,7 @@
     target[place, half:, half:] = (corner + right).astype(BF16)
 
 
-def first_kernel(ensemble_ref, dense_ref, value_ref, out_ref, pack_ref, x_ref, high_ref, centre_ref, wide_ref, left_high, left_low):
+def first_kernel(ensemble_ref, dense_ref, value_ref, out_ref, pack_ref, corner_ref, x_ref, pert_ref, high_ref, centre_ref, wide_ref, left_high, left_low):
     members, patches, fields = ensemble_ref.shape
     total = jnp.zeros((patches, fields), F32)
     chunk = 32
@@ -156,19 +166,22 @@
         lanes = slice(p * fields, (p + 1) * fields)
         part = wide_ref[pl.ds(p, members, stride=patches), :]
         x_ref[:, lanes] = part.astype(BF16)
-        high_ref[:, lanes] = (part - centre[p : p + 1, :]).astype(BF16)
-    shares((0, 2), x_ref, centre, dense_ref, value_ref, left_high, left_low)
-    for slot, *rest in weights_of(2, x_ref, left_high, left_low, out_ref):
-        pack(pack_ref, slot, *rest)
-
-
-def second_kernel(x_ref, centre_ref, dense_ref, value_ref, sent_ref, out_ref, pack_ref, left_high, left_low):
-    shares((1, 3), x_ref, centre_ref[...], dense_ref, value_ref, left_high, left_low)
+        pert = part - centre[p : p + 1, :]
+        pert_ref[:, lanes] = pert
+        high_ref[:, lanes] = pert.astype(BF16)
+    shares((0, 2), pert_ref, centre, dense_ref, value_ref, left_high, left_low)
+    for slot, spread, twice in weights_of(2, x_ref, left_high, left_low, out_ref):
+        pack(pack_ref, slot, spread, twice)
+        if slot == 0:
+            corner_ref[0] = pack_ref[0]
+
+
+def second_kernel(x_ref, pert_ref, centre_ref, dense_ref, value_ref, sent_ref, out_ref, pack_ref, left_high, left_low):
     pack_ref[0] = sent_ref[0]
-    for slot, *rest in weights_of(2, x_ref, left_high, left_low, out_ref):
+    shares((1, 3), pert_ref, centre_ref[...], dense_ref, value_ref, left_high, left_low)
+    for slot, spread, twice in weights_of(2, x_ref, left_high, left_low, out_ref):
         if slot == 0:
-            pack(pack_ref, 1, *rest)
-    pack_ref[2] = jnp.zeros(pack_ref.shape[1:], BF16)
+            pack(pack_ref, 1, spread, twice)
 
 
 def blend(parts, high_ref, mix_ref, p):
@@ -192,9 +205,10 @@
         out_ref[:, p * fields : (p + 2) * fields] = blend(parts, high_ref, mix_ref, p)
 
 
-def last_kernel(below_ref, high_ref, mix_ref, partial_ref, centre_ref, out_ref, all_ref, whole_ref):
-    for slot in range(3):
-        unpack(below_ref, slot, whole_ref, slot)
+def last_kernel(below_ref, diagonal_ref, high_ref, mix_ref, partial_ref, centre_ref, out_ref, all_ref, whole_ref):
+    unpack(below_ref, 0, whole_ref, 0)
+    unpack(below_ref, 1, whole_ref, 1)
+    unpack(diagonal_ref, 0, whole_ref, 2)
     parts = ((6, whole_ref, 0), (7, whole_ref, 1), (8, whole_ref, 2))
     members, patches, fields = out_ref.shape
     for p in range(0, patches, 2):
@@ -209,14 +223,6 @@
         out_ref[k : k + chunk] = part.reshape(chunk, patches, fields).astype(BF16)
 
 
-def outgoing_kernel(source_ref, target_ref, done):
-    copies = [pltpu.make_async_copy(source_ref.at[m], target_ref.at[:, m], done.at[m]) for m in range(source_ref.shape[0])]
-    for copy in copies:
-        copy.start()
-    for copy in copies:
-        copy.wait()
-
-
 def returned_kernel(source_ref, target_ref, done):
     copies = [pltpu.make_async_copy(source_ref.at[:, m], target_ref.at[m], done.at[m]) for m in range(target_ref.shape[0])]
     for copy in copies:
@@ -247,9 +253,7 @@
     columns = patches * fields
     copies = [pltpu.SemaphoreType.DMA((own,))]
 
-    outgoing = call(outgoing_kernel, shape((devices, own, patches, fields), BF16), [HBM], copies, HBM)(
-        pltpu.with_memory_space_constraint(background.reshape(own, devices, patches, fields), pltpu.HBM)
-    )
+    outgoing = jnp.transpose(background.reshape(own, devices, patches, fields), (1, 0, 2, 3))
     ensemble = lax.all_to_all(outgoing, "mem", split_axis=0, concat_axis=0, tiled=True).reshape(members, patches, fields)
     dense, values, mix = call(
         prepare_kernel,
@@ -261,19 +265,23 @@
     packed = (members // 2 + 16, members)
     lefts = [pltpu.VMEM((2, members + 16, columns), BF16)] * 2
     wide = pltpu.VMEM((members * patches, fields), F32)
-    one, sent, x, high, centre = call(
+    flat = (members, columns)
+    one, sent, corner, x, pert, high, centre = call(
         first_kernel,
-        (pair, shape((2,) + packed, BF16), shape((members, columns), BF16), shape((members, columns), BF16), shape((patches, fields), F32)),
+        (pair, shape((2,) + packed, BF16), shape((1,) + packed, BF16), shape(flat, BF16), shape(flat, F32), shape(flat, BF16), shape((patches, fields), F32)),
         [VMEM] * 3,
         [wide] + lefts,
     )(ensemble, dense, values)
-    beside = lax.ppermute(sent, "reg", [(r + 1, r) for r in range(regions - 1)])
-    two, top = call(second_kernel, (pair, shape((3,) + packed, BF16)), [VMEM] * 5, lefts)(x, centre, dense, values, sent)
-    top = lax.dynamic_update_slice(top, beside[:1], (2, 0, 0))
-    below = lax.ppermute(top, "mem", [((d + 1) % devices, d) for d in range(devices)])
+    down = [((d + 1) % devices, d) for d in range(devices)]
+    across = [(r + 1, r) for r in range(regions - 1)]
+    both = [(d * regions + r, e * regions + t) for d, e in down for r, t in across]
+    beside = lax.ppermute(sent, "reg", across)
+    diagonal = lax.ppermute(corner, ("mem", "reg"), both)
+    two, top = call(second_kernel, (pair, shape((2,) + packed, BF16)), [VMEM] * 6, lefts)(x, pert, centre, dense, values, sent)
+    below = lax.ppermute(top, "mem", down)
     whole = pltpu.VMEM((3, members, members), BF16)
-    partial = call(own_kernel, shape((members, columns), F32), [VMEM] * 5, [whole])(one, two, beside, high, mix)
-    analysis = call(last_kernel, shape((members, patches, fields), BF16), [VMEM] * 5, [wide, whole])(below, high, mix, partial, centre)
+    partial = call(own_kernel, shape(flat, F32), [VMEM] * 5, [whole])(one, two, beside, high, mix)
+    analysis = call(last_kernel, shape((members, patches, fields), BF16), [VMEM] * 6, [wide, whole])(below, diagonal, high, mix, partial, centre)
     returned = lax.all_to_all(analysis.reshape(devices, own, patches, fields), "mem", split_axis=0, concat_axis=0, tiled=True)
     result = call(returned_kernel, shape((own, devices, patches, fields), BF16), [VMEM], copies, HBM)(returned)
     return result.reshape(own, 1, all_patches, fields)

time: 90.7 us -> 76.2 us (0.84)
  Pallas kernels: 29 us -> 11.4 us
  local copies, waits for them, and re-layouts: 0.79 us -> 2.7 us
    pallas_call x5 -> x4, Pallas kernels: 27.2 us -> 9.56 us  [the longest x1 4.06 us: per_device(): call(first_kernel, (pair, shape((2,) + packed, BF16), shape((1,) + packed...]
    unnamed x14 -> x16, local copies, waits for them, and re-layouts: 0.63 us -> 1.66 us
    ppermute x2 -> x3, starting transfers between devices: 2.37 us -> 2.86 us  [the longest x1 1.29 us: per_device(): beside = lax.ppermute(sent, 'reg', across)]
    ppermute x2 -> x3, waiting for transfers between devices: 5.15 us -> 5.04 us  [the longest x1 4.54 us: per_device(): diagonal = lax.ppermute(corner, ('mem', 'reg'), both)]
  transfers between devices with their start and end apart: 3 -> 4, of which waited for: 3 -> 3; matrix products, arithmetic and copies ran while one was open for 0% -> 0% of each run, Pallas kernels for 7% -> 8%
where the time goes in v3:
time: 76.2 us; the launch traced here: 75.4 us
  blocking collectives  24.7 us (32%)
  waiting for transfers between devices  20.5 us (27%)
  starting transfers between devices  16 us (21%)
  Pallas kernels  11.4 us (15%)
  local copies, waits for them, and re-layouts  2.7 us (4%)
    all_to_all x1, blocking collectives, per_device(): lax.all_to_all(analysis.reshape(devices, own, patches, fields), 'mem', sp...  24.7 us
    all_to_all x1, waiting for transfers between devices, per_device(): lax.all_to_all(outgoing, 'mem', split_axis=0, concat_axis=0, tiled=True)  15.4 us
    all_to_all x1, starting transfers between devices, per_device(): lax.all_to_all(outgoing, 'mem', split_axis=0, concat_axis=0, tiled=True)  13.1 us
    ppermute x1, waiting for transfers between devices, per_device(): diagonal = lax.ppermute(corner, ('mem', 'reg'), both)  4.54 us
    pallas_call x1, Pallas kernels, per_device(): call(first_kernel, (pair, shape((2,) + packed, BF16), shape((1,) + packed...  4.06 us
    pallas_call x1, Pallas kernels, per_device(): call(second_kernel, (pair, shape((2,) + packed, BF16)), [VMEM] * 6, lefts)  3.7 us
    unnamed x16, local copies, waits for them, and re-layouts  1.66 us
  transfers between devices with their start and end apart: 4, of which 3 were waited for; matrix products, arithmetic and copies ran while one was open for 0% of the time, Pallas kernels for 8%

profile of v3, /device:TPU:1, one launch (start us, length us, event | category | flops | bytes accessed | tf_op | source)
XLA Modules:
  0.0 75.4 jit_solution(710267132011355005)
XLA Ops:
  0.0 0.0 copy-start
  0.0 1.0 %copy-done = bf16[4,1,512,128]{3,2,1,0:T(8,128)(2,1)S(1)} copy-done((bf16[4,1,512,128]{3,2,1,0:T(8,128)(2,1)S(1)}, bf16[4,1,512,128]{3,2,1,0:T(8,128)(2,1)}, u32[]{:S(2)}) %copy-start) | copy-done | bytes 524312
  1.0 0.9 %copy_bitcast_fusion = bf16[64,4,8,128]{3,2,1,0:T(8,128)(2,1)} fusion(bf16[4,1,512,128]{3,2,1,0:T(8,128)(2,1)S(1)} %copy-done), kind=kLoop, calls=%fused_computation | loop fusion | bytes 1048576 | tf_op jit(solution)/shard_map/transpose | solution.py:256
  1.9 0.0 copy-start.6
  1.9 0.0 copy-start.7
  1.9 0.0 copy-start.2
  1.9 0.0 copy-start.3
  1.9 0.0 copy-start.4
  1.9 13.1 %all-to-all-start = ((bf16[64,4,8,128]{3,2,1,0:T(8,128)(2,1)}), bf16[64,4,8,128]{3,2,1,0:T(8,128)(2,1)S(1)}, u32[]{:S(2)}, u32[]{:S(2)}) async-start(bf16[64,4,8,128]{3,2,1,0:T(8,128)(2,1)} %copy_bitcast_fusion), calls=%async_computation | async-start | bytes 1048576 | tf_op jit(solution)/shard_map/all_to_all | solution.py:257
  15.1 0.0 copy-start.1
  15.1 0.0 copy-done.6
  15.1 0.1 copy.10.corner_ref
  15.2 0.0 copy-done.7
  15.2 0.0 copy-start.5
  15.2 0.1 copy.11.coeff_ref
  15.3 0.0 copy-done.2
  15.3 0.0 copy-done.3
  15.3 0.0 copy-done.4
  15.3 0.5 copy-done.1
  15.8 0.1 copy-done.5
  15.9 1.1 %shard_map.82 = (f32[4,8,128]{2,1,0:T(8,128)S(1)}, f32[4,8,128]{2,1,0:T(8,128)S(1)}, f32[9,8,128]{2,1,0:T(8,128)S(1)}) custom-call(s32[2,2]{1,0:T(2,128)S(1)} %copy-done.5, f32[2,2,512]{2,1,0:T(2,128)S(1)} %copy-done.1, f32[2,2,512]{2,1,0:T(2,128)S(1)} %copy-done.2, s32[2,2,512]{2,1,0:T(2,128)S(1)} %copy-done.3, s32[2,2,512]{2,1,0:T(2,128)S(1)} %copy-done.4, ...), custom_call_target="tpu_custom_call" | custom-call | tf_op jit(solution)/shard_map/pallas_call | solution.py:258
  16.9 15.4 %all-to-all-done = bf16[64,4,8,128]{3,2,1,0:T(8,128)(2,1)S(1)} async-done(((bf16[64,4,8,128]{3,2,1,0:T(8,128)(2,1)}), bf16[64,4,8,128]{3,2,1,0:T(8,128)(2,1)S(1)}, u32[]{:S(2)}, u32[]{:S(2)}) %all-to-all-start) | async-done | bytes 524320 | tf_op jit(solution)/shard_map/all_to_all | solution.py:257
  32.4 4.1 %shard_map.83 = (bf16[2,256,256]{2,1,0:T(8,128)(2,1)S(1)}, bf16[2,144,256]{2,1,0:T(8,128)(2,1)S(1)}, bf16[1,144,256]{2,1,0:T(8,128)(2,1)S(1)}, bf16[256,1024]{1,...) custom-call(bf16[256,8,128]{2,1,0:T(8,128)(2,1)S(1)} %bitcast.12, ...), custom_call_target="tpu_custom_call" | custom-call | tf_op jit(solution)/shard_map/pallas_call | solution.py:269
  36.4 1.3 %collective-permute-start.2 = (bf16[2,144,256]{2,1,0:T(8,128)(2,1)S(1)}, bf16[2,144,256]{2,1,0:T(8,128)(2,1)S(1)}, u32[]{:S(2)}, u32[]{:S(2)}) collective-permute-start(bf16[2,144,256]{2,1,0:T(8,128)(2,1)S(1)} %get-tuple-element.22.sent_ref), channel_id=1, source_target_pairs={{1,0},{2,1},{3,2},{5,4},{6,5},{7,6},{9,8},{10,9},{11,10},{13,12},{... | collective-permute-start | bytes 442376 | tf_op jit(solution)/shard_map/ppermute | solution.py:278
  37.7 3.7 %shard_map.84 = (bf16[2,256,256]{2,1,0:T(8,128)(2,1)S(1)}, bf16[2,144,256]{2,1,0:T(8,128)(2,1)S(1)}) custom-call(bf16[256,1024]{1,0:T(8,128)(2,1)S(1)} %get-tuple-element.19.x_ref, f32[256,1024]{1,0:T(8,128)S(1)} %get-tuple-element.20.pert_ref, f32[8,128]{1,0:T(8,128)S(1)} %get-tuple-element.21.centre_ref, f32[4,8,128]{2,1,0:T(8,128)S(1)} %get-tuple-element.17.dense_ref, ...), custom_call_target="tpu_custom_call" | custom-call | tf_op jit(solution)/shard_map/pallas_call | solution.py:280
  41.4 0.3 collective-permute-start
  41.7 1.3 %collective-permute-start.1 = (bf16[1,144,256]{2,1,0:T(8,128)(2,1)S(1)}, bf16[1,144,256]{2,1,0:T(8,128)(2,1)S(1)}, u32[]{:S(2)}, u32[]{:S(2)}) collective-permute-start(bf16[1,144,256]{2,1,0:T(8,128)(2,1)S(1)} %get-tuple-element.24), channel_id=1, source_target_pairs={{5,0},{6,1},{7,2},{9,4},{10,5},{11,6},{13,8},{14,9},{15,10},{17,12... | collective-permute-start | bytes 221192 | tf_op jit(solution)/shard_map/ppermute | solution.py:279
  43.0 0.5 collective-permute-done.2.beside_ref
  43.5 1.0 %shard_map.85.partial_ref = f32[256,1024]{1,0:T(8,128)S(1)} custom-call(bf16[2,256,256]{2,1,0:T(8,128)(2,1)S(1)} %get-tuple-element.27.one_ref, bf16[2,256,256]{2,1,0:T(8,128)(2,1)S(1)} %get-tuple-element.28.two_ref, bf16[2,144,256]{2,1,0:T(8,128)(2,1)S(1)} %collective-permute-done.2.beside_ref, bf16[256,1024]{1,0:T(8,128)(2,1)S(1)} %get-tuple-element.25.high_ref, ...), custom_call_target="tpu_custom_call" | custom-call | tf_op jit(solution)/shard_map/pallas_call | solution.py:283
  44.5 4.5 %collective-permute-done.1.diagonal_ref = bf16[1,144,256]{2,1,0:T(8,128)(2,1)S(1)} collective-permute-done((bf16[1,144,256]{2,1,0:T(8,128)(2,1)S(1)}, bf16[1,144,256]{2,1,0:T(8,128)(2,1)S(1)}, u32[]{:S(2)}, u32[]{:S(2)}) %collective-permute-start.1) | collective-permute-done | bytes 73760 | tf_op jit(solution)/shard_map/ppermute | solution.py:279
  49.1 0.0 collective-permute-done.below_ref
  49.1 0.8 %shard_map.86 = bf16[256,8,128]{2,1,0:T(8,128)(2,1)S(1)} custom-call(bf16[2,144,256]{2,1,0:T(8,128)(2,1)S(1)} %collective-permute-done.below_ref, bf16[1,144,256]{2,1,0:T(8,128)(2,1)S(1)} %collective-permute-done.1.diagonal_ref, bf16[256,1024]{1,0:T(8,128)(2,1)S(1)} %get-tuple-element.25.high_ref, f32[9,8,128]{2,1,0:T(8,128)S(1)} %get-tuple-element.26.mix_ref, ...), custom_call_target="tpu_custom_call" | custom-call | tf_op jit(solution)/shard_map/pallas_call | solution.py:284
  49.9 24.7 %all_to_all.10.source_ref = bf16[64,4,8,128]{3,2,1,0:T(8,128)(2,1)S(1)} all-to-all(bf16[64,4,8,128]{3,2,1,0:T(8,128)(2,1)S(1)} %bitcast.13), channel_id=1, replica_groups=mesh['mem'=64,'reg'=4] {'mem'}, dimensions={0} | all-to-all | bytes 1048576 | tf_op jit(solution)/shard_map/all_to_all | solution.py:285
  74.5 0.8 %shard_map.87 = bf16[4,64,8,128]{3,2,1,0:T(8,128)(2,1)} custom-call(bf16[64,4,8,128]{3,2,1,0:T(8,128)(2,1)S(1)} %all_to_all.10.source_ref), custom_call_target="tpu_custom_call" | custom-call | tf_op jit(solution)/shard_map/pallas_call | solution.py:286
Async XLA Ops:
  0.0 1.0 %copy-start = (bf16[4,1,512,128]{3,2,1,0:T(8,128)(2,1)S(1)}, bf16[4,1,512,128]{3,2,1,0:T(8,128)(2,1)}, u32[]{:S(2)}) copy-start(bf16[4,1,512,128]{3,2,1,0:T(8,128)(2,1)} %param.8) | copy-start | bytes 1572868
  1.9 13.2 %copy-start.6 = (s32[1,8,4]{1,2,0:T(4,128)S(1)}, s32[1,8,4]{1,2,0:T(4,128)}, u32[]{:S(2)}) copy-start(s32[1,8,4]{1,2,0:T(4,128)} %param.14) | copy-start | bytes 388
  1.9 13.3 %copy-start.7 = (f32[1,8,4]{1,2,0:T(4,128)S(1)}, f32[1,8,4]{1,2,0:T(4,128)}, u32[]{:S(2)}) copy-start(f32[1,8,4]{1,2,0:T(4,128)} %param.15) | copy-start | bytes 388
  1.9 13.3 %copy-start.2 = (f32[2,2,512]{2,1,0:T(2,128)S(1)}, f32[2,2,512]{2,1,0:T(2,128)}, u32[]{:S(2)}) copy-start(f32[2,2,512]{2,1,0:T(2,128)} %error_ref.1) | copy-start | bytes 24580
  1.9 13.3 %copy-start.3 = (s32[2,2,512]{2,1,0:T(2,128)S(1)}, s32[2,2,512]{2,1,0:T(2,128)}, u32[]{:S(2)}) copy-start(s32[2,2,512]{2,1,0:T(2,128)} %patch_ref.1) | copy-start | bytes 24580
  1.9 13.3 %copy-start.4 = (s32[2,2,512]{2,1,0:T(2,128)S(1)}, s32[2,2,512]{2,1,0:T(2,128)}, u32[]{:S(2)}) copy-start(s32[2,2,512]{2,1,0:T(2,128)} %var_ref.1) | copy-start | bytes 24580
  1.9 30.4 %all-to-all-start = ((bf16[64,4,8,128]{3,2,1,0:T(8,128)(2,1)}), bf16[64,4,8,128]{3,2,1,0:T(8,128)(2,1)S(1)}, u32[]{:S(2)}, u32[]{:S(2)}) async-start(bf16[64,4,8,128]{3,2,1,0:T(8,128)(2,1)} %copy_bitcast_fusion), calls=%async_computation | async-start | bytes 1048576 | tf_op jit(solution)/shard_map/all_to_all | solution.py:257
  15.1 0.7 copy-start.1
  15.2 0.7 copy-start.5
  36.4 7.1 %collective-permute-start.2 = (bf16[2,144,256]{2,1,0:T(8,128)(2,1)S(1)}, bf16[2,144,256]{2,1,0:T(8,128)(2,1)S(1)}, u32[]{:S(2)}, u32[]{:S(2)}) collective-permute-start(bf16[2,144,256]{2,1,0:T(8,128)(2,1)S(1)} %get-tuple-element.22.sent_ref), channel_id=1, source_target_pairs={{1,0},{2,1},{3,2},{5,4},{6,5},{7,6},{9,8},{10,9},{11,10},{13,12},{... | collective-permute-start | bytes 442376 | tf_op jit(solution)/shard_map/ppermute | solution.py:278
  41.4 7.7 %collective-permute-start = (bf16[2,144,256]{2,1,0:T(8,128)(2,1)S(1)}, bf16[2,144,256]{2,1,0:T(8,128)(2,1)S(1)}, u32[]{:S(2)}, u32[]{:S(2)}) collective-permute-start(bf16[2,144,256]{2,1,0:T(8,128)(2,1)S(1)} %get-tuple-element.23), channel_id=1, source_target_pairs={{4,0},{8,4},{12,8},{16,12},{20,16},{24,20},{28,24},{32,28},{36,32}... | collective-permute-start | bytes 442376 | tf_op jit(solution)/shard_map/ppermute | solution.py:281
  41.7 7.4 %collective-permute-start.1 = (bf16[1,144,256]{2,1,0:T(8,128)(2,1)S(1)}, bf16[1,144,256]{2,1,0:T(8,128)(2,1)S(1)}, u32[]{:S(2)}, u32[]{:S(2)}) collective-permute-start(bf16[1,144,256]{2,1,0:T(8,128)(2,1)S(1)} %get-tuple-element.24), channel_id=1, source_target_pairs={{5,0},{6,1},{7,2},{9,4},{10,5},{11,6},{13,8},{14,9},{15,10},{17,12... | collective-permute-start | bytes 221192 | tf_op jit(solution)/shard_map/ppermute | solution.py:279

commit v4 on v3

--- a/solution.py
+++ b/solution.py
@@ -152,7 +152,9 @@
     target[place, half:, half:] = (corner + right).astype(BF16)
 
 
-def first_kernel(ensemble_ref, dense_ref, value_ref, out_ref, pack_ref, corner_ref, x_ref, pert_ref, high_ref, centre_ref, wide_ref, left_high, left_low):
+def first_kernel(
+    ensemble_ref, dense_ref, value_ref, out_ref, beside_ref, corner_ref, below_ref, x_ref, pert_ref, high_ref, centre_ref, wide_ref, left_high, left_low
+):
     members, patches, fields = ensemble_ref.shape
     total = jnp.zeros((patches, fields), F32)
     chunk = 32
@@ -169,19 +171,27 @@
         pert = part - centre[p : p + 1, :]
         pert_ref[:, lanes] = pert
         high_ref[:, lanes] = pert.astype(BF16)
-    shares((0, 2), pert_ref, centre, dense_ref, value_ref, left_high, left_low)
-    for slot, spread, twice in weights_of(2, x_ref, left_high, left_low, out_ref):
-        pack(pack_ref, slot, spread, twice)
+    shares((0, 1, 2), pert_ref, centre, dense_ref, value_ref, left_high, left_low)
+    for slot, spread, twice in weights_of(3, x_ref, left_high, left_low, out_ref):
         if slot == 0:
-            corner_ref[0] = pack_ref[0]
-
-
-def second_kernel(x_ref, pert_ref, centre_ref, dense_ref, value_ref, sent_ref, out_ref, pack_ref, left_high, left_low):
-    pack_ref[0] = sent_ref[0]
-    shares((1, 3), pert_ref, centre_ref[...], dense_ref, value_ref, left_high, left_low)
-    for slot, spread, twice in weights_of(2, x_ref, left_high, left_low, out_ref):
-        if slot == 0:
-            pack(pack_ref, 1, spread, twice)
+            pack(corner_ref, 0, spread, twice)
+            beside_ref[0] = corner_ref[0]
+            below_ref[0] = corner_ref[0]
+        else:
+            pack(below_ref if slot == 1 else beside_ref, 1, spread, twice)
+
+
+def second_kernel(x_ref, pert_ref, centre_ref, dense_ref, value_ref, one_ref, high_ref, mix_ref, out_ref, left_high, left_low, two_ref):
+    patches, fields = centre_ref.shape
+    shares((3,), pert_ref, centre_ref[...], dense_ref, value_ref, left_high, left_low)
+    parts = ((0, one_ref, 0), (1, one_ref, 1), (3, one_ref, 2))
+    for p in range(0, patches, 2):
+        out_ref[:, p * fields : (p + 2) * fields] = blend(parts, high_ref, mix_ref, p)
+    for _ in weights_of(1, x_ref, left_high, left_low, two_ref):
+        pass
+    for p in range(0, patches, 2):
+        lanes = slice(p * fields, (p + 2) * fields)
+        out_ref[:, lanes] = out_ref[:, lanes] + blend(((4, two_ref, 0),), high_ref, mix_ref, p)
 
 
 def blend(parts, high_ref, mix_ref, p):
@@ -196,20 +206,11 @@
     return total
 
 
-def own_kernel(one_ref, two_ref, beside_ref, high_ref, mix_ref, out_ref, whole_ref):
-    unpack(beside_ref, 0, whole_ref, 0)
-    unpack(beside_ref, 1, whole_ref, 1)
-    parts = ((0, one_ref, 0), (3, one_ref, 1), (1, two_ref, 0), (4, two_ref, 1), (2, whole_ref, 0), (5, whole_ref, 1))
-    fields = mix_ref.shape[2]
-    for p in range(0, mix_ref.shape[1], 2):
-        out_ref[:, p * fields : (p + 2) * fields] = blend(parts, high_ref, mix_ref, p)
-
-
-def last_kernel(below_ref, diagonal_ref, high_ref, mix_ref, partial_ref, centre_ref, out_ref, all_ref, whole_ref):
-    unpack(below_ref, 0, whole_ref, 0)
-    unpack(below_ref, 1, whole_ref, 1)
-    unpack(diagonal_ref, 0, whole_ref, 2)
-    parts = ((6, whole_ref, 0), (7, whole_ref, 1), (8, whole_ref, 2))
+def last_kernel(beside_ref, below_ref, diagonal_ref, high_ref, mix_ref, partial_ref, centre_ref, out_ref, all_ref, whole_ref):
+    arrived = ((2, beside_ref, 0), (5, beside_ref, 1), (6, below_ref, 0), (7, below_ref, 1), (8, diagonal_ref, 0))
+    for place, (_, ref, slot) in enumerate(arrived):
+        unpack(ref, slot, whole_ref, place)
+    parts = [(t, whole_ref, place) for place, (t, _, _) in enumerate(arrived)]
     members, patches, fields = out_ref.shape
     for p in range(0, patches, 2):
         lanes = slice(p * fields, (p + 2) * fields)
@@ -261,27 +262,43 @@
         [SMEM] + [VMEM] * 6,
     )(obs_count, obs_value, obs_error, obs_patch, obs_variable, patch_corners[0], interp_weights[0])
 
-    pair = shape((2, members, members), BF16)
     packed = (members // 2 + 16, members)
-    lefts = [pltpu.VMEM((2, members + 16, columns), BF16)] * 2
+    left = (members + 16, columns)
+    flat = (members, columns)
     wide = pltpu.VMEM((members * patches, fields), F32)
-    flat = (members, columns)
-    one, sent, corner, x, pert, high, centre = call(
-        first_kernel,
-        (pair, shape((2,) + packed, BF16), shape((1,) + packed, BF16), shape(flat, BF16), shape(flat, F32), shape(flat, BF16), shape((patches, fields), F32)),
-        [VMEM] * 3,
-        [wide] + lefts,
-    )(ensemble, dense, values)
     down = [((d + 1) % devices, d) for d in range(devices)]
     across = [(r + 1, r) for r in range(regions - 1)]
     both = [(d * regions + r, e * regions + t) for d, e in down for r, t in across]
-    beside = lax.ppermute(sent, "reg", across)
-    diagonal = lax.ppermute(corner, ("mem", "reg"), both)
-    two, top = call(second_kernel, (pair, shape((2,) + packed, BF16)), [VMEM] * 6, lefts)(x, pert, centre, dense, values, sent)
-    below = lax.ppermute(top, "mem", down)
-    whole = pltpu.VMEM((3, members, members), BF16)
-    partial = call(own_kernel, shape(flat, F32), [VMEM] * 5, [whole])(one, two, beside, high, mix)
-    analysis = call(last_kernel, shape((members, patches, fields), BF16), [VMEM] * 6, [wide, whole])(below, diagonal, high, mix, partial, centre)
+    one, to_beside, to_corner, to_below, x, pert, high, centre = call(
+        first_kernel,
+        (
+            shape((3, members, members), BF16),
+            shape((2,) + packed, BF16),
+            shape((1,) + packed, BF16),
+            shape((2,) + packed, BF16),
+            shape(flat, BF16),
+            shape(flat, F32),
+            shape(flat, BF16),
+            shape((patches, fields), F32),
+        ),
+        [VMEM] * 3,
+        [wide] + [pltpu.VMEM((3,) + left, BF16)] * 2,
+    )(ensemble, dense, values)
+    beside = lax.ppermute(to_beside, "reg", across)
+    diagonal = lax.ppermute(to_corner, ("mem", "reg"), both)
+    below = lax.ppermute(to_below, "mem", down)
+    partial = call(
+        second_kernel,
+        shape(flat, F32),
+        [VMEM] * 8,
+        [pltpu.VMEM((1,) + left, BF16)] * 2 + [pltpu.VMEM((1, members, members), BF16)],
+    )(x, pert, centre, dense, values, one, high, mix)
+    analysis = call(
+        last_kernel,
+        shape((members, patches, fields), BF16),
+        [VMEM] * 7,
+        [wide, pltpu.VMEM((5, members, members), BF16)],
+    )(beside, below, diagonal, high, mix, partial, centre)
     returned = lax.all_to_all(analysis.reshape(devices, own, patches, fields), "mem", split_axis=0, concat_axis=0, tiled=True)
     result = call(returned_kernel, shape((own, devices, patches, fields), BF16), [VMEM], copies, HBM)(returned)
     return result.reshape(own, 1, all_patches, fields)

time: 76.2 us -> 73.6 us (0.966)
  waiting for transfers between devices: 20.5 us -> 17.5 us
    ppermute x3, waiting for transfers between devices: 5.04 us -> 2.08 us  [the longest x1 2.07 us: per_device(): diagonal = lax.ppermute(to_corner, ('mem', 'reg'), both)]
    pallas_call x4 -> x3, Pallas kernels: 9.56 us -> 9.99 us  [the longest x1 4.9 us: per_device(): call(first_kernel, (shape((3, members, members), BF16), shape((2,) + pack...]
  transfers between devices with their start and end apart: 4 -> 4, of which waited for: 3 -> 2; matrix products, arithmetic and copies ran while one was open for 0% -> 0% of each run, Pallas kernels for 8% -> 7%
where the time goes in v4:
time: 73.6 us; the launch traced here: 72.8 us
  blocking collectives  24.7 us (34%)
  waiting for transfers between devices  17.5 us (24%)
  starting transfers between devices  16 us (22%)
  Pallas kernels  11.9 us (16%)
  local copies, waits for them, and re-layouts  2.7 us (4%)
    all_to_all x1, blocking collectives, per_device(): lax.all_to_all(analysis.reshape(devices, own, patches, fields), 'mem', sp...  24.7 us
    all_to_all x1, waiting for transfers between devices, per_device(): lax.all_to_all(outgoing, 'mem', split_axis=0, concat_axis=0, tiled=True)  15.4 us
    all_to_all x1, starting transfers between devices, per_device(): lax.all_to_all(outgoing, 'mem', split_axis=0, concat_axis=0, tiled=True)  13.1 us
    pallas_call x1, Pallas kernels, per_device(): call(first_kernel, (shape((3, members, members), BF16), shape((2,) + pack...  4.9 us
    pallas_call x1, Pallas kernels, per_device(): call(second_kernel, shape(flat, F32), [VMEM] * 8, [pltpu.VMEM((1,) + left...  3.99 us
    ppermute x1, waiting for transfers between devices, per_device(): diagonal = lax.ppermute(to_corner, ('mem', 'reg'), both)  2.07 us
    unnamed x16, local copies, waits for them, and re-layouts  1.66 us
  transfers between devices with their start and end apart: 4, of which 2 were waited for; matrix products, arithmetic and copies ran while one was open for 0% of the time, Pallas kernels for 7%

profile of v4, /device:TPU:1, one launch (start us, length us, event | category | flops | bytes accessed | tf_op | source)
XLA Modules:
  0.0 72.8 jit_solution(8467188607336578572)
XLA Ops:
  0.0 0.0 copy-start
  0.0 1.0 %copy-done = bf16[4,1,512,128]{3,2,1,0:T(8,128)(2,1)S(1)} copy-done((bf16[4,1,512,128]{3,2,1,0:T(8,128)(2,1)S(1)}, bf16[4,1,512,128]{3,2,1,0:T(8,128)(2,1)}, u32[]{:S(2)}) %copy-start) | copy-done | bytes 524312
  1.0 0.9 %copy_bitcast_fusion = bf16[64,4,8,128]{3,2,1,0:T(8,128)(2,1)} fusion(bf16[4,1,512,128]{3,2,1,0:T(8,128)(2,1)S(1)} %copy-done), kind=kLoop, calls=%fused_computation | loop fusion | bytes 1048576 | tf_op jit(solution)/shard_map/transpose | solution.py:257
  1.9 0.0 copy-start.6
  1.9 0.0 copy-start.7
  1.9 0.0 copy-start.2
  1.9 0.0 copy-start.3
  1.9 0.0 copy-start.4
  1.9 13.1 %all-to-all-start = ((bf16[64,4,8,128]{3,2,1,0:T(8,128)(2,1)}), bf16[64,4,8,128]{3,2,1,0:T(8,128)(2,1)S(1)}, u32[]{:S(2)}, u32[]{:S(2)}) async-start(bf16[64,4,8,128]{3,2,1,0:T(8,128)(2,1)} %copy_bitcast_fusion), calls=%async_computation | async-start | bytes 1048576 | tf_op jit(solution)/shard_map/all_to_all | solution.py:258
  15.1 0.0 copy-start.1
  15.1 0.0 copy-done.6
  15.1 0.1 copy.10.corner_ref
  15.2 0.0 copy-done.7
  15.2 0.0 copy-start.5
  15.2 0.1 copy.11.coeff_ref
  15.3 0.0 copy-done.2
  15.3 0.0 copy-done.3
  15.3 0.0 copy-done.4
  15.3 0.5 copy-done.1
  15.8 0.1 copy-done.5
  15.9 1.1 %shard_map.82 = (f32[4,8,128]{2,1,0:T(8,128)S(1)}, f32[4,8,128]{2,1,0:T(8,128)S(1)}, f32[9,8,128]{2,1,0:T(8,128)S(1)}) custom-call(s32[2,2]{1,0:T(2,128)S(1)} %copy-done.5, f32[2,2,512]{2,1,0:T(2,128)S(1)} %copy-done.1, f32[2,2,512]{2,1,0:T(2,128)S(1)} %copy-done.2, s32[2,2,512]{2,1,0:T(2,128)S(1)} %copy-done.3, s32[2,2,512]{2,1,0:T(2,128)S(1)} %copy-done.4, ...), custom_call_target="tpu_custom_call" | custom-call | tf_op jit(solution)/shard_map/pallas_call | solution.py:259
  16.9 15.4 %all-to-all-done = bf16[64,4,8,128]{3,2,1,0:T(8,128)(2,1)S(1)} async-done(((bf16[64,4,8,128]{3,2,1,0:T(8,128)(2,1)}), bf16[64,4,8,128]{3,2,1,0:T(8,128)(2,1)S(1)}, u32[]{:S(2)}, u32[]{:S(2)}) %all-to-all-start) | async-done | bytes 524320 | tf_op jit(solution)/shard_map/all_to_all | solution.py:258
  32.4 4.9 %shard_map.83 = (bf16[3,256,256]{2,1,0:T(8,128)(2,1)S(1)}, bf16[2,144,256]{2,1,0:T(8,128)(2,1)S(1)}, bf16[1,144,256]{2,1,0:T(8,128)(2,1)S(1)}, bf16[2,144,256]{2...) custom-call(bf16[256,8,128]{2,1,0:T(8,128)(2,1)S(1)} %bitcast.13, ...), custom_call_target="tpu_custom_call" | custom-call | tf_op jit(solution)/shard_map/pallas_call | solution.py:272
  37.3 1.3 %collective-permute-start = (bf16[2,144,256]{2,1,0:T(8,128)(2,1)S(1)}, bf16[2,144,256]{2,1,0:T(8,128)(2,1)S(1)}, u32[]{:S(2)}, u32[]{:S(2)}) collective-permute-start(bf16[2,144,256]{2,1,0:T(8,128)(2,1)S(1)} %get-tuple-element.18), channel_id=1, source_target_pairs={{1,0},{2,1},{3,2},{5,4},{6,5},{7,6},{9,8},{10,9},{11,10},{13,12},{... | collective-permute-start | bytes 442376 | tf_op jit(solution)/shard_map/ppermute | solution.py:287
  38.6 0.3 collective-permute-start.1
  38.9 1.3 %collective-permute-start.2 = (bf16[1,144,256]{2,1,0:T(8,128)(2,1)S(1)}, bf16[1,144,256]{2,1,0:T(8,128)(2,1)S(1)}, u32[]{:S(2)}, u32[]{:S(2)}) collective-permute-start(bf16[1,144,256]{2,1,0:T(8,128)(2,1)S(1)} %get-tuple-element.20), channel_id=1, source_target_pairs={{5,0},{6,1},{7,2},{9,4},{10,5},{11,6},{13,8},{14,9},{15,10},{17,12... | collective-permute-start | bytes 221192 | tf_op jit(solution)/shard_map/ppermute | solution.py:288
  40.2 4.0 %shard_map.84.partial_ref = f32[256,1024]{1,0:T(8,128)S(1)} custom-call(bf16[256,1024]{1,0:T(8,128)(2,1)S(1)} %get-tuple-element.23.x_ref, f32[256,1024]{1,0:T(8,128)S(1)} %get-tuple-element.24.pert_ref, f32[8,128]{1,0:T(8,128)S(1)} %get-tuple-element.25.centre_ref, f32[4,8,128]{2,1,0:T(8,128)S(1)} %get-tuple-element.16.dense_ref, ...), custom_call_target="tpu_custom_call" | custom-call | tf_op jit(solution)/shard_map/pallas_call | solution.py:290
  44.1 2.1 %collective-permute-done.2.diagonal_ref = bf16[1,144,256]{2,1,0:T(8,128)(2,1)S(1)} collective-permute-done((bf16[1,144,256]{2,1,0:T(8,128)(2,1)S(1)}, bf16[1,144,256]{2,1,0:T(8,128)(2,1)S(1)}, u32[]{:S(2)}, u32[]{:S(2)}) %collective-permute-start.2) | collective-permute-done | bytes 73760 | tf_op jit(solution)/shard_map/ppermute | solution.py:288
  46.2 0.0 collective-permute-done.beside_ref
  46.2 0.0 collective-permute-done.1.below_ref
  46.2 1.1 %shard_map.85 = bf16[256,8,128]{2,1,0:T(8,128)(2,1)S(1)} custom-call(bf16[2,144,256]{2,1,0:T(8,128)(2,1)S(1)} %collective-permute-done.beside_ref, bf16[2,144,256]{2,1,0:T(8,128)(2,1)S(1)} %collective-permute-done.1.below_ref, bf16[1,144,256]{2,1,0:T(8,128)(2,1)S(1)} %collective-permute-done.2.diagonal_ref, ...), custom_call_target="tpu_custom_call" | custom-call | tf_op jit(solution)/shard_map/pallas_call | solution.py:296
  47.3 24.7 %all_to_all.10.source_ref = bf16[64,4,8,128]{3,2,1,0:T(8,128)(2,1)S(1)} all-to-all(bf16[64,4,8,128]{3,2,1,0:T(8,128)(2,1)S(1)} %bitcast.12), channel_id=1, replica_groups=mesh['mem'=64,'reg'=4] {'mem'}, dimensions={0} | all-to-all | bytes 1048576 | tf_op jit(solution)/shard_map/all_to_all | solution.py:302
  72.0 0.8 %shard_map.86 = bf16[4,64,8,128]{3,2,1,0:T(8,128)(2,1)} custom-call(bf16[64,4,8,128]{3,2,1,0:T(8,128)(2,1)S(1)} %all_to_all.10.source_ref), custom_call_target="tpu_custom_call" | custom-call | tf_op jit(solution)/shard_map/pallas_call | solution.py:303
Async XLA Ops:
  0.0 1.0 %copy-start = (bf16[4,1,512,128]{3,2,1,0:T(8,128)(2,1)S(1)}, bf16[4,1,512,128]{3,2,1,0:T(8,128)(2,1)}, u32[]{:S(2)}) copy-start(bf16[4,1,512,128]{3,2,1,0:T(8,128)(2,1)} %param.8) | copy-start | bytes 1572868
  1.9 13.2 %copy-start.6 = (s32[1,8,4]{1,2,0:T(4,128)S(1)}, s32[1,8,4]{1,2,0:T(4,128)}, u32[]{:S(2)}) copy-start(s32[1,8,4]{1,2,0:T(4,128)} %param.14) | copy-start | bytes 388
  1.9 13.3 %copy-start.7 = (f32[1,8,4]{1,2,0:T(4,128)S(1)}, f32[1,8,4]{1,2,0:T(4,128)}, u32[]{:S(2)}) copy-start(f32[1,8,4]{1,2,0:T(4,128)} %param.15) | copy-start | bytes 388
  1.9 13.3 %copy-start.2 = (f32[2,2,512]{2,1,0:T(2,128)S(1)}, f32[2,2,512]{2,1,0:T(2,128)}, u32[]{:S(2)}) copy-start(f32[2,2,512]{2,1,0:T(2,128)} %error_ref.1) | copy-start | bytes 24580
  1.9 13.3 %copy-start.3 = (s32[2,2,512]{2,1,0:T(2,128)S(1)}, s32[2,2,512]{2,1,0:T(2,128)}, u32[]{:S(2)}) copy-start(s32[2,2,512]{2,1,0:T(2,128)} %patch_ref.1) | copy-start | bytes 24580
  1.9 13.3 %copy-start.4 = (s32[2,2,512]{2,1,0:T(2,128)S(1)}, s32[2,2,512]{2,1,0:T(2,128)}, u32[]{:S(2)}) copy-start(s32[2,2,512]{2,1,0:T(2,128)} %var_ref.1) | copy-start | bytes 24580
  1.9 30.4 %all-to-all-start = ((bf16[64,4,8,128]{3,2,1,0:T(8,128)(2,1)}), bf16[64,4,8,128]{3,2,1,0:T(8,128)(2,1)S(1)}, u32[]{:S(2)}, u32[]{:S(2)}) async-start(bf16[64,4,8,128]{3,2,1,0:T(8,128)(2,1)} %copy_bitcast_fusion), calls=%async_computation | async-start | bytes 1048576 | tf_op jit(solution)/shard_map/all_to_all | solution.py:258
  15.1 0.7 copy-start.1
  15.2 0.7 copy-start.5
  37.3 9.0 %collective-permute-start = (bf16[2,144,256]{2,1,0:T(8,128)(2,1)S(1)}, bf16[2,144,256]{2,1,0:T(8,128)(2,1)S(1)}, u32[]{:S(2)}, u32[]{:S(2)}) collective-permute-start(bf16[2,144,256]{2,1,0:T(8,128)(2,1)S(1)} %get-tuple-element.18), channel_id=1, source_target_pairs={{1,0},{2,1},{3,2},{5,4},{6,5},{7,6},{9,8},{10,9},{11,10},{13,12},{... | collective-permute-start | bytes 442376 | tf_op jit(solution)/shard_map/ppermute | solution.py:287
  38.6 7.7 %collective-permute-start.1 = (bf16[2,144,256]{2,1,0:T(8,128)(2,1)S(1)}, bf16[2,144,256]{2,1,0:T(8,128)(2,1)S(1)}, u32[]{:S(2)}, u32[]{:S(2)}) collective-permute-start(bf16[2,144,256]{2,1,0:T(8,128)(2,1)S(1)} %get-tuple-element.19), channel_id=1, source_target_pairs={{4,0},{8,4},{12,8},{16,12},{20,16},{24,20},{28,24},{32,28},{36,32}... | collective-permute-start | bytes 442376 | tf_op jit(solution)/shard_map/ppermute | solution.py:289
  38.9 7.4 %collective-permute-start.2 = (bf16[1,144,256]{2,1,0:T(8,128)(2,1)S(1)}, bf16[1,144,256]{2,1,0:T(8,128)(2,1)S(1)}, u32[]{:S(2)}, u32[]{:S(2)}) collective-permute-start(bf16[1,144,256]{2,1,0:T(8,128)(2,1)S(1)} %get-tuple-element.20), channel_id=1, source_target_pairs={{5,0},{6,1},{7,2},{9,4},{10,5},{11,6},{13,8},{14,9},{15,10},{17,12... | collective-permute-start | bytes 221192 | tf_op jit(solution)/shard_map/ppermute | solution.py:288

commit v5 on v4

--- a/solution.py
+++ b/solution.py
@@ -85,6 +85,12 @@
     return add_diagonal(product(split(square), split(inner)) - 4.875 * x, 2.25, diagonal)
 
 
+def later_factors(x):
+    rounded = x.astype(BF16)
+    square = dot(rounded, rounded)
+    return 1.5 * square - x + dot(square.astype(BF16), (square - 2.5 * x).astype(BF16))
+
+
 def weights_of(count, x_ref, left_high, left_low, out_ref):
     members = x_ref.shape[0]
     half = members // 2
@@ -104,11 +110,12 @@
         half_inverse = 0.5 / scaling
         state.append((projected, scaling, add_diagonal(gram * half_inverse, (members - 1.0) * half_inverse, diagonal)))
     parts = [split(x) for _, _, x in state]
-    z = [split(two_factors(state[s][2], parts[s], diagonal)) for s in slots]
+    roots = [two_factors(state[s][2], parts[s], diagonal) for s in slots]
+    z = [split(x) for x in roots]
     y = [split(product(parts[s], z[s])) for s in slots]
-    c = [product(y[s], z[s]) for s in slots]
-    f = [split(two_factors(c[s], split(c[s]), diagonal)) for s in slots]
-    inverses = [product(f[s], z[s]) for s in slots]
+    excess = [add_diagonal(product(y[s], z[s]), -0.5, diagonal) for s in slots]
+    rest = [later_factors(x) for x in excess]
+    inverses = [roots[s] + rest[s] + dot(rest[s].astype(BF16), add_diagonal(roots[s], -1.0, diagonal).astype(BF16)) for s in slots]
     for slot in slots:
         projected, scaling, _ = state[slot]
         inverse = inverses[slot]
@@ -184,14 +191,11 @@
 def second_kernel(x_ref, pert_ref, centre_ref, dense_ref, value_ref, one_ref, high_ref, mix_ref, out_ref, left_high, left_low, two_ref):
     patches, fields = centre_ref.shape
     shares((3,), pert_ref, centre_ref[...], dense_ref, value_ref, left_high, left_low)
-    parts = ((0, one_ref, 0), (1, one_ref, 1), (3, one_ref, 2))
-    for p in range(0, patches, 2):
-        out_ref[:, p * fields : (p + 2) * fields] = blend(parts, high_ref, mix_ref, p)
+    parts = ((0, one_ref, 0), (1, one_ref, 1), (3, one_ref, 2), (4, two_ref, 0))
     for _ in weights_of(1, x_ref, left_high, left_low, two_ref):
         pass
     for p in range(0, patches, 2):
-        lanes = slice(p * fields, (p + 2) * fields)
-        out_ref[:, lanes] = out_ref[:, lanes] + blend(((4, two_ref, 0),), high_ref, mix_ref, p)
+        out_ref[:, p * fields : (p + 2) * fields] = blend(parts, high_ref, mix_ref, p)
 
 
 def blend(parts, high_ref, mix_ref, p):
@@ -224,6 +228,23 @@
         out_ref[k : k + chunk] = part.reshape(chunk, patches, fields).astype(BF16)
 
 
+def outgoing_kernel(source_ref, target_ref, held_ref, turned_ref, read, written):
+    own, devices = source_ref.shape[:2]
+    half = devices // 2
+    spans = [slice(h * half, (h + 1) * half) for h in range(2)]
+    inward = [pltpu.make_async_copy(source_ref.at[:, s], held_ref.at[:, s], read.at[h]) for h, s in enumerate(spans)]
+    outward = [pltpu.make_async_copy(turned_ref.at[s], target_ref.at[s], written.at[h]) for h, s in enumerate(spans)]
+    for copy in inward:
+        copy.start()
+    for copy, out, s in zip(inward, outward, spans):
+        copy.wait()
+        for m in range(own):
+            turned_ref[s, m] = held_ref[m, s]
+        out.start()
+    for out in outward:
+        out.wait()
+
+
 def returned_kernel(source_ref, target_ref, done):
     copies = [pltpu.make_async_copy(source_ref.at[:, m], target_ref.at[m], done.at[m]) for m in range(target_ref.shape[0])]
     for copy in copies:
@@ -254,7 +275,14 @@
     columns = patches * fields
     copies = [pltpu.SemaphoreType.DMA((own,))]
 
-    outgoing = jnp.transpose(background.reshape(own, devices, patches, fields), (1, 0, 2, 3))
+    blocks = (devices, own, patches, fields)
+    outgoing = call(
+        outgoing_kernel,
+        shape(blocks, BF16),
+        [HBM],
+        [pltpu.VMEM((own,) + (devices,) + blocks[2:], BF16), pltpu.VMEM(blocks, BF16)] + [pltpu.SemaphoreType.DMA((2,))] * 2,
+        HBM,
+    )(pltpu.with_memory_space_constraint(background.reshape(own, devices, patches, fields), pltpu.HBM))
     ensemble = lax.all_to_all(outgoing, "mem", split_axis=0, concat_axis=0, tiled=True).reshape(members, patches, fields)
     dense, values, mix = call(
         prepare_kernel,

time: 73.6 us -> 73.1 us (level)
  local copies, waits for them, and re-layouts: 2.7 us -> 0.79 us
  Pallas kernels: 11.9 us -> 12.7 us
    pallas_call x0 -> x1, Pallas kernels: none -> 1.82 us  [per_device(): call(outgoing_kernel, shape(blocks, BF16), [HBM], [pltpu.VMEM((own,) + (d...]
    unnamed x16 -> x14, local copies, waits for them, and re-layouts: 1.66 us -> 0.63 us
    transpose x1 -> x0, local copies, waits for them, and re-layouts: 0.88 us -> none  [per_device(): jnp.transpose(background.reshape(own, devices, patches, fields), (1, 0, 2...]
  transfers between devices with their start and end apart: 4 -> 4, of which waited for: 2 -> 2; matrix products, arithmetic and copies ran while one was open for 0% -> 0% of each run, Pallas kernels for 7% -> 6%
where the time goes in v5:
time: 73.1 us; the launch traced here: 72.3 us
  blocking collectives  24.7 us (34%)
  waiting for transfers between devices  18 us (25%)
  starting transfers between devices  16 us (22%)
  Pallas kernels  12.7 us (17%)
  local copies, waits for them, and re-layouts  0.79 us (1%)
    all_to_all x1, blocking collectives, per_device(): lax.all_to_all(analysis.reshape(devices, own, patches, fields), 'mem', sp...  24.7 us
    all_to_all x1, waiting for transfers between devices, per_device(): lax.all_to_all(outgoing, 'mem', split_axis=0, concat_axis=0, tiled=True)  15.4 us
    all_to_all x1, starting transfers between devices, per_device(): lax.all_to_all(outgoing, 'mem', split_axis=0, concat_axis=0, tiled=True)  13.1 us
    pallas_call x1, Pallas kernels, per_device(): call(first_kernel, (shape((3, members, members), BF16), shape((2,) + pack...  4.43 us
    pallas_call x1, Pallas kernels, per_device(): call(second_kernel, shape(flat, F32), [VMEM] * 8, [pltpu.VMEM((1,) + left...  3.46 us
    ppermute x1, waiting for transfers between devices, per_device(): diagonal = lax.ppermute(to_corner, ('mem', 'reg'), both)  2.61 us
    pallas_call x1, Pallas kernels, per_device(): call(outgoing_kernel, shape(blocks, BF16), [HBM], [pltpu.VMEM((own,) + (d...  1.82 us
  transfers between devices with their start and end apart: 4, of which 2 were waited for; matrix products, arithmetic and copies ran while one was open for 0% of the time, Pallas kernels for 6%

profile of v5, /device:TPU:1, one launch (start us, length us, event | category | flops | bytes accessed | tf_op | source)
XLA Modules:
  0.0 72.3 jit_solution(7628895380404661477)
XLA Ops:
  0.0 1.8 %shard_map.82 = bf16[64,4,8,128]{3,2,1,0:T(8,128)(2,1)} custom-call(bf16[4,64,8,128]{3,2,1,0:T(8,128)(2,1)} %bitcast.10), custom_call_target="tpu_custom_call" | custom-call | tf_op jit(solution)/shard_map/pallas_call | solution.py:279
  1.8 0.0 copy-start.5
  1.8 0.0 copy-start.6
  1.8 0.0 copy-start.1
  1.9 0.0 copy-start.2
  1.9 0.0 copy-start.3
  1.9 13.1 %all-to-all-start = ((bf16[64,4,8,128]{3,2,1,0:T(8,128)(2,1)}), bf16[64,4,8,128]{3,2,1,0:T(8,128)(2,1)S(1)}, u32[]{:S(2)}, u32[]{:S(2)}) async-start(bf16[64,4,8,128]{3,2,1,0:T(8,128)(2,1)} %shard_map.82), calls=%async_computation | async-start | bytes 1048576 | tf_op jit(solution)/shard_map/all_to_all | solution.py:286
  15.0 0.0 copy-start
  15.0 0.0 copy-done.5
  15.0 0.1 copy.9.corner_ref
  15.1 0.0 copy-done.6
  15.1 0.0 copy-start.4
  15.1 0.1 copy.10.coeff_ref
  15.2 0.0 copy-done.1
  15.2 0.0 copy-done.2
  15.2 0.0 copy-done.3
  15.2 0.5 copy-done
  15.7 0.1 copy-done.4
  15.8 1.1 %shard_map.83 = (f32[4,8,128]{2,1,0:T(8,128)S(1)}, f32[4,8,128]{2,1,0:T(8,128)S(1)}, f32[9,8,128]{2,1,0:T(8,128)S(1)}) custom-call(s32[2,2]{1,0:T(2,128)S(1)} %copy-done.4, f32[2,2,512]{2,1,0:T(2,128)S(1)} %copy-done, f32[2,2,512]{2,1,0:T(2,128)S(1)} %copy-done.1, s32[2,2,512]{2,1,0:T(2,128)S(1)} %copy-done.2, s32[2,2,512]{2,1,0:T(2,128)S(1)} %copy-done.3, ...), custom_call_target="tpu_custom_call" | custom-call | tf_op jit(solution)/shard_map/pallas_call | solution.py:287
  16.9 15.4 %all-to-all-done = bf16[64,4,8,128]{3,2,1,0:T(8,128)(2,1)S(1)} async-done(((bf16[64,4,8,128]{3,2,1,0:T(8,128)(2,1)}), bf16[64,4,8,128]{3,2,1,0:T(8,128)(2,1)S(1)}, u32[]{:S(2)}, u32[]{:S(2)}) %all-to-all-start) | async-done | bytes 524320 | tf_op jit(solution)/shard_map/all_to_all | solution.py:286
  32.3 4.4 %shard_map.84 = (bf16[3,256,256]{2,1,0:T(8,128)(2,1)S(1)}, bf16[2,144,256]{2,1,0:T(8,128)(2,1)S(1)}, bf16[1,144,256]{2,1,0:T(8,128)(2,1)S(1)}, bf16[2,144,256]{2...) custom-call(bf16[256,8,128]{2,1,0:T(8,128)(2,1)S(1)} %bitcast.9, ...), custom_call_target="tpu_custom_call" | custom-call | tf_op jit(solution)/shard_map/pallas_call | solution.py:300
  36.7 1.3 %collective-permute-start = (bf16[2,144,256]{2,1,0:T(8,128)(2,1)S(1)}, bf16[2,144,256]{2,1,0:T(8,128)(2,1)S(1)}, u32[]{:S(2)}, u32[]{:S(2)}) collective-permute-start(bf16[2,144,256]{2,1,0:T(8,128)(2,1)S(1)} %get-tuple-element.18), channel_id=1, source_target_pairs={{1,0},{2,1},{3,2},{5,4},{6,5},{7,6},{9,8},{10,9},{11,10},{13,12},{... | collective-permute-start | bytes 442376 | tf_op jit(solution)/shard_map/ppermute | solution.py:315
  38.0 0.3 collective-permute-start.1
  38.3 1.3 %collective-permute-start.2 = (bf16[1,144,256]{2,1,0:T(8,128)(2,1)S(1)}, bf16[1,144,256]{2,1,0:T(8,128)(2,1)S(1)}, u32[]{:S(2)}, u32[]{:S(2)}) collective-permute-start(bf16[1,144,256]{2,1,0:T(8,128)(2,1)S(1)} %get-tuple-element.20), channel_id=1, source_target_pairs={{5,0},{6,1},{7,2},{9,4},{10,5},{11,6},{13,8},{14,9},{15,10},{17,12... | collective-permute-start | bytes 221192 | tf_op jit(solution)/shard_map/ppermute | solution.py:316
  39.6 3.5 %shard_map.85.partial_ref = f32[256,1024]{1,0:T(8,128)S(1)} custom-call(bf16[256,1024]{1,0:T(8,128)(2,1)S(1)} %get-tuple-element.23.x_ref, f32[256,1024]{1,0:T(8,128)S(1)} %get-tuple-element.24.pert_ref, f32[8,128]{1,0:T(8,128)S(1)} %get-tuple-element.25.centre_ref, f32[4,8,128]{2,1,0:T(8,128)S(1)} %get-tuple-element.16.dense_ref, ...), custom_call_target="tpu_custom_call" | custom-call | tf_op jit(solution)/shard_map/pallas_call | solution.py:318
  43.1 2.6 %collective-permute-done.2.diagonal_ref = bf16[1,144,256]{2,1,0:T(8,128)(2,1)S(1)} collective-permute-done((bf16[1,144,256]{2,1,0:T(8,128)(2,1)S(1)}, bf16[1,144,256]{2,1,0:T(8,128)(2,1)S(1)}, u32[]{:S(2)}, u32[]{:S(2)}) %collective-permute-start.2) | collective-permute-done | bytes 73760 | tf_op jit(solution)/shard_map/ppermute | solution.py:316
  45.7 0.0 collective-permute-done.beside_ref
  45.7 0.0 collective-permute-done.1.below_ref
  45.7 1.1 %shard_map.86 = bf16[256,8,128]{2,1,0:T(8,128)(2,1)S(1)} custom-call(bf16[2,144,256]{2,1,0:T(8,128)(2,1)S(1)} %collective-permute-done.beside_ref, bf16[2,144,256]{2,1,0:T(8,128)(2,1)S(1)} %collective-permute-done.1.below_ref, bf16[1,144,256]{2,1,0:T(8,128)(2,1)S(1)} %collective-permute-done.2.diagonal_ref, ...), custom_call_target="tpu_custom_call" | custom-call | tf_op jit(solution)/shard_map/pallas_call | solution.py:324
  46.8 24.7 %all_to_all.10.source_ref = bf16[64,4,8,128]{3,2,1,0:T(8,128)(2,1)S(1)} all-to-all(bf16[64,4,8,128]{3,2,1,0:T(8,128)(2,1)S(1)} %bitcast.8), channel_id=1, replica_groups=mesh['mem'=64,'reg'=4] {'mem'}, dimensions={0} | all-to-all | bytes 1048576 | tf_op jit(solution)/shard_map/all_to_all | solution.py:330
  71.5 0.8 %shard_map.87 = bf16[4,64,8,128]{3,2,1,0:T(8,128)(2,1)} custom-call(bf16[64,4,8,128]{3,2,1,0:T(8,128)(2,1)S(1)} %all_to_all.10.source_ref), custom_call_target="tpu_custom_call" | custom-call | tf_op jit(solution)/shard_map/pallas_call | solution.py:331
Async XLA Ops:
  1.8 13.2 %copy-start.5 = (s32[1,8,4]{1,2,0:T(4,128)S(1)}, s32[1,8,4]{1,2,0:T(4,128)}, u32[]{:S(2)}) copy-start(s32[1,8,4]{1,2,0:T(4,128)} %param.14) | copy-start | bytes 388
  1.8 13.3 %copy-start.6 = (f32[1,8,4]{1,2,0:T(4,128)S(1)}, f32[1,8,4]{1,2,0:T(4,128)}, u32[]{:S(2)}) copy-start(f32[1,8,4]{1,2,0:T(4,128)} %param.15) | copy-start | bytes 388
  1.8 13.4 %copy-start.1 = (f32[2,2,512]{2,1,0:T(2,128)S(1)}, f32[2,2,512]{2,1,0:T(2,128)}, u32[]{:S(2)}) copy-start(f32[2,2,512]{2,1,0:T(2,128)} %error_ref.1) | copy-start | bytes 24580
  1.9 13.3 %copy-start.2 = (s32[2,2,512]{2,1,0:T(2,128)S(1)}, s32[2,2,512]{2,1,0:T(2,128)}, u32[]{:S(2)}) copy-start(s32[2,2,512]{2,1,0:T(2,128)} %patch_ref.1) | copy-start | bytes 24580
  1.9 13.3 %copy-start.3 = (s32[2,2,512]{2,1,0:T(2,128)S(1)}, s32[2,2,512]{2,1,0:T(2,128)}, u32[]{:S(2)}) copy-start(s32[2,2,512]{2,1,0:T(2,128)} %var_ref.1) | copy-start | bytes 24580
  1.9 30.4 %all-to-all-start = ((bf16[64,4,8,128]{3,2,1,0:T(8,128)(2,1)}), bf16[64,4,8,128]{3,2,1,0:T(8,128)(2,1)S(1)}, u32[]{:S(2)}, u32[]{:S(2)}) async-start(bf16[64,4,8,128]{3,2,1,0:T(8,128)(2,1)} %shard_map.82), calls=%async_computation | async-start | bytes 1048576 | tf_op jit(solution)/shard_map/all_to_all | solution.py:286
  15.0 0.7 copy-start
  15.1 0.7 copy-start.4
  36.7 9.0 %collective-permute-start = (bf16[2,144,256]{2,1,0:T(8,128)(2,1)S(1)}, bf16[2,144,256]{2,1,0:T(8,128)(2,1)S(1)}, u32[]{:S(2)}, u32[]{:S(2)}) collective-permute-start(bf16[2,144,256]{2,1,0:T(8,128)(2,1)S(1)} %get-tuple-element.18), channel_id=1, source_target_pairs={{1,0},{2,1},{3,2},{5,4},{6,5},{7,6},{9,8},{10,9},{11,10},{13,12},{... | collective-permute-start | bytes 442376 | tf_op jit(solution)/shard_map/ppermute | solution.py:315
  38.0 7.7 %collective-permute-start.1 = (bf16[2,144,256]{2,1,0:T(8,128)(2,1)S(1)}, bf16[2,144,256]{2,1,0:T(8,128)(2,1)S(1)}, u32[]{:S(2)}, u32[]{:S(2)}) collective-permute-start(bf16[2,144,256]{2,1,0:T(8,128)(2,1)S(1)} %get-tuple-element.19), channel_id=1, source_target_pairs={{4,0},{8,4},{12,8},{16,12},{20,16},{24,20},{28,24},{32,28},{36,32}... | collective-permute-start | bytes 442376 | tf_op jit(solution)/shard_map/ppermute | solution.py:317
  38.3 7.4 %collective-permute-start.2 = (bf16[1,144,256]{2,1,0:T(8,128)(2,1)S(1)}, bf16[1,144,256]{2,1,0:T(8,128)(2,1)S(1)}, u32[]{:S(2)}, u32[]{:S(2)}) collective-permute-start(bf16[1,144,256]{2,1,0:T(8,128)(2,1)S(1)} %get-tuple-element.20), channel_id=1, source_target_pairs={{5,0},{6,1},{7,2},{9,4},{10,5},{11,6},{13,8},{14,9},{15,10},{17,12... | collective-permute-start | bytes 221192 | tf_op jit(solution)/shard_map/ppermute | solution.py:316

commit v6 on v5

--- a/solution.py
+++ b/solution.py
@@ -210,11 +210,22 @@
     return total
 
 
-def last_kernel(beside_ref, below_ref, diagonal_ref, high_ref, mix_ref, partial_ref, centre_ref, out_ref, all_ref, whole_ref):
-    arrived = ((2, beside_ref, 0), (5, beside_ref, 1), (6, below_ref, 0), (7, below_ref, 1), (8, diagonal_ref, 0))
+def arrivals(arrived, whole_ref):
     for place, (_, ref, slot) in enumerate(arrived):
         unpack(ref, slot, whole_ref, place)
-    parts = [(t, whole_ref, place) for place, (t, _, _) in enumerate(arrived)]
+    return [(t, whole_ref, place) for place, (t, _, _) in enumerate(arrived)]
+
+
+def middle_kernel(beside_ref, below_ref, high_ref, mix_ref, partial_ref, out_ref, whole_ref):
+    parts = arrivals(((2, beside_ref, 0), (5, beside_ref, 1), (6, below_ref, 0), (7, below_ref, 1)), whole_ref)
+    fields = mix_ref.shape[2]
+    for p in range(0, mix_ref.shape[1], 2):
+        lanes = slice(p * fields, (p + 2) * fields)
+        out_ref[:, lanes] = partial_ref[:, lanes] + blend(parts, high_ref, mix_ref, p)
+
+
+def last_kernel(diagonal_ref, high_ref, mix_ref, partial_ref, centre_ref, out_ref, all_ref, whole_ref):
+    parts = arrivals(((8, diagonal_ref, 0),), whole_ref)
     members, patches, fields = out_ref.shape
     for p in range(0, patches, 2):
         lanes = slice(p * fields, (p + 2) * fields)
@@ -321,12 +332,15 @@
         [VMEM] * 8,
         [pltpu.VMEM((1,) + left, BF16)] * 2 + [pltpu.VMEM((1, members, members), BF16)],
     )(x, pert, centre, dense, values, one, high, mix)
+    partial = call(middle_kernel, shape(flat, F32), [VMEM] * 5, [pltpu.VMEM((4, members, members), BF16)])(
+        beside, below, high, mix, partial
+    )
     analysis = call(
         last_kernel,
         shape((members, patches, fields), BF16),
-        [VMEM] * 7,
-        [wide, pltpu.VMEM((5, members, members), BF16)],
-    )(beside, below, diagonal, high, mix, partial, centre)
+        [VMEM] * 5,
+        [wide, pltpu.VMEM((1, members, members), BF16)],
+    )(diagonal, high, mix, partial, centre)
     returned = lax.all_to_all(analysis.reshape(devices, own, patches, fields), "mem", split_axis=0, concat_axis=0, tiled=True)
     result = call(returned_kernel, shape((own, devices, patches, fields), BF16), [VMEM], copies, HBM)(returned)
     return result.reshape(own, 1, all_patches, fields)

time: 73.1 us -> 72.7 us (level)
  waiting for transfers between devices: 18 us -> 17.2 us
    ppermute x1, waiting for transfers between devices: 2.61 us -> 1.03 us  [per_device(): diagonal = lax.ppermute(to_corner, ('mem', 'reg'), both)]
    ppermute x1, waiting for transfers between devices: 0.01 us -> 0.76 us  [per_device(): beside = lax.ppermute(to_beside, 'reg', across)]
  transfers between devices with their start and end apart: 4 -> 4, of which waited for: 2 -> 3; matrix products, arithmetic and copies ran while one was open for 0% -> 0% of each run, Pallas kernels for 6% -> 7%
where the time goes in v6:
time: 72.7 us; the launch traced here: 71.6 us
  blocking collectives  24.7 us (34%)
  waiting for transfers between devices  17.2 us (24%)
  starting transfers between devices  16 us (22%)
  Pallas kernels  12.9 us (18%)
  local copies, waits for them, and re-layouts  0.79 us (1%)
    all_to_all x1, blocking collectives, per_device(): lax.all_to_all(analysis.reshape(devices, own, patches, fields), 'mem', sp...  24.7 us
    all_to_all x1, waiting for transfers between devices, per_device(): lax.all_to_all(outgoing, 'mem', split_axis=0, concat_axis=0, tiled=True)  15.4 us
    all_to_all x1, starting transfers between devices, per_device(): lax.all_to_all(outgoing, 'mem', split_axis=0, concat_axis=0, tiled=True)  13.1 us
    pallas_call x1, Pallas kernels, per_device(): call(first_kernel, (shape((3, members, members), BF16), shape((2,) + pack...  4.43 us
    pallas_call x1, Pallas kernels, per_device(): call(second_kernel, shape(flat, F32), [VMEM] * 8, [pltpu.VMEM((1,) + left...  3.43 us
    pallas_call x1, Pallas kernels, per_device(): call(outgoing_kernel, shape(blocks, BF16), [HBM], [pltpu.VMEM((own,) + (d...  1.82 us
  transfers between devices with their start and end apart: 4, of which 3 were waited for; matrix products, arithmetic and copies ran while one was open for 0% of the time, Pallas kernels for 7%

profile of v6, /device:TPU:1, one launch (start us, length us, event | category | flops | bytes accessed | tf_op | source)
XLA Modules:
  0.0 71.6 jit_solution(10516572188880314767)
XLA Ops:
  0.0 1.8 %shard_map.82 = bf16[64,4,8,128]{3,2,1,0:T(8,128)(2,1)} custom-call(bf16[4,64,8,128]{3,2,1,0:T(8,128)(2,1)} %bitcast.10), custom_call_target="tpu_custom_call" | custom-call | tf_op jit(solution)/shard_map/pallas_call | solution.py:290
  1.8 0.0 copy-start.5
  1.8 0.0 copy-start.6
  1.8 0.0 copy-start.1
  1.9 0.0 copy-start.2
  1.9 0.0 copy-start.3
  1.9 13.1 %all-to-all-start = ((bf16[64,4,8,128]{3,2,1,0:T(8,128)(2,1)}), bf16[64,4,8,128]{3,2,1,0:T(8,128)(2,1)S(1)}, u32[]{:S(2)}, u32[]{:S(2)}) async-start(bf16[64,4,8,128]{3,2,1,0:T(8,128)(2,1)} %shard_map.82), calls=%async_computation | async-start | bytes 1048576 | tf_op jit(solution)/shard_map/all_to_all | solution.py:297
  15.0 0.0 copy-start
  15.0 0.0 copy-done.5
  15.0 0.1 copy.9.corner_ref
  15.1 0.0 copy-done.6
  15.1 0.0 copy-start.4
  15.1 0.1 copy.10.coeff_ref
  15.2 0.0 copy-done.1
  15.2 0.0 copy-done.2
  15.2 0.0 copy-done.3
  15.2 0.5 copy-done
  15.7 0.1 copy-done.4
  15.8 1.1 %shard_map.83 = (f32[4,8,128]{2,1,0:T(8,128)S(1)}, f32[4,8,128]{2,1,0:T(8,128)S(1)}, f32[9,8,128]{2,1,0:T(8,128)S(1)}) custom-call(s32[2,2]{1,0:T(2,128)S(1)} %copy-done.4, f32[2,2,512]{2,1,0:T(2,128)S(1)} %copy-done, f32[2,2,512]{2,1,0:T(2,128)S(1)} %copy-done.1, s32[2,2,512]{2,1,0:T(2,128)S(1)} %copy-done.2, s32[2,2,512]{2,1,0:T(2,128)S(1)} %copy-done.3, ...), custom_call_target="tpu_custom_call" | custom-call | tf_op jit(solution)/shard_map/pallas_call | solution.py:298
  16.9 15.4 %all-to-all-done = bf16[64,4,8,128]{3,2,1,0:T(8,128)(2,1)S(1)} async-done(((bf16[64,4,8,128]{3,2,1,0:T(8,128)(2,1)}), bf16[64,4,8,128]{3,2,1,0:T(8,128)(2,1)S(1)}, u32[]{:S(2)}, u32[]{:S(2)}) %all-to-all-start) | async-done | bytes 524320 | tf_op jit(solution)/shard_map/all_to_all | solution.py:297
  32.3 4.4 %shard_map.84 = (bf16[3,256,256]{2,1,0:T(8,128)(2,1)S(1)}, bf16[2,144,256]{2,1,0:T(8,128)(2,1)S(1)}, bf16[1,144,256]{2,1,0:T(8,128)(2,1)S(1)}, bf16[2,144,256]{2...) custom-call(bf16[256,8,128]{2,1,0:T(8,128)(2,1)S(1)} %bitcast.8, ...), custom_call_target="tpu_custom_call" | custom-call | tf_op jit(solution)/shard_map/pallas_call | solution.py:311
  36.7 1.3 %collective-permute-start.1 = (bf16[2,144,256]{2,1,0:T(8,128)(2,1)S(1)}, bf16[2,144,256]{2,1,0:T(8,128)(2,1)S(1)}, u32[]{:S(2)}, u32[]{:S(2)}) collective-permute-start(bf16[2,144,256]{2,1,0:T(8,128)(2,1)S(1)} %get-tuple-element.21), channel_id=1, source_target_pairs={{1,0},{2,1},{3,2},{5,4},{6,5},{7,6},{9,8},{10,9},{11,10},{13,12},{... | collective-permute-start | bytes 442376 | tf_op jit(solution)/shard_map/ppermute | solution.py:326
  38.0 0.3 collective-permute-start.2
  38.3 1.3 %collective-permute-start = (bf16[1,144,256]{2,1,0:T(8,128)(2,1)S(1)}, bf16[1,144,256]{2,1,0:T(8,128)(2,1)S(1)}, u32[]{:S(2)}, u32[]{:S(2)}) collective-permute-start(bf16[1,144,256]{2,1,0:T(8,128)(2,1)S(1)} %get-tuple-element.18), channel_id=1, source_target_pairs={{5,0},{6,1},{7,2},{9,4},{10,5},{11,6},{13,8},{14,9},{15,10},{17,12... | collective-permute-start | bytes 221192 | tf_op jit(solution)/shard_map/ppermute | solution.py:327
  39.6 3.4 %shard_map.85.partial_ref = f32[256,1024]{1,0:T(8,128)S(1)} custom-call(bf16[256,1024]{1,0:T(8,128)(2,1)S(1)} %get-tuple-element.23.x_ref, f32[256,1024]{1,0:T(8,128)S(1)} %get-tuple-element.24.pert_ref, f32[8,128]{1,0:T(8,128)S(1)} %get-tuple-element.25.centre_ref, f32[4,8,128]{2,1,0:T(8,128)S(1)} %get-tuple-element.16.dense_ref, ...), custom_call_target="tpu_custom_call" | custom-call | tf_op jit(solution)/shard_map/pallas_call | solution.py:329
  43.1 0.8 %collective-permute-done.1.beside_ref = bf16[2,144,256]{2,1,0:T(8,128)(2,1)S(1)} collective-permute-done((bf16[2,144,256]{2,1,0:T(8,128)(2,1)S(1)}, bf16[2,144,256]{2,1,0:T(8,128)(2,1)S(1)}, u32[]{:S(2)}, u32[]{:S(2)}) %collective-permute-start.1) | collective-permute-done | bytes 147488 | tf_op jit(solution)/shard_map/ppermute | solution.py:326
  43.8 0.0 collective-permute-done.2.below_ref
  43.8 0.8 %shard_map.86.partial_ref = f32[256,1024]{1,0:T(8,128)S(1)} custom-call(bf16[2,144,256]{2,1,0:T(8,128)(2,1)S(1)} %collective-permute-done.1.beside_ref, bf16[2,144,256]{2,1,0:T(8,128)(2,1)S(1)} %collective-permute-done.2.below_ref, bf16[256,1024]{1,0:T(8,128)(2,1)S(1)} %get-tuple-element.19.high_ref, f32[9,8,128]{2,1,0:T(8,128)S(1)} %get-tuple-element.20.mix_ref, ...), custom_call_target="tpu_custom_call" | custom-call | tf_op jit(solution)/shard_map/pallas_call | solution.py:335
  44.7 1.0 %collective-permute-done.diagonal_ref = bf16[1,144,256]{2,1,0:T(8,128)(2,1)S(1)} collective-permute-done((bf16[1,144,256]{2,1,0:T(8,128)(2,1)S(1)}, bf16[1,144,256]{2,1,0:T(8,128)(2,1)S(1)}, u32[]{:S(2)}, u32[]{:S(2)}) %collective-permute-start) | collective-permute-done | bytes 73760 | tf_op jit(solution)/shard_map/ppermute | solution.py:327
  45.7 0.5 shard_map.87
  46.2 24.7 %all_to_all.10.source_ref = bf16[64,4,8,128]{3,2,1,0:T(8,128)(2,1)S(1)} all-to-all(bf16[64,4,8,128]{3,2,1,0:T(8,128)(2,1)S(1)} %bitcast.9), channel_id=1, replica_groups=mesh['mem'=64,'reg'=4] {'mem'}, dimensions={0} | all-to-all | bytes 1048576 | tf_op jit(solution)/shard_map/all_to_all | solution.py:344
  70.8 0.8 %shard_map.88 = bf16[4,64,8,128]{3,2,1,0:T(8,128)(2,1)} custom-call(bf16[64,4,8,128]{3,2,1,0:T(8,128)(2,1)S(1)} %all_to_all.10.source_ref), custom_call_target="tpu_custom_call" | custom-call | tf_op jit(solution)/shard_map/pallas_call | solution.py:345
Async XLA Ops:
  1.8 13.2 %copy-start.5 = (s32[1,8,4]{1,2,0:T(4,128)S(1)}, s32[1,8,4]{1,2,0:T(4,128)}, u32[]{:S(2)}) copy-start(s32[1,8,4]{1,2,0:T(4,128)} %param.14) | copy-start | bytes 388
  1.8 13.3 %copy-start.6 = (f32[1,8,4]{1,2,0:T(4,128)S(1)}, f32[1,8,4]{1,2,0:T(4,128)}, u32[]{:S(2)}) copy-start(f32[1,8,4]{1,2,0:T(4,128)} %param.15) | copy-start | bytes 388
  1.8 13.4 %copy-start.1 = (f32[2,2,512]{2,1,0:T(2,128)S(1)}, f32[2,2,512]{2,1,0:T(2,128)}, u32[]{:S(2)}) copy-start(f32[2,2,512]{2,1,0:T(2,128)} %error_ref.1) | copy-start | bytes 24580
  1.9 13.3 %copy-start.2 = (s32[2,2,512]{2,1,0:T(2,128)S(1)}, s32[2,2,512]{2,1,0:T(2,128)}, u32[]{:S(2)}) copy-start(s32[2,2,512]{2,1,0:T(2,128)} %patch_ref.1) | copy-start | bytes 24580
  1.9 13.3 %copy-start.3 = (s32[2,2,512]{2,1,0:T(2,128)S(1)}, s32[2,2,512]{2,1,0:T(2,128)}, u32[]{:S(2)}) copy-start(s32[2,2,512]{2,1,0:T(2,128)} %var_ref.1) | copy-start | bytes 24580
  1.9 30.4 %all-to-all-start = ((bf16[64,4,8,128]{3,2,1,0:T(8,128)(2,1)}), bf16[64,4,8,128]{3,2,1,0:T(8,128)(2,1)S(1)}, u32[]{:S(2)}, u32[]{:S(2)}) async-start(bf16[64,4,8,128]{3,2,1,0:T(8,128)(2,1)} %shard_map.82), calls=%async_computation | async-start | bytes 1048576 | tf_op jit(solution)/shard_map/all_to_all | solution.py:297
  15.0 0.7 copy-start
  15.1 0.7 copy-start.4
  36.7 7.1 %collective-permute-start.1 = (bf16[2,144,256]{2,1,0:T(8,128)(2,1)S(1)}, bf16[2,144,256]{2,1,0:T(8,128)(2,1)S(1)}, u32[]{:S(2)}, u32[]{:S(2)}) collective-permute-start(bf16[2,144,256]{2,1,0:T(8,128)(2,1)S(1)} %get-tuple-element.21), channel_id=1, source_target_pairs={{1,0},{2,1},{3,2},{5,4},{6,5},{7,6},{9,8},{10,9},{11,10},{13,12},{... | collective-permute-start | bytes 442376 | tf_op jit(solution)/shard_map/ppermute | solution.py:326
  38.0 5.8 %collective-permute-start.2 = (bf16[2,144,256]{2,1,0:T(8,128)(2,1)S(1)}, bf16[2,144,256]{2,1,0:T(8,128)(2,1)S(1)}, u32[]{:S(2)}, u32[]{:S(2)}) collective-permute-start(bf16[2,144,256]{2,1,0:T(8,128)(2,1)S(1)} %get-tuple-element.22), channel_id=1, source_target_pairs={{4,0},{8,4},{12,8},{16,12},{20,16},{24,20},{28,24},{32,28},{36,32}... | collective-permute-start | bytes 442376 | tf_op jit(solution)/shard_map/ppermute | solution.py:328
  38.3 7.4 %collective-permute-start = (bf16[1,144,256]{2,1,0:T(8,128)(2,1)S(1)}, bf16[1,144,256]{2,1,0:T(8,128)(2,1)S(1)}, u32[]{:S(2)}, u32[]{:S(2)}) collective-permute-start(bf16[1,144,256]{2,1,0:T(8,128)(2,1)S(1)} %get-tuple-element.18), channel_id=1, source_target_pairs={{5,0},{6,1},{7,2},{9,4},{10,5},{11,6},{13,8},{14,9},{15,10},{17,12... | collective-permute-start | bytes 221192 | tf_op jit(solution)/shard_map/ppermute | solution.py:327

commit v7 on v6

--- a/solution.py
+++ b/solution.py
@@ -91,7 +91,7 @@
     return 1.5 * square - x + dot(square.astype(BF16), (square - 2.5 * x).astype(BF16))
 
 
-def weights_of(count, x_ref, left_high, left_low, out_ref):
+def weights_of(count, x_ref, left_high, left_low, out_ref, fill=lambda: None):
     members = x_ref.shape[0]
     half = members // 2
     row = lax.broadcasted_iota(jnp.int32, (half, half), 0)
@@ -111,10 +111,14 @@
         state.append((projected, scaling, add_diagonal(gram * half_inverse, (members - 1.0) * half_inverse, diagonal)))
     parts = [split(x) for _, _, x in state]
     roots = [two_factors(state[s][2], parts[s], diagonal) for s in slots]
+    fill()
     z = [split(x) for x in roots]
     y = [split(product(parts[s], z[s])) for s in slots]
+    fill()
     excess = [add_diagonal(product(y[s], z[s]), -0.5, diagonal) for s in slots]
+    fill()
     rest = [later_factors(x) for x in excess]
+    fill()
     inverses = [roots[s] + rest[s] + dot(rest[s].astype(BF16), add_diagonal(roots[s], -1.0, diagonal).astype(BF16)) for s in slots]
     for slot in slots:
         projected, scaling, _ = state[slot]
@@ -188,14 +192,18 @@
             pack(below_ref if slot == 1 else beside_ref, 1, spread, twice)
 
 
-def second_kernel(x_ref, pert_ref, centre_ref, dense_ref, value_ref, one_ref, high_ref, mix_ref, out_ref, left_high, left_low, two_ref):
+def second_kernel(x_ref, pert_ref, centre_ref, dense_ref, value_ref, one_ref, high_ref, mix_ref, out_ref, two_ref, left_high, left_low):
     patches, fields = centre_ref.shape
+    tiles = iter(range(0, patches, 2))
+
+    def fill():
+        p = next(tiles)
+        parts = ((0, one_ref, 0), (1, one_ref, 1), (3, one_ref, 2))
+        out_ref[:, p * fields : (p + 2) * fields] = blend(parts, high_ref, mix_ref, p)
+
     shares((3,), pert_ref, centre_ref[...], dense_ref, value_ref, left_high, left_low)
-    parts = ((0, one_ref, 0), (1, one_ref, 1), (3, one_ref, 2), (4, two_ref, 0))
-    for _ in weights_of(1, x_ref, left_high, left_low, two_ref):
+    for _ in weights_of(1, x_ref, left_high, left_low, two_ref, fill):
         pass
-    for p in range(0, patches, 2):
-        out_ref[:, p * fields : (p + 2) * fields] = blend(parts, high_ref, mix_ref, p)
 
 
 def blend(parts, high_ref, mix_ref, p):
@@ -216,8 +224,8 @@
     return [(t, whole_ref, place) for place, (t, _, _) in enumerate(arrived)]
 
 
-def middle_kernel(beside_ref, below_ref, high_ref, mix_ref, partial_ref, out_ref, whole_ref):
-    parts = arrivals(((2, beside_ref, 0), (5, beside_ref, 1), (6, below_ref, 0), (7, below_ref, 1)), whole_ref)
+def middle_kernel(beside_ref, below_ref, two_ref, high_ref, mix_ref, partial_ref, out_ref, whole_ref):
+    parts = arrivals(((2, beside_ref, 0), (5, beside_ref, 1), (6, below_ref, 0), (7, below_ref, 1)), whole_ref) + [(4, two_ref, 0)]
     fields = mix_ref.shape[2]
     for p in range(0, mix_ref.shape[1], 2):
         lanes = slice(p * fields, (p + 2) * fields)
@@ -326,14 +334,14 @@
     beside = lax.ppermute(to_beside, "reg", across)
     diagonal = lax.ppermute(to_corner, ("mem", "reg"), both)
     below = lax.ppermute(to_below, "mem", down)
-    partial = call(
+    partial, two = call(
         second_kernel,
-        shape(flat, F32),
+        (shape(flat, F32), shape((1, members, members), BF16)),
         [VMEM] * 8,
-        [pltpu.VMEM((1,) + left, BF16)] * 2 + [pltpu.VMEM((1, members, members), BF16)],
+        [pltpu.VMEM((1,) + left, BF16)] * 2,
     )(x, pert, centre, dense, values, one, high, mix)
-    partial = call(middle_kernel, shape(flat, F32), [VMEM] * 5, [pltpu.VMEM((4, members, members), BF16)])(
-        beside, below, high, mix, partial
+    partial = call(middle_kernel, shape(flat, F32), [VMEM] * 6, [pltpu.VMEM((4, members, members), BF16)])(
+        beside, below, two, high, mix, partial
     )
     analysis = call(
         last_kernel,

time: 72.7 us -> 72.4 us (level)
  no operation moved by 1% of the time
where the time goes in v7:
time: 72.4 us; the launch traced here: 71.6 us
  blocking collectives  24.7 us (34%)
  waiting for transfers between devices  17.7 us (24%)
  starting transfers between devices  16 us (22%)
  Pallas kernels  12.4 us (17%)
  local copies, waits for them, and re-layouts  0.79 us (1%)
    all_to_all x1, blocking collectives, per_device(): lax.all_to_all(analysis.reshape(devices, own, patches, fields), 'mem', sp...  24.7 us
    all_to_all x1, waiting for transfers between devices, per_device(): lax.all_to_all(outgoing, 'mem', split_axis=0, concat_axis=0, tiled=True)  15.4 us
    all_to_all x1, starting transfers between devices, per_device(): lax.all_to_all(outgoing, 'mem', split_axis=0, concat_axis=0, tiled=True)  13.1 us
    pallas_call x1, Pallas kernels, per_device(): call(first_kernel, (shape((3, members, members), BF16), shape((2,) + pack...  4.43 us
    pallas_call x1, Pallas kernels, per_device(): call(second_kernel, (shape(flat, F32), shape((1, members, members), BF16)...  2.84 us
    pallas_call x1, Pallas kernels, per_device(): call(outgoing_kernel, shape(blocks, BF16), [HBM], [pltpu.VMEM((own,) + (d...  1.82 us
  transfers between devices with their start and end apart: 4, of which 3 were waited for; matrix products, arithmetic and copies ran while one was open for 0% of the time, Pallas kernels for 7%

profile of v7, /device:TPU:1, one launch (start us, length us, event | category | flops | bytes accessed | tf_op | source)
XLA Modules:
  0.0 71.6 jit_solution(7769343940127921008)
XLA Ops:
  0.0 1.8 %shard_map.82 = bf16[64,4,8,128]{3,2,1,0:T(8,128)(2,1)} custom-call(bf16[4,64,8,128]{3,2,1,0:T(8,128)(2,1)} %bitcast.10), custom_call_target="tpu_custom_call" | custom-call | tf_op jit(solution)/shard_map/pallas_call | solution.py:298
  1.8 0.0 copy-start.5
  1.8 0.0 copy-start.6
  1.8 0.0 copy-start.1
  1.9 0.0 copy-start.2
  1.9 0.0 copy-start.3
  1.9 13.1 %all-to-all-start = ((bf16[64,4,8,128]{3,2,1,0:T(8,128)(2,1)}), bf16[64,4,8,128]{3,2,1,0:T(8,128)(2,1)S(1)}, u32[]{:S(2)}, u32[]{:S(2)}) async-start(bf16[64,4,8,128]{3,2,1,0:T(8,128)(2,1)} %shard_map.82), calls=%async_computation | async-start | bytes 1048576 | tf_op jit(solution)/shard_map/all_to_all | solution.py:305
  15.0 0.0 copy-start
  15.0 0.0 copy-done.5
  15.0 0.1 copy.9.corner_ref
  15.1 0.0 copy-done.6
  15.1 0.0 copy-start.4
  15.1 0.1 copy.10.coeff_ref
  15.2 0.0 copy-done.1
  15.2 0.0 copy-done.2
  15.2 0.0 copy-done.3
  15.2 0.5 copy-done
  15.7 0.1 copy-done.4
  15.8 1.1 %shard_map.83 = (f32[4,8,128]{2,1,0:T(8,128)S(1)}, f32[4,8,128]{2,1,0:T(8,128)S(1)}, f32[9,8,128]{2,1,0:T(8,128)S(1)}) custom-call(s32[2,2]{1,0:T(2,128)S(1)} %copy-done.4, f32[2,2,512]{2,1,0:T(2,128)S(1)} %copy-done, f32[2,2,512]{2,1,0:T(2,128)S(1)} %copy-done.1, s32[2,2,512]{2,1,0:T(2,128)S(1)} %copy-done.2, s32[2,2,512]{2,1,0:T(2,128)S(1)} %copy-done.3, ...), custom_call_target="tpu_custom_call" | custom-call | tf_op jit(solution)/shard_map/pallas_call | solution.py:306
  16.9 15.4 %all-to-all-done = bf16[64,4,8,128]{3,2,1,0:T(8,128)(2,1)S(1)} async-done(((bf16[64,4,8,128]{3,2,1,0:T(8,128)(2,1)}), bf16[64,4,8,128]{3,2,1,0:T(8,128)(2,1)S(1)}, u32[]{:S(2)}, u32[]{:S(2)}) %all-to-all-start) | async-done | bytes 524320 | tf_op jit(solution)/shard_map/all_to_all | solution.py:305
  32.3 4.4 %shard_map.84 = (bf16[3,256,256]{2,1,0:T(8,128)(2,1)S(1)}, bf16[2,144,256]{2,1,0:T(8,128)(2,1)S(1)}, bf16[1,144,256]{2,1,0:T(8,128)(2,1)S(1)}, bf16[2,144,256]{2...) custom-call(bf16[256,8,128]{2,1,0:T(8,128)(2,1)S(1)} %bitcast.8, ...), custom_call_target="tpu_custom_call" | custom-call | tf_op jit(solution)/shard_map/pallas_call | solution.py:319
  36.7 1.3 %collective-permute-start.1 = (bf16[2,144,256]{2,1,0:T(8,128)(2,1)S(1)}, bf16[2,144,256]{2,1,0:T(8,128)(2,1)S(1)}, u32[]{:S(2)}, u32[]{:S(2)}) collective-permute-start(bf16[2,144,256]{2,1,0:T(8,128)(2,1)S(1)} %get-tuple-element.23), channel_id=1, source_target_pairs={{1,0},{2,1},{3,2},{5,4},{6,5},{7,6},{9,8},{10,9},{11,10},{13,12},{... | collective-permute-start | bytes 442376 | tf_op jit(solution)/shard_map/ppermute | solution.py:334
  38.0 0.3 collective-permute-start.2
  38.3 1.3 %collective-permute-start = (bf16[1,144,256]{2,1,0:T(8,128)(2,1)S(1)}, bf16[1,144,256]{2,1,0:T(8,128)(2,1)S(1)}, u32[]{:S(2)}, u32[]{:S(2)}) collective-permute-start(bf16[1,144,256]{2,1,0:T(8,128)(2,1)S(1)} %get-tuple-element.20), channel_id=1, source_target_pairs={{5,0},{6,1},{7,2},{9,4},{10,5},{11,6},{13,8},{14,9},{15,10},{17,12... | collective-permute-start | bytes 221192 | tf_op jit(solution)/shard_map/ppermute | solution.py:335
  39.6 2.8 %shard_map.85 = (f32[256,1024]{1,0:T(8,128)S(1)}, bf16[1,256,256]{2,1,0:T(8,128)(2,1)S(1)}) custom-call(bf16[256,1024]{1,0:T(8,128)(2,1)S(1)} %get-tuple-element.25.x_ref, f32[256,1024]{1,0:T(8,128)S(1)} %get-tuple-element.26.pert_ref, f32[8,128]{1,0:T(8,128)S(1)} %get-tuple-element.27.centre_ref, f32[4,8,128]{2,1,0:T(8,128)S(1)} %get-tuple-element.18.dense_ref, ...), custom_call_target="tpu_custom_call" | custom-call | tf_op jit(solution)/shard_map/pallas_call | solution.py:337
  42.5 1.4 %collective-permute-done.1.beside_ref = bf16[2,144,256]{2,1,0:T(8,128)(2,1)S(1)} collective-permute-done((bf16[2,144,256]{2,1,0:T(8,128)(2,1)S(1)}, bf16[2,144,256]{2,1,0:T(8,128)(2,1)S(1)}, u32[]{:S(2)}, u32[]{:S(2)}) %collective-permute-start.1) | collective-permute-done | bytes 147488 | tf_op jit(solution)/shard_map/ppermute | solution.py:334
  43.8 0.0 collective-permute-done.2.below_ref
  43.8 1.0 %shard_map.86.partial_ref = f32[256,1024]{1,0:T(8,128)S(1)} custom-call(bf16[2,144,256]{2,1,0:T(8,128)(2,1)S(1)} %collective-permute-done.1.beside_ref, bf16[2,144,256]{2,1,0:T(8,128)(2,1)S(1)} %collective-permute-done.2.below_ref, bf16[1,256,256]{2,1,0:T(8,128)(2,1)S(1)} %get-tuple-element.29.two_ref, bf16[256,1024]{1,0:T(8,128)(2,1)S(1)} %get-tuple-element.21.high_ref, ...), custom_call_target="tpu_custom_call" | custom-call | tf_op jit(solution)/shard_map/pallas_call | solution.py:343
  44.8 0.9 %collective-permute-done.diagonal_ref = bf16[1,144,256]{2,1,0:T(8,128)(2,1)S(1)} collective-permute-done((bf16[1,144,256]{2,1,0:T(8,128)(2,1)S(1)}, bf16[1,144,256]{2,1,0:T(8,128)(2,1)S(1)}, u32[]{:S(2)}, u32[]{:S(2)}) %collective-permute-start) | collective-permute-done | bytes 73760 | tf_op jit(solution)/shard_map/ppermute | solution.py:335
  45.7 0.5 shard_map.87
  46.2 24.7 %all_to_all.10.source_ref = bf16[64,4,8,128]{3,2,1,0:T(8,128)(2,1)S(1)} all-to-all(bf16[64,4,8,128]{3,2,1,0:T(8,128)(2,1)S(1)} %bitcast.9), channel_id=1, replica_groups=mesh['mem'=64,'reg'=4] {'mem'}, dimensions={0} | all-to-all | bytes 1048576 | tf_op jit(solution)/shard_map/all_to_all | solution.py:352
  70.8 0.8 %shard_map.88 = bf16[4,64,8,128]{3,2,1,0:T(8,128)(2,1)} custom-call(bf16[64,4,8,128]{3,2,1,0:T(8,128)(2,1)S(1)} %all_to_all.10.source_ref), custom_call_target="tpu_custom_call" | custom-call | tf_op jit(solution)/shard_map/pallas_call | solution.py:353
Async XLA Ops:
  1.8 13.2 %copy-start.5 = (s32[1,8,4]{1,2,0:T(4,128)S(1)}, s32[1,8,4]{1,2,0:T(4,128)}, u32[]{:S(2)}) copy-start(s32[1,8,4]{1,2,0:T(4,128)} %param.14) | copy-start | bytes 388
  1.8 13.3 %copy-start.6 = (f32[1,8,4]{1,2,0:T(4,128)S(1)}, f32[1,8,4]{1,2,0:T(4,128)}, u32[]{:S(2)}) copy-start(f32[1,8,4]{1,2,0:T(4,128)} %param.15) | copy-start | bytes 388
  1.8 13.4 %copy-start.1 = (f32[2,2,512]{2,1,0:T(2,128)S(1)}, f32[2,2,512]{2,1,0:T(2,128)}, u32[]{:S(2)}) copy-start(f32[2,2,512]{2,1,0:T(2,128)} %error_ref.1) | copy-start | bytes 24580
  1.9 13.3 %copy-start.2 = (s32[2,2,512]{2,1,0:T(2,128)S(1)}, s32[2,2,512]{2,1,0:T(2,128)}, u32[]{:S(2)}) copy-start(s32[2,2,512]{2,1,0:T(2,128)} %patch_ref.1) | copy-start | bytes 24580
  1.9 13.3 %copy-start.3 = (s32[2,2,512]{2,1,0:T(2,128)S(1)}, s32[2,2,512]{2,1,0:T(2,128)}, u32[]{:S(2)}) copy-start(s32[2,2,512]{2,1,0:T(2,128)} %var_ref.1) | copy-start | bytes 24580
  1.9 30.4 %all-to-all-start = ((bf16[64,4,8,128]{3,2,1,0:T(8,128)(2,1)}), bf16[64,4,8,128]{3,2,1,0:T(8,128)(2,1)S(1)}, u32[]{:S(2)}, u32[]{:S(2)}) async-start(bf16[64,4,8,128]{3,2,1,0:T(8,128)(2,1)} %shard_map.82), calls=%async_computation | async-start | bytes 1048576 | tf_op jit(solution)/shard_map/all_to_all | solution.py:305
  15.0 0.7 copy-start
  15.1 0.7 copy-start.4
  36.7 7.1 %collective-permute-start.1 = (bf16[2,144,256]{2,1,0:T(8,128)(2,1)S(1)}, bf16[2,144,256]{2,1,0:T(8,128)(2,1)S(1)}, u32[]{:S(2)}, u32[]{:S(2)}) collective-permute-start(bf16[2,144,256]{2,1,0:T(8,128)(2,1)S(1)} %get-tuple-element.23), channel_id=1, source_target_pairs={{1,0},{2,1},{3,2},{5,4},{6,5},{7,6},{9,8},{10,9},{11,10},{13,12},{... | collective-permute-start | bytes 442376 | tf_op jit(solution)/shard_map/ppermute | solution.py:334
  38.0 5.8 %collective-permute-start.2 = (bf16[2,144,256]{2,1,0:T(8,128)(2,1)S(1)}, bf16[2,144,256]{2,1,0:T(8,128)(2,1)S(1)}, u32[]{:S(2)}, u32[]{:S(2)}) collective-permute-start(bf16[2,144,256]{2,1,0:T(8,128)(2,1)S(1)} %get-tuple-element.24), channel_id=1, source_target_pairs={{4,0},{8,4},{12,8},{16,12},{20,16},{24,20},{28,24},{32,28},{36,32}... | collective-permute-start | bytes 442376 | tf_op jit(solution)/shard_map/ppermute | solution.py:336
  38.3 7.4 %collective-permute-start = (bf16[1,144,256]{2,1,0:T(8,128)(2,1)S(1)}, bf16[1,144,256]{2,1,0:T(8,128)(2,1)S(1)}, u32[]{:S(2)}, u32[]{:S(2)}) collective-permute-start(bf16[1,144,256]{2,1,0:T(8,128)(2,1)S(1)} %get-tuple-element.20), channel_id=1, source_target_pairs={{5,0},{6,1},{7,2},{9,4},{10,5},{11,6},{13,8},{14,9},{15,10},{17,12... | collective-permute-start | bytes 221192 | tf_op jit(solution)/shard_map/ppermute | solution.py:335

commit v8 on v7

--- a/solution.py
+++ b/solution.py
@@ -164,7 +164,7 @@
 
 
 def first_kernel(
-    ensemble_ref, dense_ref, value_ref, out_ref, beside_ref, corner_ref, below_ref, x_ref, pert_ref, high_ref, centre_ref, wide_ref, left_high, left_low
+    ensemble_ref, dense_ref, value_ref, out_ref, corner_ref, below_ref, x_ref, pert_ref, high_ref, centre_ref, wide_ref, left_high, left_low
 ):
     members, patches, fields = ensemble_ref.shape
     total = jnp.zeros((patches, fields), F32)
@@ -182,28 +182,28 @@
         pert = part - centre[p : p + 1, :]
         pert_ref[:, lanes] = pert
         high_ref[:, lanes] = pert.astype(BF16)
-    shares((0, 1, 2), pert_ref, centre, dense_ref, value_ref, left_high, left_low)
-    for slot, spread, twice in weights_of(3, x_ref, left_high, left_low, out_ref):
+    shares((0, 1), pert_ref, centre, dense_ref, value_ref, left_high, left_low)
+    for slot, spread, twice in weights_of(2, x_ref, left_high, left_low, out_ref):
+        pack(below_ref, slot, spread, twice)
         if slot == 0:
-            pack(corner_ref, 0, spread, twice)
-            beside_ref[0] = corner_ref[0]
-            below_ref[0] = corner_ref[0]
-        else:
-            pack(below_ref if slot == 1 else beside_ref, 1, spread, twice)
-
-
-def second_kernel(x_ref, pert_ref, centre_ref, dense_ref, value_ref, one_ref, high_ref, mix_ref, out_ref, two_ref, left_high, left_low):
+            corner_ref[0] = below_ref[0]
+
+
+def second_kernel(
+    x_ref, pert_ref, centre_ref, dense_ref, value_ref, one_ref, corner_ref, high_ref, mix_ref, out_ref, two_ref, beside_ref, left_high, left_low
+):
     patches, fields = centre_ref.shape
     tiles = iter(range(0, patches, 2))
 
     def fill():
         p = next(tiles)
-        parts = ((0, one_ref, 0), (1, one_ref, 1), (3, one_ref, 2))
-        out_ref[:, p * fields : (p + 2) * fields] = blend(parts, high_ref, mix_ref, p)
-
-    shares((3,), pert_ref, centre_ref[...], dense_ref, value_ref, left_high, left_low)
-    for _ in weights_of(1, x_ref, left_high, left_low, two_ref, fill):
-        pass
+        out_ref[:, p * fields : (p + 2) * fields] = blend(((0, one_ref, 0), (1, one_ref, 1)), high_ref, mix_ref, p)
+
+    beside_ref[0] = corner_ref[0]
+    shares((2, 3), pert_ref, centre_ref[...], dense_ref, value_ref, left_high, left_low)
+    for slot, spread, twice in weights_of(2, x_ref, left_high, left_low, two_ref, fill):
+        if slot == 0:
+            pack(beside_ref, 1, spread, twice)
 
 
 def blend(parts, high_ref, mix_ref, p):
@@ -224,16 +224,16 @@
     return [(t, whole_ref, place) for place, (t, _, _) in enumerate(arrived)]
 
 
-def middle_kernel(beside_ref, below_ref, two_ref, high_ref, mix_ref, partial_ref, out_ref, whole_ref):
-    parts = arrivals(((2, beside_ref, 0), (5, beside_ref, 1), (6, below_ref, 0), (7, below_ref, 1)), whole_ref) + [(4, two_ref, 0)]
+def middle_kernel(below_ref, diagonal_ref, two_ref, high_ref, mix_ref, partial_ref, out_ref, whole_ref):
+    parts = arrivals(((6, below_ref, 0), (7, below_ref, 1), (8, diagonal_ref, 0)), whole_ref) + [(3, two_ref, 0), (4, two_ref, 1)]
     fields = mix_ref.shape[2]
     for p in range(0, mix_ref.shape[1], 2):
         lanes = slice(p * fields, (p + 2) * fields)
         out_ref[:, lanes] = partial_ref[:, lanes] + blend(parts, high_ref, mix_ref, p)
 
 
-def last_kernel(diagonal_ref, high_ref, mix_ref, partial_ref, centre_ref, out_ref, all_ref, whole_ref):
-    parts = arrivals(((8, diagonal_ref, 0),), whole_ref)
+def last_kernel(beside_ref, high_ref, mix_ref, partial_ref, centre_ref, out_ref, all_ref, whole_ref):
+    parts = arrivals(((2, beside_ref, 0), (5, beside_ref, 1)), whole_ref)
     members, patches, fields = out_ref.shape
     for p in range(0, patches, 2):
         lanes = slice(p * fields, (p + 2) * fields)
@@ -316,11 +316,12 @@
     down = [((d + 1) % devices, d) for d in range(devices)]
     across = [(r + 1, r) for r in range(regions - 1)]
     both = [(d * regions + r, e * regions + t) for d, e in down for r, t in across]
-    one, to_beside, to_corner, to_below, x, pert, high, centre = call(
+    pair = shape((2, members, members), BF16)
+    lefts = [pltpu.VMEM((2,) + left, BF16)] * 2
+    one, to_corner, to_below, x, pert, high, centre = call(
         first_kernel,
         (
-            shape((3, members, members), BF16),
-            shape((2,) + packed, BF16),
+            pair,
             shape((1,) + packed, BF16),
             shape((2,) + packed, BF16),
             shape(flat, BF16),
@@ -329,26 +330,23 @@
             shape((patches, fields), F32),
         ),
         [VMEM] * 3,
-        [wide] + [pltpu.VMEM((3,) + left, BF16)] * 2,
+        [wide] + lefts,
     )(ensemble, dense, values)
-    beside = lax.ppermute(to_beside, "reg", across)
     diagonal = lax.ppermute(to_corner, ("mem", "reg"), both)
     below = lax.ppermute(to_below, "mem", down)
-    partial, two = call(
-        second_kernel,
-        (shape(flat, F32), shape((1, members, members), BF16)),
-        [VMEM] * 8,
-        [pltpu.VMEM((1,) + left, BF16)] * 2,
-    )(x, pert, centre, dense, values, one, high, mix)
-    partial = call(middle_kernel, shape(flat, F32), [VMEM] * 6, [pltpu.VMEM((4, members, members), BF16)])(
-        beside, below, two, high, mix, partial
+    partial, two, to_beside = call(second_kernel, (shape(flat, F32), pair, shape((2,) + packed, BF16)), [VMEM] * 9, lefts)(
+        x, pert, centre, dense, values, one, to_corner, high, mix
+    )
+    beside = lax.ppermute(to_beside, "reg", across)
+    partial = call(middle_kernel, shape(flat, F32), [VMEM] * 6, [pltpu.VMEM((3, members, members), BF16)])(
+        below, diagonal, two, high, mix, partial
     )
     analysis = call(
         last_kernel,
         shape((members, patches, fields), BF16),
         [VMEM] * 5,
-        [wide, pltpu.VMEM((1, members, members), BF16)],
-    )(diagonal, high, mix, partial, centre)
+        [wide, pltpu.VMEM((2, members, members), BF16)],
+    )(beside, high, mix, partial, centre)
     returned = lax.all_to_all(analysis.reshape(devices, own, patches, fields), "mem", split_axis=0, concat_axis=0, tiled=True)
     result = call(returned_kernel, shape((own, devices, patches, fields), BF16), [VMEM], copies, HBM)(returned)
     return result.reshape(own, 1, all_patches, fields)

time: 72.4 us -> 75.8 us (1.047)
  waiting for transfers between devices: 17.7 us -> 21.8 us
    ppermute x1, waiting for transfers between devices: 0.88 us -> 6.35 us  [per_device(): diagonal = lax.ppermute(to_corner, ('mem', 'reg'), both)]
    ppermute x1, waiting for transfers between devices: 1.35 us -> 0.01 us  [per_device(): beside = lax.ppermute(to_beside, 'reg', across)]
  transfers between devices with their start and end apart: 4 -> 4, of which waited for: 3 -> 2; matrix products, arithmetic and copies ran while one was open for 0% -> 0% of each run, Pallas kernels for 7% -> 7%
where the time goes in v8:
time: 75.8 us; the launch traced here: 75.5 us
  blocking collectives  24.5 us (32%)
  waiting for transfers between devices  21.8 us (29%)
  starting transfers between devices  16 us (21%)
  Pallas kernels  12.2 us (16%)
  local copies, waits for them, and re-layouts  0.79 us (1%)
    all_to_all x1, blocking collectives, per_device(): lax.all_to_all(analysis.reshape(devices, own, patches, fields), 'mem', sp...  24.5 us
    all_to_all x1, waiting for transfers between devices, per_device(): lax.all_to_all(outgoing, 'mem', split_axis=0, concat_axis=0, tiled=True)  15.4 us
    all_to_all x1, starting transfers between devices, per_device(): lax.all_to_all(outgoing, 'mem', split_axis=0, concat_axis=0, tiled=True)  13.1 us
    ppermute x1, waiting for transfers between devices, per_device(): diagonal = lax.ppermute(to_corner, ('mem', 'reg'), both)  6.35 us
    pallas_call x1, Pallas kernels, per_device(): call(first_kernel, (pair, shape((1,) + packed, BF16), shape((2,) + packed...  3.64 us
    pallas_call x1, Pallas kernels, per_device(): call(second_kernel, (shape(flat, F32), pair, shape((2,) + packed, BF16)),...  3.33 us
    pallas_call x1, Pallas kernels, per_device(): call(outgoing_kernel, shape(blocks, BF16), [HBM], [pltpu.VMEM((own,) + (d...  1.82 us
  transfers between devices with their start and end apart: 4, of which 2 were waited for; matrix products, arithmetic and copies ran while one was open for 0% of the time, Pallas kernels for 7%

profile of v8, /device:TPU:1, one launch (start us, length us, event | category | flops | bytes accessed | tf_op | source)
XLA Modules:
  0.0 75.5 jit_solution(3331024443198129441)
XLA Ops:
  0.0 1.8 %shard_map.82 = bf16[64,4,8,128]{3,2,1,0:T(8,128)(2,1)} custom-call(bf16[4,64,8,128]{3,2,1,0:T(8,128)(2,1)} %bitcast.10), custom_call_target="tpu_custom_call" | custom-call | tf_op jit(solution)/shard_map/pallas_call | solution.py:298
  1.8 0.0 copy-start.5
  1.8 0.0 copy-start.6
  1.8 0.0 copy-start.1
  1.9 0.0 copy-start.2
  1.9 0.0 copy-start.3
  1.9 13.1 %all-to-all-start = ((bf16[64,4,8,128]{3,2,1,0:T(8,128)(2,1)}), bf16[64,4,8,128]{3,2,1,0:T(8,128)(2,1)S(1)}, u32[]{:S(2)}, u32[]{:S(2)}) async-start(bf16[64,4,8,128]{3,2,1,0:T(8,128)(2,1)} %shard_map.82), calls=%async_computation | async-start | bytes 1048576 | tf_op jit(solution)/shard_map/all_to_all | solution.py:305
  15.0 0.0 copy-start
  15.0 0.0 copy-done.5
  15.0 0.1 copy.9.corner_ref
  15.1 0.0 copy-done.6
  15.1 0.0 copy-start.4
  15.1 0.1 copy.10.coeff_ref
  15.2 0.0 copy-done.1
  15.2 0.0 copy-done.2
  15.2 0.0 copy-done.3
  15.2 0.5 copy-done
  15.7 0.1 copy-done.4
  15.8 1.1 %shard_map.83 = (f32[4,8,128]{2,1,0:T(8,128)S(1)}, f32[4,8,128]{2,1,0:T(8,128)S(1)}, f32[9,8,128]{2,1,0:T(8,128)S(1)}) custom-call(s32[2,2]{1,0:T(2,128)S(1)} %copy-done.4, f32[2,2,512]{2,1,0:T(2,128)S(1)} %copy-done, f32[2,2,512]{2,1,0:T(2,128)S(1)} %copy-done.1, s32[2,2,512]{2,1,0:T(2,128)S(1)} %copy-done.2, s32[2,2,512]{2,1,0:T(2,128)S(1)} %copy-done.3, ...), custom_call_target="tpu_custom_call" | custom-call | tf_op jit(solution)/shard_map/pallas_call | solution.py:306
  16.9 15.4 %all-to-all-done = bf16[64,4,8,128]{3,2,1,0:T(8,128)(2,1)S(1)} async-done(((bf16[64,4,8,128]{3,2,1,0:T(8,128)(2,1)}), bf16[64,4,8,128]{3,2,1,0:T(8,128)(2,1)S(1)}, u32[]{:S(2)}, u32[]{:S(2)}) %all-to-all-start) | async-done | bytes 524320 | tf_op jit(solution)/shard_map/all_to_all | solution.py:305
  32.3 3.6 %shard_map.84 = (bf16[2,256,256]{2,1,0:T(8,128)(2,1)S(1)}, bf16[1,144,256]{2,1,0:T(8,128)(2,1)S(1)}, bf16[2,144,256]{2,1,0:T(8,128)(2,1)S(1)}, bf16[256,1024]{1,...) custom-call(bf16[256,8,128]{2,1,0:T(8,128)(2,1)S(1)} %bitcast.8, ...), custom_call_target="tpu_custom_call" | custom-call | tf_op jit(solution)/shard_map/pallas_call | solution.py:321
  35.9 0.3 collective-permute-start.1
  36.2 3.3 %shard_map.85 = (f32[256,1024]{1,0:T(8,128)S(1)}, bf16[2,256,256]{2,1,0:T(8,128)(2,1)S(1)}, bf16[2,144,256]{2,1,0:T(8,128)(2,1)S(1)}) custom-call(bf16[256,1024]{1,0:T(8,128)(2,1)S(1)} %get-tuple-element.20.x_ref, f32[256,1024]{1,0:T(8,128)S(1)} %get-tuple-element.21.pert_ref, f32[8,128]{1,0:T(8,128)S(1)} %get-tuple-element.22.centre_ref, ...), custom_call_target="tpu_custom_call" | custom-call | tf_op jit(solution)/shard_map/pallas_call | solution.py:337
  39.6 1.3 %collective-permute-start = (bf16[2,144,256]{2,1,0:T(8,128)(2,1)S(1)}, bf16[2,144,256]{2,1,0:T(8,128)(2,1)S(1)}, u32[]{:S(2)}, u32[]{:S(2)}) collective-permute-start(bf16[2,144,256]{2,1,0:T(8,128)(2,1)S(1)} %get-tuple-element.27), channel_id=1, source_target_pairs={{1,0},{2,1},{3,2},{5,4},{6,5},{7,6},{9,8},{10,9},{11,10},{13,12},{... | collective-permute-start | bytes 442376 | tf_op jit(solution)/shard_map/ppermute | solution.py:340
  40.9 1.3 %collective-permute-start.2 = (bf16[1,144,256]{2,1,0:T(8,128)(2,1)S(1)}, bf16[1,144,256]{2,1,0:T(8,128)(2,1)S(1)}, u32[]{:S(2)}, u32[]{:S(2)}) collective-permute-start(bf16[1,144,256]{2,1,0:T(8,128)(2,1)S(1)} %get-tuple-element.24.corner_ref), channel_id=1, source_target_pairs={{5,0},{6,1},{7,2},{9,4},{10,5},{11,6},{13,8},{14,9},{15,10},{17,12... | collective-permute-start | bytes 221192 | tf_op jit(solution)/shard_map/ppermute | solution.py:335
  42.2 6.3 %collective-permute-done.2.diagonal_ref = bf16[1,144,256]{2,1,0:T(8,128)(2,1)S(1)} collective-permute-done((bf16[1,144,256]{2,1,0:T(8,128)(2,1)S(1)}, bf16[1,144,256]{2,1,0:T(8,128)(2,1)S(1)}, u32[]{:S(2)}, u32[]{:S(2)}) %collective-permute-start.2) | collective-permute-done | bytes 73760 | tf_op jit(solution)/shard_map/ppermute | solution.py:335
  48.5 0.0 collective-permute-done.1.below_ref
  48.5 1.0 %shard_map.86.partial_ref = f32[256,1024]{1,0:T(8,128)S(1)} custom-call(bf16[2,144,256]{2,1,0:T(8,128)(2,1)S(1)} %collective-permute-done.1.below_ref, bf16[1,144,256]{2,1,0:T(8,128)(2,1)S(1)} %collective-permute-done.2.diagonal_ref, bf16[2,256,256]{2,1,0:T(8,128)(2,1)S(1)} %get-tuple-element.29.two_ref, bf16[256,1024]{1,0:T(8,128)(2,1)S(1)} %get-tuple-element.25.high_ref, ...), custom_call_target="tpu_custom_call" | custom-call | tf_op jit(solution)/shard_map/pallas_call | solution.py:341
  49.5 0.0 collective-permute-done.beside_ref
  49.5 0.6 shard_map.87
  50.1 24.5 %all_to_all.10.source_ref = bf16[64,4,8,128]{3,2,1,0:T(8,128)(2,1)S(1)} all-to-all(bf16[64,4,8,128]{3,2,1,0:T(8,128)(2,1)S(1)} %bitcast.9), channel_id=1, replica_groups=mesh['mem'=64,'reg'=4] {'mem'}, dimensions={0} | all-to-all | bytes 1048576 | tf_op jit(solution)/shard_map/all_to_all | solution.py:350
  74.6 0.8 %shard_map.88 = bf16[4,64,8,128]{3,2,1,0:T(8,128)(2,1)} custom-call(bf16[64,4,8,128]{3,2,1,0:T(8,128)(2,1)S(1)} %all_to_all.10.source_ref), custom_call_target="tpu_custom_call" | custom-call | tf_op jit(solution)/shard_map/pallas_call | solution.py:351
Async XLA Ops:
  1.8 13.2 %copy-start.5 = (s32[1,8,4]{1,2,0:T(4,128)S(1)}, s32[1,8,4]{1,2,0:T(4,128)}, u32[]{:S(2)}) copy-start(s32[1,8,4]{1,2,0:T(4,128)} %param.14) | copy-start | bytes 388
  1.8 13.3 %copy-start.6 = (f32[1,8,4]{1,2,0:T(4,128)S(1)}, f32[1,8,4]{1,2,0:T(4,128)}, u32[]{:S(2)}) copy-start(f32[1,8,4]{1,2,0:T(4,128)} %param.15) | copy-start | bytes 388
  1.8 13.4 %copy-start.1 = (f32[2,2,512]{2,1,0:T(2,128)S(1)}, f32[2,2,512]{2,1,0:T(2,128)}, u32[]{:S(2)}) copy-start(f32[2,2,512]{2,1,0:T(2,128)} %error_ref.1) | copy-start | bytes 24580
  1.9 13.3 %copy-start.2 = (s32[2,2,512]{2,1,0:T(2,128)S(1)}, s32[2,2,512]{2,1,0:T(2,128)}, u32[]{:S(2)}) copy-start(s32[2,2,512]{2,1,0:T(2,128)} %patch_ref.1) | copy-start | bytes 24580
  1.9 13.3 %copy-start.3 = (s32[2,2,512]{2,1,0:T(2,128)S(1)}, s32[2,2,512]{2,1,0:T(2,128)}, u32[]{:S(2)}) copy-start(s32[2,2,512]{2,1,0:T(2,128)} %var_ref.1) | copy-start | bytes 24580
  1.9 30.4 %all-to-all-start = ((bf16[64,4,8,128]{3,2,1,0:T(8,128)(2,1)}), bf16[64,4,8,128]{3,2,1,0:T(8,128)(2,1)S(1)}, u32[]{:S(2)}, u32[]{:S(2)}) async-start(bf16[64,4,8,128]{3,2,1,0:T(8,128)(2,1)} %shard_map.82), calls=%async_computation | async-start | bytes 1048576 | tf_op jit(solution)/shard_map/all_to_all | solution.py:305
  15.0 0.7 copy-start
  15.1 0.7 copy-start.4
  35.9 12.6 %collective-permute-start.1 = (bf16[2,144,256]{2,1,0:T(8,128)(2,1)S(1)}, bf16[2,144,256]{2,1,0:T(8,128)(2,1)S(1)}, u32[]{:S(2)}, u32[]{:S(2)}) collective-permute-start(bf16[2,144,256]{2,1,0:T(8,128)(2,1)S(1)} %get-tuple-element.28), channel_id=1, source_target_pairs={{4,0},{8,4},{12,8},{16,12},{20,16},{24,20},{28,24},{32,28},{36,32}... | collective-permute-start | bytes 442376 | tf_op jit(solution)/shard_map/ppermute | solution.py:336
  39.6 9.9 %collective-permute-start = (bf16[2,144,256]{2,1,0:T(8,128)(2,1)S(1)}, bf16[2,144,256]{2,1,0:T(8,128)(2,1)S(1)}, u32[]{:S(2)}, u32[]{:S(2)}) collective-permute-start(bf16[2,144,256]{2,1,0:T(8,128)(2,1)S(1)} %get-tuple-element.27), channel_id=1, source_target_pairs={{1,0},{2,1},{3,2},{5,4},{6,5},{7,6},{9,8},{10,9},{11,10},{13,12},{... | collective-permute-start | bytes 442376 | tf_op jit(solution)/shard_map/ppermute | solution.py:340
  40.9 7.6 %collective-permute-start.2 = (bf16[1,144,256]{2,1,0:T(8,128)(2,1)S(1)}, bf16[1,144,256]{2,1,0:T(8,128)(2,1)S(1)}, u32[]{:S(2)}, u32[]{:S(2)}) collective-permute-start(bf16[1,144,256]{2,1,0:T(8,128)(2,1)S(1)} %get-tuple-element.24.corner_ref), channel_id=1, source_target_pairs={{5,0},{6,1},{7,2},{9,4},{10,5},{11,6},{13,8},{14,9},{15,10},{17,12... | collective-permute-start | bytes 221192 | tf_op jit(solution)/shard_map/ppermute | solution.py:335

commit v9 on v7

--- a/solution.py
+++ b/solution.py
@@ -35,7 +35,7 @@
     return dot(a[0], b[0]) + (dot(a[0], b[1]) + dot(a[1], b[0]))
 
 
-def prepare_kernel(count_ref, value_ref, error_ref, patch_ref, var_ref, corner_ref, coeff_ref, dense_ref, value_out_ref, mix_ref):
+def prepare(count_ref, value_ref, error_ref, patch_ref, var_ref, corner_ref, coeff_ref, dense_ref, value_out_ref, mix_ref):
     rows, cols, slots = value_ref.shape
     patches, fields = dense_ref.shape[1:]
     slot_index = lax.broadcasted_iota(jnp.int32, (1, slots), 1)
@@ -43,7 +43,7 @@
     patch_index = lax.broadcasted_iota(jnp.int32, (patches, slots), 0)
     for a in range(rows):
         for b in range(cols):
-            weight = jnp.where(slot_index < count_ref[a, b], 1.0 / error_ref[a, b : b + 1, :], 0.0)
+            weight = jnp.where(slot_index < count_ref[a : a + 1, b : b + 1], 1.0 / error_ref[a, b : b + 1, :], 0.0)
             weighted = weight * value_ref[a, b : b + 1, :]
             chosen = (field_index == var_ref[a, b : b + 1, :]).astype(F32).astype(BF16)
             at_patch = patch_index == patch_ref[a, b : b + 1, :]
@@ -53,20 +53,22 @@
             dense_ref[a * cols + b] = sums[:patches]
             value_out_ref[a * cols + b] = sums[patches:]
     corners, coeffs = corner_ref[...], coeff_ref[...]
+    square = (patches, patches)
+    own_place = lax.broadcasted_iota(jnp.int32, square, 0) == lax.broadcasted_iota(jnp.int32, square, 1)
     for t in range(mix_ref.shape[0]):
-        used = jnp.sum(jnp.where(corners == t, coeffs, 0.0), axis=1, keepdims=True)
-        mix_ref[t] = jnp.broadcast_to(used, (patches, fields))
+        used = jnp.sum(jnp.where(corners == t, coeffs, 0.0), axis=0, keepdims=True)
+        column = jnp.sum(jnp.where(own_place, used, 0.0), axis=1, keepdims=True)
+        mix_ref[t] = jnp.broadcast_to(column, (patches, fields))
 
 
 def shares(points, pert_ref, centre, dense_ref, value_ref, left_high, left_low):
     members = pert_ref.shape[0]
     patches, fields = centre.shape
     pulls = [value_ref[n] - dense_ref[n] * centre for n in points]
-    for p in range(patches):
-        lanes = slice(p * fields, (p + 1) * fields)
-        pert = pert_ref[:, lanes]
-        for slot, n in enumerate(points):
-            left_high[slot, :members, lanes], left_low[slot, :members, lanes] = split(pert * dense_ref[n, p : p + 1, :])
+    for slot, n in enumerate(points):
+        for p in range(patches):
+            lanes = slice(p * fields, (p + 1) * fields)
+            left_high[slot, :members, lanes], left_low[slot, :members, lanes] = split(pert_ref[:, lanes] * dense_ref[n, p : p + 1, :])
             tail = jnp.broadcast_to(pulls[slot][p : p + 1, :], (left_high.shape[1] - members, fields))
             left_high[slot, members:, lanes], left_low[slot, members:, lanes] = split(tail)
 
@@ -247,14 +249,20 @@
         out_ref[k : k + chunk] = part.reshape(chunk, patches, fields).astype(BF16)
 
 
-def outgoing_kernel(source_ref, target_ref, held_ref, turned_ref, read, written):
+def entry_kernel(*refs):
+    small, source_ref, target_ref, results = refs[:7], refs[7], refs[8], refs[9:12]
+    copied, held_ref, turned_ref, loaded, read, written = refs[12:19], refs[19], refs[20], refs[21], refs[22], refs[23]
     own, devices = source_ref.shape[:2]
     half = devices // 2
     spans = [slice(h * half, (h + 1) * half) for h in range(2)]
+    fetch = [pltpu.make_async_copy(a, b, loaded.at[i]) for i, (a, b) in enumerate(zip(small, copied))]
     inward = [pltpu.make_async_copy(source_ref.at[:, s], held_ref.at[:, s], read.at[h]) for h, s in enumerate(spans)]
     outward = [pltpu.make_async_copy(turned_ref.at[s], target_ref.at[s], written.at[h]) for h, s in enumerate(spans)]
-    for copy in inward:
+    for copy in fetch + inward:
         copy.start()
+    for copy in fetch:
+        copy.wait()
+    prepare(*copied, *results)
     for copy, out, s in zip(inward, outward, spans):
         copy.wait()
         for m in range(own):
@@ -279,7 +287,7 @@
         in_specs=specs,
         out_specs=jax.tree.map(lambda _: to, outs),
         scratch_shapes=list(scratch),
-        compiler_params=pltpu.CompilerParams(vmem_limit_bytes=48 << 20),
+        compiler_params=pltpu.CompilerParams(vmem_limit_bytes=32 << 20),
     )
 
 
@@ -295,19 +303,21 @@
     copies = [pltpu.SemaphoreType.DMA((own,))]
 
     blocks = (devices, own, patches, fields)
-    outgoing = call(
-        outgoing_kernel,
-        shape(blocks, BF16),
-        [HBM],
-        [pltpu.VMEM((own,) + (devices,) + blocks[2:], BF16), pltpu.VMEM(blocks, BF16)] + [pltpu.SemaphoreType.DMA((2,))] * 2,
-        HBM,
-    )(pltpu.with_memory_space_constraint(background.reshape(own, devices, patches, fields), pltpu.HBM))
+    small = (obs_count, obs_value, obs_error, obs_patch, obs_variable, patch_corners[0].T, interp_weights[0].T)
+    given = [pltpu.with_memory_space_constraint(x, pltpu.HBM) for x in small + (background.reshape(own, devices, patches, fields),)]
+    sums = (points, patches, fields)
+    outgoing, dense, values, mix = pl.pallas_call(
+        entry_kernel,
+        out_shape=(shape(blocks, BF16), shape(sums, F32), shape(sums, F32), shape((9, patches, fields), F32)),
+        in_specs=[HBM] * 8,
+        out_specs=(HBM, VMEM, VMEM, VMEM),
+        scratch_shapes=[pltpu.VMEM(x.shape, x.dtype) for x in small]
+        + [pltpu.VMEM((own, devices) + blocks[2:], BF16), pltpu.VMEM(blocks, BF16)]
+        + [pltpu.SemaphoreType.DMA((len(small),))]
+        + [pltpu.SemaphoreType.DMA((2,))] * 2,
+        compiler_params=pltpu.CompilerParams(vmem_limit_bytes=32 << 20),
+    )(*given)
     ensemble = lax.all_to_all(outgoing, "mem", split_axis=0, concat_axis=0, tiled=True).reshape(members, patches, fields)
-    dense, values, mix = call(
-        prepare_kernel,
-        (shape((points, patches, fields), F32), shape((points, patches, fields), F32), shape((9, patches, fields), F32)),
-        [SMEM] + [VMEM] * 6,
-    )(obs_count, obs_value, obs_error, obs_patch, obs_variable, patch_corners[0], interp_weights[0])
 
     packed = (members // 2 + 16, members)
     left = (members + 16, columns)

time: 72.4 us -> 71.7 us (level)
  blocking collectives: 24.7 us -> 54.7 us
  waiting for transfers between devices: 17.7 us -> 2.25 us
  starting transfers between devices: 16 us -> 2.87 us
  Pallas kernels: 12.4 us -> 11.2 us
  local copies, waits for them, and re-layouts: 0.79 us -> 0 us
    all_to_all x0 -> x1, blocking collectives: none -> 30.1 us  [per_device(): lax.all_to_all(outgoing, 'mem', split_axis=0, concat_axis=0, tiled=True)]
    all_to_all x1 -> x0, waiting for transfers between devices: 15.4 us -> none  [per_device(): lax.all_to_all(outgoing, 'mem', split_axis=0, concat_axis=0, tiled=True)]
    all_to_all x1 -> x0, starting transfers between devices: 13.1 us -> none  [per_device(): lax.all_to_all(outgoing, 'mem', split_axis=0, concat_axis=0, tiled=True)]
    pallas_call x2 -> x1, Pallas kernels: 2.88 us -> 1.67 us  [per_device(): pl.pallas_call(entry_kernel, out_shape=(shape(blocks, BF16), shape(sums,...]
  transfers between devices with their start and end apart: 4 -> 3, of which waited for: 3 -> 2; matrix products, arithmetic and copies ran while one was open for 0% -> 0% of each run, Pallas kernels for 7% -> 5%
where the time goes in v9:
time: 71.7 us; the launch traced here: 71.1 us
  blocking collectives  54.7 us (76%)
  Pallas kernels  11.2 us (16%)
  starting transfers between devices  2.87 us (4%)
  waiting for transfers between devices  2.25 us (3%)
    all_to_all x1, blocking collectives, per_device(): lax.all_to_all(outgoing, 'mem', split_axis=0, concat_axis=0, tiled=True)  30.1 us
    all_to_all x1, blocking collectives, per_device(): lax.all_to_all(analysis.reshape(devices, own, patches, fields), 'mem', sp...  24.7 us
    pallas_call x1, Pallas kernels, per_device(): call(first_kernel, (shape((3, members, members), BF16), shape((2,) + pack...  4.43 us
    pallas_call x1, Pallas kernels, per_device(): call(second_kernel, (shape(flat, F32), shape((1, members, members), BF16)...  2.83 us
    pallas_call x1, Pallas kernels, per_device(): pl.pallas_call(entry_kernel, out_shape=(shape(blocks, BF16), shape(sums,...  1.67 us
  transfers between devices with their start and end apart: 3, of which 2 were waited for; matrix products, arithmetic and copies ran while one was open for 0% of the time, Pallas kernels for 5%

profile of v9, /device:TPU:1, one launch (start us, length us, event | category | flops | bytes accessed | tf_op | source)
XLA Modules:
  0.0 71.1 jit_solution(14470198157508502797)
XLA Ops:
  0.0 1.7 %shard_map.82 = (bf16[64,4,8,128]{3,2,1,0:T(8,128)(2,1)S(1)}, f32[4,8,128]{2,1,0:T(8,128)S(1)}, f32[4,8,128]{2,1,0:T(8,128)S(1)}, f32[9,8,128]{2,1,0:T(8,128)S(1)}) custom-call(s32[2,2]{1,0:T(2,128)} %refs_0_.1, f32[2,2,512]{2,1,0:T(2,128)} %refs_1_.1, f32[2,2,512]{2,1,0:T(2,128)} %refs_2_.1, s32[2,2,512]{2,1,0:T(2,128)} %refs_3_.1, s32[2,2,512]{2,1,0:T(2,128)} %refs_4_.1, ...), custom_call_target="tpu_custom_call" | custom-call | tf_op jit(solution)/shard_map/pallas_call | solution.py:309
  1.7 30.1 %all_to_all.10 = bf16[64,4,8,128]{3,2,1,0:T(8,128)(2,1)S(1)} all-to-all(bf16[64,4,8,128]{3,2,1,0:T(8,128)(2,1)S(1)} %get-tuple-element.19), channel_id=1, replica_groups=mesh['mem'=64,'reg'=4] {'mem'}, dimensions={0} | all-to-all | bytes 1048576 | tf_op jit(solution)/shard_map/all_to_all | solution.py:320
  31.7 4.4 %shard_map.83 = (bf16[3,256,256]{2,1,0:T(8,128)(2,1)S(1)}, bf16[2,144,256]{2,1,0:T(8,128)(2,1)S(1)}, bf16[1,144,256]{2,1,0:T(8,128)(2,1)S(1)}, bf16[2,144,256]{2...) custom-call(bf16[256,8,128]{2,1,0:T(8,128)(2,1)S(1)} %bitcast.12, ...), custom_call_target="tpu_custom_call" | custom-call | tf_op jit(solution)/shard_map/pallas_call | solution.py:329
  36.2 1.3 %collective-permute-start.1 = (bf16[2,144,256]{2,1,0:T(8,128)(2,1)S(1)}, bf16[2,144,256]{2,1,0:T(8,128)(2,1)S(1)}, u32[]{:S(2)}, u32[]{:S(2)}) collective-permute-start(bf16[2,144,256]{2,1,0:T(8,128)(2,1)S(1)} %get-tuple-element.25), channel_id=1, source_target_pairs={{1,0},{2,1},{3,2},{5,4},{6,5},{7,6},{9,8},{10,9},{11,10},{13,12},{... | collective-permute-start | bytes 442376 | tf_op jit(solution)/shard_map/ppermute | solution.py:344
  37.5 0.3 collective-permute-start.2
  37.8 1.3 %collective-permute-start = (bf16[1,144,256]{2,1,0:T(8,128)(2,1)S(1)}, bf16[1,144,256]{2,1,0:T(8,128)(2,1)S(1)}, u32[]{:S(2)}, u32[]{:S(2)}) collective-permute-start(bf16[1,144,256]{2,1,0:T(8,128)(2,1)S(1)} %get-tuple-element.22), channel_id=1, source_target_pairs={{5,0},{6,1},{7,2},{9,4},{10,5},{11,6},{13,8},{14,9},{15,10},{17,12... | collective-permute-start | bytes 221192 | tf_op jit(solution)/shard_map/ppermute | solution.py:345
  39.1 2.8 %shard_map.84 = (f32[256,1024]{1,0:T(8,128)S(1)}, bf16[1,256,256]{2,1,0:T(8,128)(2,1)S(1)}) custom-call(bf16[256,1024]{1,0:T(8,128)(2,1)S(1)} %get-tuple-element.27.x_ref, f32[256,1024]{1,0:T(8,128)S(1)} %get-tuple-element.28.pert_ref, f32[8,128]{1,0:T(8,128)S(1)} %get-tuple-element.29.centre_ref, f32[4,8,128]{2,1,0:T(8,128)S(1)} %get-tuple-element.20.dense_ref, ...), custom_call_target="tpu_custom_call" | custom-call | tf_op jit(solution)/shard_map/pallas_call | solution.py:347
  41.9 1.4 %collective-permute-done.1.beside_ref = bf16[2,144,256]{2,1,0:T(8,128)(2,1)S(1)} collective-permute-done((bf16[2,144,256]{2,1,0:T(8,128)(2,1)S(1)}, bf16[2,144,256]{2,1,0:T(8,128)(2,1)S(1)}, u32[]{:S(2)}, u32[]{:S(2)}) %collective-permute-start.1) | collective-permute-done | bytes 147488 | tf_op jit(solution)/shard_map/ppermute | solution.py:344
  43.3 0.0 collective-permute-done.2.below_ref
  43.3 1.0 %shard_map.85.partial_ref = f32[256,1024]{1,0:T(8,128)S(1)} custom-call(bf16[2,144,256]{2,1,0:T(8,128)(2,1)S(1)} %collective-permute-done.1.beside_ref, bf16[2,144,256]{2,1,0:T(8,128)(2,1)S(1)} %collective-permute-done.2.below_ref, bf16[1,256,256]{2,1,0:T(8,128)(2,1)S(1)} %get-tuple-element.31.two_ref, bf16[256,1024]{1,0:T(8,128)(2,1)S(1)} %get-tuple-element.23.high_ref, ...), custom_call_target="tpu_custom_call" | custom-call | tf_op jit(solution)/shard_map/pallas_call | solution.py:353
  44.2 0.9 %collective-permute-done.diagonal_ref = bf16[1,144,256]{2,1,0:T(8,128)(2,1)S(1)} collective-permute-done((bf16[1,144,256]{2,1,0:T(8,128)(2,1)S(1)}, bf16[1,144,256]{2,1,0:T(8,128)(2,1)S(1)}, u32[]{:S(2)}, u32[]{:S(2)}) %collective-permute-start) | collective-permute-done | bytes 73760 | tf_op jit(solution)/shard_map/ppermute | solution.py:345
  45.1 0.5 shard_map.86
  45.6 24.7 %all_to_all.11.source_ref = bf16[64,4,8,128]{3,2,1,0:T(8,128)(2,1)S(1)} all-to-all(bf16[64,4,8,128]{3,2,1,0:T(8,128)(2,1)S(1)} %bitcast.13), channel_id=1, replica_groups=mesh['mem'=64,'reg'=4] {'mem'}, dimensions={0} | all-to-all | bytes 1048576 | tf_op jit(solution)/shard_map/all_to_all | solution.py:362
  70.3 0.8 %shard_map.87 = bf16[4,64,8,128]{3,2,1,0:T(8,128)(2,1)} custom-call(bf16[64,4,8,128]{3,2,1,0:T(8,128)(2,1)S(1)} %all_to_all.11.source_ref), custom_call_target="tpu_custom_call" | custom-call | tf_op jit(solution)/shard_map/pallas_call | solution.py:363
Async XLA Ops:
  36.2 7.1 %collective-permute-start.1 = (bf16[2,144,256]{2,1,0:T(8,128)(2,1)S(1)}, bf16[2,144,256]{2,1,0:T(8,128)(2,1)S(1)}, u32[]{:S(2)}, u32[]{:S(2)}) collective-permute-start(bf16[2,144,256]{2,1,0:T(8,128)(2,1)S(1)} %get-tuple-element.25), channel_id=1, source_target_pairs={{1,0},{2,1},{3,2},{5,4},{6,5},{7,6},{9,8},{10,9},{11,10},{13,12},{... | collective-permute-start | bytes 442376 | tf_op jit(solution)/shard_map/ppermute | solution.py:344
  37.5 5.8 %collective-permute-start.2 = (bf16[2,144,256]{2,1,0:T(8,128)(2,1)S(1)}, bf16[2,144,256]{2,1,0:T(8,128)(2,1)S(1)}, u32[]{:S(2)}, u32[]{:S(2)}) collective-permute-start(bf16[2,144,256]{2,1,0:T(8,128)(2,1)S(1)} %get-tuple-element.26), channel_id=1, source_target_pairs={{4,0},{8,4},{12,8},{16,12},{20,16},{24,20},{28,24},{32,28},{36,32}... | collective-permute-start | bytes 442376 | tf_op jit(solution)/shard_map/ppermute | solution.py:346
  37.8 7.4 %collective-permute-start = (bf16[1,144,256]{2,1,0:T(8,128)(2,1)S(1)}, bf16[1,144,256]{2,1,0:T(8,128)(2,1)S(1)}, u32[]{:S(2)}, u32[]{:S(2)}) collective-permute-start(bf16[1,144,256]{2,1,0:T(8,128)(2,1)S(1)} %get-tuple-element.22), channel_id=1, source_target_pairs={{5,0},{6,1},{7,2},{9,4},{10,5},{11,6},{13,8},{14,9},{15,10},{17,12... | collective-permute-start | bytes 221192 | tf_op jit(solution)/shard_map/ppermute | solution.py:345

commit v10 on v9

--- a/solution.py
+++ b/solution.py
@@ -9,7 +9,6 @@
 F32 = jnp.float32
 BF16 = jnp.bfloat16
 VMEM = pl.BlockSpec(memory_space=pltpu.VMEM)
-SMEM = pl.BlockSpec(memory_space=pltpu.SMEM)
 HBM = pl.BlockSpec(memory_space=pltpu.HBM)
 NN = (((1,), (0,)), ((), ()))
 NT = (((1,), (1,)), ((), ()))
@@ -251,25 +250,16 @@
 
 def entry_kernel(*refs):
     small, source_ref, target_ref, results = refs[:7], refs[7], refs[8], refs[9:12]
-    copied, held_ref, turned_ref, loaded, read, written = refs[12:19], refs[19], refs[20], refs[21], refs[22], refs[23]
-    own, devices = source_ref.shape[:2]
-    half = devices // 2
-    spans = [slice(h * half, (h + 1) * half) for h in range(2)]
+    copied, loaded, read = refs[12:19], refs[19], refs[20]
     fetch = [pltpu.make_async_copy(a, b, loaded.at[i]) for i, (a, b) in enumerate(zip(small, copied))]
-    inward = [pltpu.make_async_copy(source_ref.at[:, s], held_ref.at[:, s], read.at[h]) for h, s in enumerate(spans)]
-    outward = [pltpu.make_async_copy(turned_ref.at[s], target_ref.at[s], written.at[h]) for h, s in enumerate(spans)]
+    inward = [pltpu.make_async_copy(source_ref.at[m], target_ref.at[:, m], read.at[m]) for m in range(source_ref.shape[0])]
     for copy in fetch + inward:
         copy.start()
     for copy in fetch:
         copy.wait()
     prepare(*copied, *results)
-    for copy, out, s in zip(inward, outward, spans):
+    for copy in inward:
         copy.wait()
-        for m in range(own):
-            turned_ref[s, m] = held_ref[m, s]
-        out.start()
-    for out in outward:
-        out.wait()
 
 
 def returned_kernel(source_ref, target_ref, done):
@@ -310,11 +300,9 @@
         entry_kernel,
         out_shape=(shape(blocks, BF16), shape(sums, F32), shape(sums, F32), shape((9, patches, fields), F32)),
         in_specs=[HBM] * 8,
-        out_specs=(HBM, VMEM, VMEM, VMEM),
+        out_specs=(VMEM, VMEM, VMEM, VMEM),
         scratch_shapes=[pltpu.VMEM(x.shape, x.dtype) for x in small]
-        + [pltpu.VMEM((own, devices) + blocks[2:], BF16), pltpu.VMEM(blocks, BF16)]
-        + [pltpu.SemaphoreType.DMA((len(small),))]
-        + [pltpu.SemaphoreType.DMA((2,))] * 2,
+        + [pltpu.SemaphoreType.DMA((len(small),)), pltpu.SemaphoreType.DMA((own,))],
         compiler_params=pltpu.CompilerParams(vmem_limit_bytes=32 << 20),
     )(*given)
     ensemble = lax.all_to_all(outgoing, "mem", split_axis=0, concat_axis=0, tiled=True).reshape(members, patches, fields)

time: 71.7 us -> 71.7 us (level)
  no operation moved by 1% of the time
where the time goes in v10:
time: 71.7 us; the launch traced here: 71.1 us
  blocking collectives  54.7 us (76%)
  Pallas kernels  11.2 us (16%)
  starting transfers between devices  2.87 us (4%)
  waiting for transfers between devices  2.25 us (3%)
    all_to_all x1, blocking collectives, per_device(): lax.all_to_all(outgoing, 'mem', split_axis=0, concat_axis=0, tiled=True)  30.1 us
    all_to_all x1, blocking collectives, per_device(): lax.all_to_all(analysis.reshape(devices, own, patches, fields), 'mem', sp...  24.7 us
    pallas_call x1, Pallas kernels, per_device(): call(first_kernel, (shape((3, members, members), BF16), shape((2,) + pack...  4.43 us
    pallas_call x1, Pallas kernels, per_device(): call(second_kernel, (shape(flat, F32), shape((1, members, members), BF16)...  2.83 us
    pallas_call x1, Pallas kernels, per_device(): pl.pallas_call(entry_kernel, out_shape=(shape(blocks, BF16), shape(sums,...  1.65 us
  transfers between devices with their start and end apart: 3, of which 2 were waited for; matrix products, arithmetic and copies ran while one was open for 0% of the time, Pallas kernels for 5%

profile of v10, /device:TPU:1, one launch (start us, length us, event | category | flops | bytes accessed | tf_op | source)
XLA Modules:
  0.0 71.1 jit_solution(10165516909211461121)
XLA Ops:
  0.0 1.7 %shard_map.82 = (bf16[64,4,8,128]{3,2,1,0:T(8,128)(2,1)S(1)}, f32[4,8,128]{2,1,0:T(8,128)S(1)}, f32[4,8,128]{2,1,0:T(8,128)S(1)}, f32[9,8,128]{2,1,0:T(8,128)S(1)}) custom-call(s32[2,2]{1,0:T(2,128)} %refs_0_.1, f32[2,2,512]{2,1,0:T(2,128)} %refs_1_.1, f32[2,2,512]{2,1,0:T(2,128)} %refs_2_.1, s32[2,2,512]{2,1,0:T(2,128)} %refs_3_.1, s32[2,2,512]{2,1,0:T(2,128)} %refs_4_.1, ...), custom_call_target="tpu_custom_call" | custom-call | tf_op jit(solution)/shard_map/pallas_call | solution.py:299
  1.7 30.1 %all_to_all.10 = bf16[64,4,8,128]{3,2,1,0:T(8,128)(2,1)S(1)} all-to-all(bf16[64,4,8,128]{3,2,1,0:T(8,128)(2,1)S(1)} %get-tuple-element.19), channel_id=1, replica_groups=mesh['mem'=64,'reg'=4] {'mem'}, dimensions={0} | all-to-all | bytes 1048576 | tf_op jit(solution)/shard_map/all_to_all | solution.py:308
  31.7 4.4 %shard_map.83 = (bf16[3,256,256]{2,1,0:T(8,128)(2,1)S(1)}, bf16[2,144,256]{2,1,0:T(8,128)(2,1)S(1)}, bf16[1,144,256]{2,1,0:T(8,128)(2,1)S(1)}, bf16[2,144,256]{2...) custom-call(bf16[256,8,128]{2,1,0:T(8,128)(2,1)S(1)} %bitcast.12, ...), custom_call_target="tpu_custom_call" | custom-call | tf_op jit(solution)/shard_map/pallas_call | solution.py:317
  36.2 1.3 %collective-permute-start.1 = (bf16[2,144,256]{2,1,0:T(8,128)(2,1)S(1)}, bf16[2,144,256]{2,1,0:T(8,128)(2,1)S(1)}, u32[]{:S(2)}, u32[]{:S(2)}) collective-permute-start(bf16[2,144,256]{2,1,0:T(8,128)(2,1)S(1)} %get-tuple-element.25), channel_id=1, source_target_pairs={{1,0},{2,1},{3,2},{5,4},{6,5},{7,6},{9,8},{10,9},{11,10},{13,12},{... | collective-permute-start | bytes 442376 | tf_op jit(solution)/shard_map/ppermute | solution.py:332
  37.5 0.3 collective-permute-start.2
  37.8 1.3 %collective-permute-start = (bf16[1,144,256]{2,1,0:T(8,128)(2,1)S(1)}, bf16[1,144,256]{2,1,0:T(8,128)(2,1)S(1)}, u32[]{:S(2)}, u32[]{:S(2)}) collective-permute-start(bf16[1,144,256]{2,1,0:T(8,128)(2,1)S(1)} %get-tuple-element.22), channel_id=1, source_target_pairs={{5,0},{6,1},{7,2},{9,4},{10,5},{11,6},{13,8},{14,9},{15,10},{17,12... | collective-permute-start | bytes 221192 | tf_op jit(solution)/shard_map/ppermute | solution.py:333
  39.0 2.8 %shard_map.84 = (f32[256,1024]{1,0:T(8,128)S(1)}, bf16[1,256,256]{2,1,0:T(8,128)(2,1)S(1)}) custom-call(bf16[256,1024]{1,0:T(8,128)(2,1)S(1)} %get-tuple-element.27.x_ref, f32[256,1024]{1,0:T(8,128)S(1)} %get-tuple-element.28.pert_ref, f32[8,128]{1,0:T(8,128)S(1)} %get-tuple-element.29.centre_ref, f32[4,8,128]{2,1,0:T(8,128)S(1)} %get-tuple-element.20.dense_ref, ...), custom_call_target="tpu_custom_call" | custom-call | tf_op jit(solution)/shard_map/pallas_call | solution.py:335
  41.9 1.4 %collective-permute-done.1.beside_ref = bf16[2,144,256]{2,1,0:T(8,128)(2,1)S(1)} collective-permute-done((bf16[2,144,256]{2,1,0:T(8,128)(2,1)S(1)}, bf16[2,144,256]{2,1,0:T(8,128)(2,1)S(1)}, u32[]{:S(2)}, u32[]{:S(2)}) %collective-permute-start.1) | collective-permute-done | bytes 147488 | tf_op jit(solution)/shard_map/ppermute | solution.py:332
  43.2 0.0 collective-permute-done.2.below_ref
  43.2 1.0 %shard_map.85.partial_ref = f32[256,1024]{1,0:T(8,128)S(1)} custom-call(bf16[2,144,256]{2,1,0:T(8,128)(2,1)S(1)} %collective-permute-done.1.beside_ref, bf16[2,144,256]{2,1,0:T(8,128)(2,1)S(1)} %collective-permute-done.2.below_ref, bf16[1,256,256]{2,1,0:T(8,128)(2,1)S(1)} %get-tuple-element.31.two_ref, bf16[256,1024]{1,0:T(8,128)(2,1)S(1)} %get-tuple-element.23.high_ref, ...), custom_call_target="tpu_custom_call" | custom-call | tf_op jit(solution)/shard_map/pallas_call | solution.py:341
  44.2 0.9 %collective-permute-done.diagonal_ref = bf16[1,144,256]{2,1,0:T(8,128)(2,1)S(1)} collective-permute-done((bf16[1,144,256]{2,1,0:T(8,128)(2,1)S(1)}, bf16[1,144,256]{2,1,0:T(8,128)(2,1)S(1)}, u32[]{:S(2)}, u32[]{:S(2)}) %collective-permute-start) | collective-permute-done | bytes 73760 | tf_op jit(solution)/shard_map/ppermute | solution.py:333
  45.1 0.5 shard_map.86
  45.6 24.7 %all_to_all.11.source_ref = bf16[64,4,8,128]{3,2,1,0:T(8,128)(2,1)S(1)} all-to-all(bf16[64,4,8,128]{3,2,1,0:T(8,128)(2,1)S(1)} %bitcast.13), channel_id=1, replica_groups=mesh['mem'=64,'reg'=4] {'mem'}, dimensions={0} | all-to-all | bytes 1048576 | tf_op jit(solution)/shard_map/all_to_all | solution.py:350
  70.2 0.8 %shard_map.87 = bf16[4,64,8,128]{3,2,1,0:T(8,128)(2,1)} custom-call(bf16[64,4,8,128]{3,2,1,0:T(8,128)(2,1)S(1)} %all_to_all.11.source_ref), custom_call_target="tpu_custom_call" | custom-call | tf_op jit(solution)/shard_map/pallas_call | solution.py:351
Async XLA Ops:
  36.2 7.1 %collective-permute-start.1 = (bf16[2,144,256]{2,1,0:T(8,128)(2,1)S(1)}, bf16[2,144,256]{2,1,0:T(8,128)(2,1)S(1)}, u32[]{:S(2)}, u32[]{:S(2)}) collective-permute-start(bf16[2,144,256]{2,1,0:T(8,128)(2,1)S(1)} %get-tuple-element.25), channel_id=1, source_target_pairs={{1,0},{2,1},{3,2},{5,4},{6,5},{7,6},{9,8},{10,9},{11,10},{13,12},{... | collective-permute-start | bytes 442376 | tf_op jit(solution)/shard_map/ppermute | solution.py:332
  37.5 5.8 %collective-permute-start.2 = (bf16[2,144,256]{2,1,0:T(8,128)(2,1)S(1)}, bf16[2,144,256]{2,1,0:T(8,128)(2,1)S(1)}, u32[]{:S(2)}, u32[]{:S(2)}) collective-permute-start(bf16[2,144,256]{2,1,0:T(8,128)(2,1)S(1)} %get-tuple-element.26), channel_id=1, source_target_pairs={{4,0},{8,4},{12,8},{16,12},{20,16},{24,20},{28,24},{32,28},{36,32}... | collective-permute-start | bytes 442376 | tf_op jit(solution)/shard_map/ppermute | solution.py:334
  37.8 7.4 %collective-permute-start = (bf16[1,144,256]{2,1,0:T(8,128)(2,1)S(1)}, bf16[1,144,256]{2,1,0:T(8,128)(2,1)S(1)}, u32[]{:S(2)}, u32[]{:S(2)}) collective-permute-start(bf16[1,144,256]{2,1,0:T(8,128)(2,1)S(1)} %get-tuple-element.22), channel_id=1, source_target_pairs={{5,0},{6,1},{7,2},{9,4},{10,5},{11,6},{13,8},{14,9},{15,10},{17,12... | collective-permute-start | bytes 221192 | tf_op jit(solution)/shard_map/ppermute | solution.py:333

commit v11 on v10

--- a/solution.py
+++ b/solution.py
@@ -225,16 +225,16 @@
     return [(t, whole_ref, place) for place, (t, _, _) in enumerate(arrived)]
 
 
-def middle_kernel(beside_ref, below_ref, two_ref, high_ref, mix_ref, partial_ref, out_ref, whole_ref):
-    parts = arrivals(((2, beside_ref, 0), (5, beside_ref, 1), (6, below_ref, 0), (7, below_ref, 1)), whole_ref) + [(4, two_ref, 0)]
+def middle_kernel(beside_ref, two_ref, high_ref, mix_ref, partial_ref, out_ref, whole_ref):
+    parts = arrivals(((2, beside_ref, 0), (5, beside_ref, 1)), whole_ref) + [(4, two_ref, 0)]
     fields = mix_ref.shape[2]
     for p in range(0, mix_ref.shape[1], 2):
         lanes = slice(p * fields, (p + 2) * fields)
         out_ref[:, lanes] = partial_ref[:, lanes] + blend(parts, high_ref, mix_ref, p)
 
 
-def last_kernel(diagonal_ref, high_ref, mix_ref, partial_ref, centre_ref, out_ref, all_ref, whole_ref):
-    parts = arrivals(((8, diagonal_ref, 0),), whole_ref)
+def last_kernel(below_ref, diagonal_ref, high_ref, mix_ref, partial_ref, centre_ref, out_ref, all_ref, whole_ref):
+    parts = arrivals(((6, below_ref, 0), (7, below_ref, 1), (8, diagonal_ref, 0)), whole_ref)
     members, patches, fields = out_ref.shape
     for p in range(0, patches, 2):
         lanes = slice(p * fields, (p + 2) * fields)
@@ -338,15 +338,15 @@
         [VMEM] * 8,
         [pltpu.VMEM((1,) + left, BF16)] * 2,
     )(x, pert, centre, dense, values, one, high, mix)
-    partial = call(middle_kernel, shape(flat, F32), [VMEM] * 6, [pltpu.VMEM((4, members, members), BF16)])(
-        beside, below, two, high, mix, partial
+    partial = call(middle_kernel, shape(flat, F32), [VMEM] * 5, [pltpu.VMEM((2, members, members), BF16)])(
+        beside, two, high, mix, partial
     )
     analysis = call(
         last_kernel,
         shape((members, patches, fields), BF16),
-        [VMEM] * 5,
-        [wide, pltpu.VMEM((1, members, members), BF16)],
-    )(diagonal, high, mix, partial, centre)
+        [VMEM] * 6,
+        [wide, pltpu.VMEM((3, members, members), BF16)],
+    )(below, diagonal, high, mix, partial, centre)
     returned = lax.all_to_all(analysis.reshape(devices, own, patches, fields), "mem", split_axis=0, concat_axis=0, tiled=True)
     result = call(returned_kernel, shape((own, devices, patches, fields), BF16), [VMEM], copies, HBM)(returned)
     return result.reshape(own, 1, all_patches, fields)

time: 71.7 us -> 72 us (level)
  no operation moved by 1% of the time
where the time goes in v11:
time: 72 us; the launch traced here: 71.4 us
  blocking collectives  54.7 us (76%)
  Pallas kernels  11.2 us (16%)
  starting transfers between devices  2.87 us (4%)
  waiting for transfers between devices  2.52 us (4%)
    all_to_all x1, blocking collectives, per_device(): lax.all_to_all(outgoing, 'mem', split_axis=0, concat_axis=0, tiled=True)  30.1 us
    all_to_all x1, blocking collectives, per_device(): lax.all_to_all(analysis.reshape(devices, own, patches, fields), 'mem', sp...  24.7 us
    pallas_call x1, Pallas kernels, per_device(): call(first_kernel, (shape((3, members, members), BF16), shape((2,) + pack...  4.43 us
    pallas_call x1, Pallas kernels, per_device(): call(second_kernel, (shape(flat, F32), shape((1, members, members), BF16)...  2.83 us
    pallas_call x1, Pallas kernels, per_device(): pl.pallas_call(entry_kernel, out_shape=(shape(blocks, BF16), shape(sums,...  1.65 us
  transfers between devices with their start and end apart: 3, of which 2 were waited for; matrix products, arithmetic and copies ran while one was open for 0% of the time, Pallas kernels for 5%

profile of v11, /device:TPU:1, one launch (start us, length us, event | category | flops | bytes accessed | tf_op | source)
XLA Modules:
  0.0 71.4 jit_solution(4353486593366829190)
XLA Ops:
  0.0 1.7 %shard_map.82 = (bf16[64,4,8,128]{3,2,1,0:T(8,128)(2,1)S(1)}, f32[4,8,128]{2,1,0:T(8,128)S(1)}, f32[4,8,128]{2,1,0:T(8,128)S(1)}, f32[9,8,128]{2,1,0:T(8,128)S(1)}) custom-call(s32[2,2]{1,0:T(2,128)} %refs_0_.1, f32[2,2,512]{2,1,0:T(2,128)} %refs_1_.1, f32[2,2,512]{2,1,0:T(2,128)} %refs_2_.1, s32[2,2,512]{2,1,0:T(2,128)} %refs_3_.1, s32[2,2,512]{2,1,0:T(2,128)} %refs_4_.1, ...), custom_call_target="tpu_custom_call" | custom-call | tf_op jit(solution)/shard_map/pallas_call | solution.py:299
  1.7 30.1 %all_to_all.10 = bf16[64,4,8,128]{3,2,1,0:T(8,128)(2,1)S(1)} all-to-all(bf16[64,4,8,128]{3,2,1,0:T(8,128)(2,1)S(1)} %get-tuple-element.19), channel_id=1, replica_groups=mesh['mem'=64,'reg'=4] {'mem'}, dimensions={0} | all-to-all | bytes 1048576 | tf_op jit(solution)/shard_map/all_to_all | solution.py:308
  31.7 4.4 %shard_map.83 = (bf16[3,256,256]{2,1,0:T(8,128)(2,1)S(1)}, bf16[2,144,256]{2,1,0:T(8,128)(2,1)S(1)}, bf16[1,144,256]{2,1,0:T(8,128)(2,1)S(1)}, bf16[2,144,256]{2...) custom-call(bf16[256,8,128]{2,1,0:T(8,128)(2,1)S(1)} %bitcast.12, ...), custom_call_target="tpu_custom_call" | custom-call | tf_op jit(solution)/shard_map/pallas_call | solution.py:317
  36.2 1.3 %collective-permute-start.2 = (bf16[2,144,256]{2,1,0:T(8,128)(2,1)S(1)}, bf16[2,144,256]{2,1,0:T(8,128)(2,1)S(1)}, u32[]{:S(2)}, u32[]{:S(2)}) collective-permute-start(bf16[2,144,256]{2,1,0:T(8,128)(2,1)S(1)} %get-tuple-element.26), channel_id=1, source_target_pairs={{1,0},{2,1},{3,2},{5,4},{6,5},{7,6},{9,8},{10,9},{11,10},{13,12},{... | collective-permute-start | bytes 442376 | tf_op jit(solution)/shard_map/ppermute | solution.py:332
  37.5 0.3 collective-permute-start
  37.8 1.3 %collective-permute-start.1 = (bf16[1,144,256]{2,1,0:T(8,128)(2,1)S(1)}, bf16[1,144,256]{2,1,0:T(8,128)(2,1)S(1)}, u32[]{:S(2)}, u32[]{:S(2)}) collective-permute-start(bf16[1,144,256]{2,1,0:T(8,128)(2,1)S(1)} %get-tuple-element.23), channel_id=1, source_target_pairs={{5,0},{6,1},{7,2},{9,4},{10,5},{11,6},{13,8},{14,9},{15,10},{17,12... | collective-permute-start | bytes 221192 | tf_op jit(solution)/shard_map/ppermute | solution.py:333
  39.0 2.8 %shard_map.84 = (f32[256,1024]{1,0:T(8,128)S(1)}, bf16[1,256,256]{2,1,0:T(8,128)(2,1)S(1)}) custom-call(bf16[256,1024]{1,0:T(8,128)(2,1)S(1)} %get-tuple-element.27.x_ref, f32[256,1024]{1,0:T(8,128)S(1)} %get-tuple-element.28.pert_ref, f32[8,128]{1,0:T(8,128)S(1)} %get-tuple-element.29.centre_ref, f32[4,8,128]{2,1,0:T(8,128)S(1)} %get-tuple-element.20.dense_ref, ...), custom_call_target="tpu_custom_call" | custom-call | tf_op jit(solution)/shard_map/pallas_call | solution.py:335
  41.9 1.4 %collective-permute-done.2.beside_ref = bf16[2,144,256]{2,1,0:T(8,128)(2,1)S(1)} collective-permute-done((bf16[2,144,256]{2,1,0:T(8,128)(2,1)S(1)}, bf16[2,144,256]{2,1,0:T(8,128)(2,1)S(1)}, u32[]{:S(2)}, u32[]{:S(2)}) %collective-permute-start.2) | collective-permute-done | bytes 147488 | tf_op jit(solution)/shard_map/ppermute | solution.py:332
  43.2 0.7 shard_map.85.partial_ref
  44.0 1.1 %collective-permute-done.1.diagonal_ref = bf16[1,144,256]{2,1,0:T(8,128)(2,1)S(1)} collective-permute-done((bf16[1,144,256]{2,1,0:T(8,128)(2,1)S(1)}, bf16[1,144,256]{2,1,0:T(8,128)(2,1)S(1)}, u32[]{:S(2)}, u32[]{:S(2)}) %collective-permute-start.1) | collective-permute-done | bytes 73760 | tf_op jit(solution)/shard_map/ppermute | solution.py:333
  45.1 0.0 collective-permute-done.below_ref
  45.1 0.8 %shard_map.86 = bf16[256,8,128]{2,1,0:T(8,128)(2,1)S(1)} custom-call(bf16[2,144,256]{2,1,0:T(8,128)(2,1)S(1)} %collective-permute-done.below_ref, bf16[1,144,256]{2,1,0:T(8,128)(2,1)S(1)} %collective-permute-done.1.diagonal_ref, bf16[256,1024]{1,0:T(8,128)(2,1)S(1)} %get-tuple-element.24.high_ref, f32[9,8,128]{2,1,0:T(8,128)S(1)} %get-tuple-element.25.mix_ref, ...), custom_call_target="tpu_custom_call" | custom-call | tf_op jit(solution)/shard_map/pallas_call | solution.py:344
  45.9 24.7 %all_to_all.11.source_ref = bf16[64,4,8,128]{3,2,1,0:T(8,128)(2,1)S(1)} all-to-all(bf16[64,4,8,128]{3,2,1,0:T(8,128)(2,1)S(1)} %bitcast.13), channel_id=1, replica_groups=mesh['mem'=64,'reg'=4] {'mem'}, dimensions={0} | all-to-all | bytes 1048576 | tf_op jit(solution)/shard_map/all_to_all | solution.py:350
  70.6 0.8 %shard_map.87 = bf16[4,64,8,128]{3,2,1,0:T(8,128)(2,1)} custom-call(bf16[64,4,8,128]{3,2,1,0:T(8,128)(2,1)S(1)} %all_to_all.11.source_ref), custom_call_target="tpu_custom_call" | custom-call | tf_op jit(solution)/shard_map/pallas_call | solution.py:351
Async XLA Ops:
  36.2 7.1 %collective-permute-start.2 = (bf16[2,144,256]{2,1,0:T(8,128)(2,1)S(1)}, bf16[2,144,256]{2,1,0:T(8,128)(2,1)S(1)}, u32[]{:S(2)}, u32[]{:S(2)}) collective-permute-start(bf16[2,144,256]{2,1,0:T(8,128)(2,1)S(1)} %get-tuple-element.26), channel_id=1, source_target_pairs={{1,0},{2,1},{3,2},{5,4},{6,5},{7,6},{9,8},{10,9},{11,10},{13,12},{... | collective-permute-start | bytes 442376 | tf_op jit(solution)/shard_map/ppermute | solution.py:332
  37.5 7.7 %collective-permute-start = (bf16[2,144,256]{2,1,0:T(8,128)(2,1)S(1)}, bf16[2,144,256]{2,1,0:T(8,128)(2,1)S(1)}, u32[]{:S(2)}, u32[]{:S(2)}) collective-permute-start(bf16[2,144,256]{2,1,0:T(8,128)(2,1)S(1)} %get-tuple-element.22), channel_id=1, source_target_pairs={{4,0},{8,4},{12,8},{16,12},{20,16},{24,20},{28,24},{32,28},{36,32}... | collective-permute-start | bytes 442376 | tf_op jit(solution)/shard_map/ppermute | solution.py:334
  37.8 7.4 %collective-permute-start.1 = (bf16[1,144,256]{2,1,0:T(8,128)(2,1)S(1)}, bf16[1,144,256]{2,1,0:T(8,128)(2,1)S(1)}, u32[]{:S(2)}, u32[]{:S(2)}) collective-permute-start(bf16[1,144,256]{2,1,0:T(8,128)(2,1)S(1)} %get-tuple-element.23), channel_id=1, source_target_pairs={{5,0},{6,1},{7,2},{9,4},{10,5},{11,6},{13,8},{14,9},{15,10},{17,12... | collective-permute-start | bytes 221192 | tf_op jit(solution)/shard_map/ppermute | solution.py:333

commit v12 on v10

--- a/solution.py
+++ b/solution.py
@@ -136,7 +136,7 @@
     half = members // 2
     small_row = lax.broadcasted_iota(jnp.int32, (half, half), 0)
     small_col = lax.broadcasted_iota(jnp.int32, (half, half), 1)
-    tail_row = lax.broadcasted_iota(jnp.int32, (16, members), 0)
+    tail_row = lax.broadcasted_iota(jnp.int32, (8, members), 0)
     corner = spread[half:, half:]
     target[slot, :half, :half] = jnp.where(small_row >= small_col, spread[:half, :half], corner).astype(BF16)
     target[slot, :half, half:] = spread[:half, half:].astype(BF16)
@@ -148,7 +148,7 @@
 
 
 def unpack(source, slot, target, place):
-    half = source.shape[1] - 16
+    half = source.shape[1] - 8
     row = lax.broadcasted_iota(jnp.int32, (half, half), 0)
     col = lax.broadcasted_iota(jnp.int32, (half, half), 1)
     mixed = source[slot, :half, :half].astype(F32)
@@ -164,9 +164,11 @@
     target[place, half:, half:] = (corner + right).astype(BF16)
 
 
-def first_kernel(
-    ensemble_ref, dense_ref, value_ref, out_ref, beside_ref, corner_ref, below_ref, x_ref, pert_ref, high_ref, centre_ref, wide_ref, left_high, left_low
-):
+def first_kernel(*refs):
+    ensemble_ref, small, sums = refs[0], refs[1:8], refs[8:11]
+    out_ref, beside_ref, corner_ref, below_ref, x_ref, pert_ref, high_ref, centre_ref, wide_ref, left_high, left_low = refs[11:]
+    dense_ref, value_ref, _ = sums
+    prepare(*small, *sums)
     members, patches, fields = ensemble_ref.shape
     total = jnp.zeros((patches, fields), F32)
     chunk = 32
@@ -249,16 +251,12 @@
 
 
 def entry_kernel(*refs):
-    small, source_ref, target_ref, results = refs[:7], refs[7], refs[8], refs[9:12]
-    copied, loaded, read = refs[12:19], refs[19], refs[20]
-    fetch = [pltpu.make_async_copy(a, b, loaded.at[i]) for i, (a, b) in enumerate(zip(small, copied))]
-    inward = [pltpu.make_async_copy(source_ref.at[m], target_ref.at[:, m], read.at[m]) for m in range(source_ref.shape[0])]
-    for copy in fetch + inward:
+    source_ref, small, target_ref, copied, read, loaded = refs[0], refs[1:8], refs[8], refs[9:16], refs[16], refs[17]
+    copies = [pltpu.make_async_copy(a, b, loaded.at[i]) for i, (a, b) in enumerate(zip(small, copied))]
+    copies += [pltpu.make_async_copy(source_ref.at[m], target_ref.at[:, m], read.at[m]) for m in range(source_ref.shape[0])]
+    for copy in copies:
         copy.start()
-    for copy in fetch:
-        copy.wait()
-    prepare(*copied, *results)
-    for copy in inward:
+    for copy in copies:
         copy.wait()
 
 
@@ -294,29 +292,29 @@
 
     blocks = (devices, own, patches, fields)
     small = (obs_count, obs_value, obs_error, obs_patch, obs_variable, patch_corners[0].T, interp_weights[0].T)
-    given = [pltpu.with_memory_space_constraint(x, pltpu.HBM) for x in small + (background.reshape(own, devices, patches, fields),)]
     sums = (points, patches, fields)
-    outgoing, dense, values, mix = pl.pallas_call(
+    given = [pltpu.with_memory_space_constraint(x, pltpu.HBM) for x in (background.reshape(own, devices, patches, fields),) + small]
+    outgoing, *small = call(
         entry_kernel,
-        out_shape=(shape(blocks, BF16), shape(sums, F32), shape(sums, F32), shape((9, patches, fields), F32)),
-        in_specs=[HBM] * 8,
-        out_specs=(VMEM, VMEM, VMEM, VMEM),
-        scratch_shapes=[pltpu.VMEM(x.shape, x.dtype) for x in small]
-        + [pltpu.SemaphoreType.DMA((len(small),)), pltpu.SemaphoreType.DMA((own,))],
-        compiler_params=pltpu.CompilerParams(vmem_limit_bytes=32 << 20),
+        (shape(blocks, BF16),) + tuple(shape(x.shape, x.dtype) for x in small),
+        [HBM] * 8,
+        copies + [pltpu.SemaphoreType.DMA((len(small),))],
     )(*given)
     ensemble = lax.all_to_all(outgoing, "mem", split_axis=0, concat_axis=0, tiled=True).reshape(members, patches, fields)
 
-    packed = (members // 2 + 16, members)
+    packed = (members // 2 + 8, members)
     left = (members + 16, columns)
     flat = (members, columns)
     wide = pltpu.VMEM((members * patches, fields), F32)
     down = [((d + 1) % devices, d) for d in range(devices)]
     across = [(r + 1, r) for r in range(regions - 1)]
     both = [(d * regions + r, e * regions + t) for d, e in down for r, t in across]
-    one, to_beside, to_corner, to_below, x, pert, high, centre = call(
+    dense, values, mix, one, to_beside, to_corner, to_below, x, pert, high, centre = call(
         first_kernel,
         (
+            shape(sums, F32),
+            shape(sums, F32),
+            shape((9, patches, fields), F32),
             shape((3, members, members), BF16),
             shape((2,) + packed, BF16),
             shape((1,) + packed, BF16),
@@ -326,9 +324,9 @@
             shape(flat, BF16),
             shape((patches, fields), F32),
         ),
-        [VMEM] * 3,
+        [VMEM] * 8,
         [wide] + [pltpu.VMEM((3,) + left, BF16)] * 2,
-    )(ensemble, dense, values)
+    )(ensemble, *small)
     beside = lax.ppermute(to_beside, "reg", across)
     diagonal = lax.ppermute(to_corner, ("mem", "reg"), both)
     below = lax.ppermute(to_below, "mem", down)

time: 71.7 us -> 71.7 us (level)
  no operation moved by 1% of the time
where the time goes in v12:
time: 71.7 us; the launch traced here: 71.1 us
  blocking collectives  54.7 us (76%)
  Pallas kernels  11.3 us (16%)
  starting transfers between devices  2.87 us (4%)
  waiting for transfers between devices  2.2 us (3%)
    all_to_all x1, blocking collectives, per_device(): lax.all_to_all(outgoing, 'mem', split_axis=0, concat_axis=0, tiled=True)  30.1 us
    all_to_all x1, blocking collectives, per_device(): lax.all_to_all(analysis.reshape(devices, own, patches, fields), 'mem', sp...  24.7 us
    pallas_call x1, Pallas kernels, per_device(): call(first_kernel, (shape(sums, F32), shape(sums, F32), shape((9, patches...  4.87 us
    pallas_call x1, Pallas kernels, per_device(): call(second_kernel, (shape(flat, F32), shape((1, members, members), BF16)...  2.83 us
  transfers between devices with their start and end apart: 3, of which 2 were waited for; matrix products, arithmetic and copies ran while one was open for 0% of the time, Pallas kernels for 5%

profile of v12, /device:TPU:1, one launch (start us, length us, event | category | flops | bytes accessed | tf_op | source)
XLA Modules:
  0.0 71.1 jit_solution(13510873820470348165)
XLA Ops:
  0.0 1.3 %shard_map.82 = (bf16[64,4,8,128]{3,2,1,0:T(8,128)(2,1)S(1)}, s32[2,2]{1,0:T(2,128)S(1)}, f32[2,2,512]{2,1,0:T(2,128)S(1)}, f32[2,2,512]{2,1,0:T(2,128)S(1)}, s3...) custom-call(bf16[4,64,8,128]{3,2,1,0:T(8,128)(2,1)} %bitcast.14, ...), custom_call_target="tpu_custom_call" | custom-call | tf_op jit(solution)/shard_map/pallas_call | solution.py:297
  1.3 30.1 %all_to_all.10 = bf16[64,4,8,128]{3,2,1,0:T(8,128)(2,1)S(1)} all-to-all(bf16[64,4,8,128]{3,2,1,0:T(8,128)(2,1)S(1)} %get-tuple-element.26), channel_id=1, replica_groups=mesh['mem'=64,'reg'=4] {'mem'}, dimensions={0} | all-to-all | bytes 1048576 | tf_op jit(solution)/shard_map/all_to_all | solution.py:303
  31.4 4.9 %shard_map.83 = (f32[4,8,128]{2,1,0:T(8,128)S(1)}, f32[4,8,128]{2,1,0:T(8,128)S(1)}, f32[9,8,128]{2,1,0:T(8,128)S(1)}, bf16[3,256,256]{2,1,0:T(8,128)(2,1)S(1)},...) custom-call(bf16[256,8,128]{2,1,0:T(8,128)(2,1)S(1)} %bitcast.12, ...), custom_call_target="tpu_custom_call" | custom-call | tf_op jit(solution)/shard_map/pallas_call | solution.py:312
  36.2 1.3 %collective-permute-start.1 = (bf16[2,136,256]{2,1,0:T(8,128)(2,1)S(1)}, bf16[2,136,256]{2,1,0:T(8,128)(2,1)S(1)}, u32[]{:S(2)}, u32[]{:S(2)}) collective-permute-start(bf16[2,136,256]{2,1,0:T(8,128)(2,1)S(1)} %get-tuple-element.37), channel_id=1, source_target_pairs={{1,0},{2,1},{3,2},{5,4},{6,5},{7,6},{9,8},{10,9},{11,10},{13,12},{... | collective-permute-start | bytes 417800 | tf_op jit(solution)/shard_map/ppermute | solution.py:330
  37.5 0.3 collective-permute-start.2
  37.8 1.3 %collective-permute-start = (bf16[1,136,256]{2,1,0:T(8,128)(2,1)S(1)}, bf16[1,136,256]{2,1,0:T(8,128)(2,1)S(1)}, u32[]{:S(2)}, u32[]{:S(2)}) collective-permute-start(bf16[1,136,256]{2,1,0:T(8,128)(2,1)S(1)} %get-tuple-element.34), channel_id=1, source_target_pairs={{5,0},{6,1},{7,2},{9,4},{10,5},{11,6},{13,8},{14,9},{15,10},{17,12... | collective-permute-start | bytes 208904 | tf_op jit(solution)/shard_map/ppermute | solution.py:331
  39.1 2.8 %shard_map.84 = (f32[256,1024]{1,0:T(8,128)S(1)}, bf16[1,256,256]{2,1,0:T(8,128)(2,1)S(1)}) custom-call(bf16[256,1024]{1,0:T(8,128)(2,1)S(1)} %get-tuple-element.39.x_ref, f32[256,1024]{1,0:T(8,128)S(1)} %get-tuple-element.40.pert_ref, f32[8,128]{1,0:T(8,128)S(1)} %get-tuple-element.41.centre_ref, f32[4,8,128]{2,1,0:T(8,128)S(1)} %get-tuple-element.42.dense_ref, ...), custom_call_target="tpu_custom_call" | custom-call | tf_op jit(solution)/shard_map/pallas_call | solution.py:333
  41.9 1.2 %collective-permute-done.1.beside_ref = bf16[2,136,256]{2,1,0:T(8,128)(2,1)S(1)} collective-permute-done((bf16[2,136,256]{2,1,0:T(8,128)(2,1)S(1)}, bf16[2,136,256]{2,1,0:T(8,128)(2,1)S(1)}, u32[]{:S(2)}, u32[]{:S(2)}) %collective-permute-start.1) | collective-permute-done | bytes 139296 | tf_op jit(solution)/shard_map/ppermute | solution.py:330
  43.1 0.0 collective-permute-done.2.below_ref
  43.1 1.0 %shard_map.85.partial_ref = f32[256,1024]{1,0:T(8,128)S(1)} custom-call(bf16[2,136,256]{2,1,0:T(8,128)(2,1)S(1)} %collective-permute-done.1.beside_ref, bf16[2,136,256]{2,1,0:T(8,128)(2,1)S(1)} %collective-permute-done.2.below_ref, bf16[1,256,256]{2,1,0:T(8,128)(2,1)S(1)} %get-tuple-element.45.two_ref, bf16[256,1024]{1,0:T(8,128)(2,1)S(1)} %get-tuple-element.35.high_ref, ...), custom_call_target="tpu_custom_call" | custom-call | tf_op jit(solution)/shard_map/pallas_call | solution.py:339
  44.1 1.0 %collective-permute-done.diagonal_ref = bf16[1,136,256]{2,1,0:T(8,128)(2,1)S(1)} collective-permute-done((bf16[1,136,256]{2,1,0:T(8,128)(2,1)S(1)}, bf16[1,136,256]{2,1,0:T(8,128)(2,1)S(1)}, u32[]{:S(2)}, u32[]{:S(2)}) %collective-permute-start) | collective-permute-done | bytes 69664 | tf_op jit(solution)/shard_map/ppermute | solution.py:331
  45.1 0.5 shard_map.86
  45.6 24.7 %all_to_all.11.source_ref = bf16[64,4,8,128]{3,2,1,0:T(8,128)(2,1)S(1)} all-to-all(bf16[64,4,8,128]{3,2,1,0:T(8,128)(2,1)S(1)} %bitcast.13), channel_id=1, replica_groups=mesh['mem'=64,'reg'=4] {'mem'}, dimensions={0} | all-to-all | bytes 1048576 | tf_op jit(solution)/shard_map/all_to_all | solution.py:348
  70.3 0.8 %shard_map.87 = bf16[4,64,8,128]{3,2,1,0:T(8,128)(2,1)} custom-call(bf16[64,4,8,128]{3,2,1,0:T(8,128)(2,1)S(1)} %all_to_all.11.source_ref), custom_call_target="tpu_custom_call" | custom-call | tf_op jit(solution)/shard_map/pallas_call | solution.py:349
Async XLA Ops:
  36.2 6.9 %collective-permute-start.1 = (bf16[2,136,256]{2,1,0:T(8,128)(2,1)S(1)}, bf16[2,136,256]{2,1,0:T(8,128)(2,1)S(1)}, u32[]{:S(2)}, u32[]{:S(2)}) collective-permute-start(bf16[2,136,256]{2,1,0:T(8,128)(2,1)S(1)} %get-tuple-element.37), channel_id=1, source_target_pairs={{1,0},{2,1},{3,2},{5,4},{6,5},{7,6},{9,8},{10,9},{11,10},{13,12},{... | collective-permute-start | bytes 417800 | tf_op jit(solution)/shard_map/ppermute | solution.py:330
  37.5 5.6 %collective-permute-start.2 = (bf16[2,136,256]{2,1,0:T(8,128)(2,1)S(1)}, bf16[2,136,256]{2,1,0:T(8,128)(2,1)S(1)}, u32[]{:S(2)}, u32[]{:S(2)}) collective-permute-start(bf16[2,136,256]{2,1,0:T(8,128)(2,1)S(1)} %get-tuple-element.38), channel_id=1, source_target_pairs={{4,0},{8,4},{12,8},{16,12},{20,16},{24,20},{28,24},{32,28},{36,32}... | collective-permute-start | bytes 417800 | tf_op jit(solution)/shard_map/ppermute | solution.py:332
  37.8 7.3 %collective-permute-start = (bf16[1,136,256]{2,1,0:T(8,128)(2,1)S(1)}, bf16[1,136,256]{2,1,0:T(8,128)(2,1)S(1)}, u32[]{:S(2)}, u32[]{:S(2)}) collective-permute-start(bf16[1,136,256]{2,1,0:T(8,128)(2,1)S(1)} %get-tuple-element.34), channel_id=1, source_target_pairs={{5,0},{6,1},{7,2},{9,4},{10,5},{11,6},{13,8},{14,9},{15,10},{17,12... | collective-permute-start | bytes 208904 | tf_op jit(solution)/shard_map/ppermute | solution.py:331

commit v13 on v12

--- a/solution.py
+++ b/solution.py
@@ -34,7 +34,7 @@
     return dot(a[0], b[0]) + (dot(a[0], b[1]) + dot(a[1], b[0]))
 
 
-def prepare(count_ref, value_ref, error_ref, patch_ref, var_ref, corner_ref, coeff_ref, dense_ref, value_out_ref, mix_ref):
+def prepare(chosen_points, count_ref, value_ref, error_ref, patch_ref, var_ref, dense_ref, value_out_ref):
     rows, cols, slots = value_ref.shape
     patches, fields = dense_ref.shape[1:]
     slot_index = lax.broadcasted_iota(jnp.int32, (1, slots), 1)
@@ -42,6 +42,8 @@
     patch_index = lax.broadcasted_iota(jnp.int32, (patches, slots), 0)
     for a in range(rows):
         for b in range(cols):
+            if a * cols + b not in chosen_points:
+                continue
             weight = jnp.where(slot_index < count_ref[a : a + 1, b : b + 1], 1.0 / error_ref[a, b : b + 1, :], 0.0)
             weighted = weight * value_ref[a, b : b + 1, :]
             chosen = (field_index == var_ref[a, b : b + 1, :]).astype(F32).astype(BF16)
@@ -51,6 +53,10 @@
             sums = high + (middle + low)
             dense_ref[a * cols + b] = sums[:patches]
             value_out_ref[a * cols + b] = sums[patches:]
+
+
+def mix(corner_ref, coeff_ref, mix_ref):
+    patches, fields = mix_ref.shape[1:]
     corners, coeffs = corner_ref[...], coeff_ref[...]
     square = (patches, patches)
     own_place = lax.broadcasted_iota(jnp.int32, square, 0) == lax.broadcasted_iota(jnp.int32, square, 1)
@@ -165,10 +171,9 @@
 
 
 def first_kernel(*refs):
-    ensemble_ref, small, sums = refs[0], refs[1:8], refs[8:11]
-    out_ref, beside_ref, corner_ref, below_ref, x_ref, pert_ref, high_ref, centre_ref, wide_ref, left_high, left_low = refs[11:]
-    dense_ref, value_ref, _ = sums
-    prepare(*small, *sums)
+    ensemble_ref, small = refs[0], refs[1:6]
+    out_ref, beside_ref, corner_ref, below_ref, x_ref, pert_ref, high_ref, centre_ref, dense_ref, value_ref, wide_ref, left_high, left_low = refs[6:]
+    prepare((0, 1, 2), *small, dense_ref, value_ref)
     members, patches, fields = ensemble_ref.shape
     total = jnp.zeros((patches, fields), F32)
     chunk = 32
@@ -195,7 +200,11 @@
             pack(below_ref if slot == 1 else beside_ref, 1, spread, twice)
 
 
-def second_kernel(x_ref, pert_ref, centre_ref, dense_ref, value_ref, one_ref, high_ref, mix_ref, out_ref, two_ref, left_high, left_low):
+def second_kernel(*refs):
+    x_ref, pert_ref, centre_ref, one_ref, high_ref = refs[:5]
+    small, out_ref, two_ref, mix_ref, dense_ref, value_ref, left_high, left_low = refs[5:12], *refs[12:]
+    prepare((3,), *small[:5], dense_ref, value_ref)
+    mix(*small[5:], mix_ref)
     patches, fields = centre_ref.shape
     tiles = iter(range(0, patches, 2))
 
@@ -309,12 +318,9 @@
     down = [((d + 1) % devices, d) for d in range(devices)]
     across = [(r + 1, r) for r in range(regions - 1)]
     both = [(d * regions + r, e * regions + t) for d, e in down for r, t in across]
-    dense, values, mix, one, to_beside, to_corner, to_below, x, pert, high, centre = call(
+    one, to_beside, to_corner, to_below, x, pert, high, centre = call(
         first_kernel,
         (
-            shape(sums, F32),
-            shape(sums, F32),
-            shape((9, patches, fields), F32),
             shape((3, members, members), BF16),
             shape((2,) + packed, BF16),
             shape((1,) + packed, BF16),
@@ -324,27 +330,27 @@
             shape(flat, BF16),
             shape((patches, fields), F32),
         ),
-        [VMEM] * 8,
-        [wide] + [pltpu.VMEM((3,) + left, BF16)] * 2,
-    )(ensemble, *small)
+        [VMEM] * 6,
+        [pltpu.VMEM(sums, F32)] * 2 + [wide] + [pltpu.VMEM((3,) + left, BF16)] * 2,
+    )(ensemble, *small[:5])
     beside = lax.ppermute(to_beside, "reg", across)
     diagonal = lax.ppermute(to_corner, ("mem", "reg"), both)
     below = lax.ppermute(to_below, "mem", down)
-    partial, two = call(
+    partial, two, shared = call(
         second_kernel,
-        (shape(flat, F32), shape((1, members, members), BF16)),
-        [VMEM] * 8,
-        [pltpu.VMEM((1,) + left, BF16)] * 2,
-    )(x, pert, centre, dense, values, one, high, mix)
+        (shape(flat, F32), shape((1, members, members), BF16), shape((9, patches, fields), F32)),
+        [VMEM] * 12,
+        [pltpu.VMEM(sums, F32)] * 2 + [pltpu.VMEM((1,) + left, BF16)] * 2,
+    )(x, pert, centre, one, high, *small)
     partial = call(middle_kernel, shape(flat, F32), [VMEM] * 6, [pltpu.VMEM((4, members, members), BF16)])(
-        beside, below, two, high, mix, partial
+        beside, below, two, high, shared, partial
     )
     analysis = call(
         last_kernel,
         shape((members, patches, fields), BF16),
         [VMEM] * 5,
         [wide, pltpu.VMEM((1, members, members), BF16)],
-    )(diagonal, high, mix, partial, centre)
+    )(diagonal, high, shared, partial, centre)
     returned = lax.all_to_all(analysis.reshape(devices, own, patches, fields), "mem", split_axis=0, concat_axis=0, tiled=True)
     result = call(returned_kernel, shape((own, devices, patches, fields), BF16), [VMEM], copies, HBM)(returned)
     return result.reshape(own, 1, all_patches, fields)

time: 71.7 us -> 72 us (level)
  waiting for transfers between devices: 2.2 us -> 1.48 us
    pallas_call x1, Pallas kernels: 2.83 us -> 3.55 us  [per_device(): call(second_kernel, (shape(flat, F32), shape((1, members, members), BF16)...]
    ppermute x1, waiting for transfers between devices: 1.19 us -> 0.47 us  [per_device(): beside = lax.ppermute(to_beside, 'reg', across)]
  transfers between devices with their start and end apart: 3 -> 3, of which waited for: 2 -> 2; matrix products, arithmetic and copies ran while one was open for 0% -> 0% of each run, Pallas kernels for 5% -> 6%
where the time goes in v13:
time: 72 us; the launch traced here: 70.8 us
  blocking collectives  54.7 us (76%)
  Pallas kernels  11.6 us (16%)
  starting transfers between devices  2.86 us (4%)
  waiting for transfers between devices  1.48 us (2%)
    all_to_all x1, blocking collectives, per_device(): lax.all_to_all(outgoing, 'mem', split_axis=0, concat_axis=0, tiled=True)  30.1 us
    all_to_all x1, blocking collectives, per_device(): lax.all_to_all(analysis.reshape(devices, own, patches, fields), 'mem', sp...  24.7 us
    pallas_call x1, Pallas kernels, per_device(): call(first_kernel, (shape((3, members, members), BF16), shape((2,) + pack...  4.53 us
    pallas_call x1, Pallas kernels, per_device(): call(second_kernel, (shape(flat, F32), shape((1, members, members), BF16)...  3.55 us
  transfers between devices with their start and end apart: 3, of which 2 were waited for; matrix products, arithmetic and copies ran while one was open for 0% of the time, Pallas kernels for 6%

profile of v13, /device:TPU:1, one launch (start us, length us, event | category | flops | bytes accessed | tf_op | source)
XLA Modules:
  0.0 70.8 jit_solution(8711755592116285151)
XLA Ops:
  0.0 1.3 %shard_map.82 = (bf16[64,4,8,128]{3,2,1,0:T(8,128)(2,1)S(1)}, s32[2,2]{1,0:T(2,128)S(1)}, f32[2,2,512]{2,1,0:T(2,128)S(1)}, f32[2,2,512]{2,1,0:T(2,128)S(1)}, s3...) custom-call(bf16[4,64,8,128]{3,2,1,0:T(8,128)(2,1)} %bitcast.14, ...), custom_call_target="tpu_custom_call" | custom-call | tf_op jit(solution)/shard_map/pallas_call | solution.py:306
  1.3 30.1 %all_to_all.10 = bf16[64,4,8,128]{3,2,1,0:T(8,128)(2,1)S(1)} all-to-all(bf16[64,4,8,128]{3,2,1,0:T(8,128)(2,1)S(1)} %get-tuple-element.24), channel_id=1, replica_groups=mesh['mem'=64,'reg'=4] {'mem'}, dimensions={0} | all-to-all | bytes 1048576 | tf_op jit(solution)/shard_map/all_to_all | solution.py:312
  31.4 4.5 %shard_map.83 = (bf16[3,256,256]{2,1,0:T(8,128)(2,1)S(1)}, bf16[2,136,256]{2,1,0:T(8,128)(2,1)S(1)}, bf16[1,136,256]{2,1,0:T(8,128)(2,1)S(1)}, bf16[2,136,256]{2...) custom-call(bf16[256,8,128]{2,1,0:T(8,128)(2,1)S(1)} %bitcast.12, ...), custom_call_target="tpu_custom_call" | custom-call | tf_op jit(solution)/shard_map/pallas_call | solution.py:321
  35.9 1.3 %collective-permute-start.1 = (bf16[2,136,256]{2,1,0:T(8,128)(2,1)S(1)}, bf16[2,136,256]{2,1,0:T(8,128)(2,1)S(1)}, u32[]{:S(2)}, u32[]{:S(2)}) collective-permute-start(bf16[2,136,256]{2,1,0:T(8,128)(2,1)S(1)} %get-tuple-element.39), channel_id=1, source_target_pairs={{1,0},{2,1},{3,2},{5,4},{6,5},{7,6},{9,8},{10,9},{11,10},{13,12},{... | collective-permute-start | bytes 417800 | tf_op jit(solution)/shard_map/ppermute | solution.py:336
  37.2 0.3 collective-permute-start.2
  37.5 1.3 %collective-permute-start = (bf16[1,136,256]{2,1,0:T(8,128)(2,1)S(1)}, bf16[1,136,256]{2,1,0:T(8,128)(2,1)S(1)}, u32[]{:S(2)}, u32[]{:S(2)}) collective-permute-start(bf16[1,136,256]{2,1,0:T(8,128)(2,1)S(1)} %get-tuple-element.30), channel_id=1, source_target_pairs={{5,0},{6,1},{7,2},{9,4},{10,5},{11,6},{13,8},{14,9},{15,10},{17,12... | collective-permute-start | bytes 208904 | tf_op jit(solution)/shard_map/ppermute | solution.py:337
  38.8 3.6 %shard_map.84 = (f32[256,1024]{1,0:T(8,128)S(1)}, bf16[1,256,256]{2,1,0:T(8,128)(2,1)S(1)}, f32[9,8,128]{2,1,0:T(8,128)S(1)}) custom-call(bf16[256,1024]{1,0:T(8,128)(2,1)S(1)} %get-tuple-element.32.refs_0_, f32[256,1024]{1,0:T(8,128)S(1)} %get-tuple-element.33.refs_1_, f32[8,128]{1,0:T(8,128)S(1)} %get-tuple-element.34.refs_2_.centre_ref, ...), custom_call_target="tpu_custom_call" | custom-call | tf_op jit(solution)/shard_map/pallas_call | solution.py:339
  42.3 0.5 collective-permute-done.1.beside_ref
  42.8 0.0 collective-permute-done.2.below_ref
  42.8 1.0 %shard_map.85.partial_ref = f32[256,1024]{1,0:T(8,128)S(1)} custom-call(bf16[2,136,256]{2,1,0:T(8,128)(2,1)S(1)} %collective-permute-done.1.beside_ref, bf16[2,136,256]{2,1,0:T(8,128)(2,1)S(1)} %collective-permute-done.2.below_ref, bf16[1,256,256]{2,1,0:T(8,128)(2,1)S(1)} %get-tuple-element.41.two_ref, ...), custom_call_target="tpu_custom_call" | custom-call | tf_op jit(solution)/shard_map/pallas_call | solution.py:345
  43.8 1.0 %collective-permute-done.diagonal_ref = bf16[1,136,256]{2,1,0:T(8,128)(2,1)S(1)} collective-permute-done((bf16[1,136,256]{2,1,0:T(8,128)(2,1)S(1)}, bf16[1,136,256]{2,1,0:T(8,128)(2,1)S(1)}, u32[]{:S(2)}, u32[]{:S(2)}) %collective-permute-start) | collective-permute-done | bytes 69664 | tf_op jit(solution)/shard_map/ppermute | solution.py:337
  44.8 0.5 shard_map.86
  45.3 24.7 %all_to_all.11.source_ref = bf16[64,4,8,128]{3,2,1,0:T(8,128)(2,1)S(1)} all-to-all(bf16[64,4,8,128]{3,2,1,0:T(8,128)(2,1)S(1)} %bitcast.13), channel_id=1, replica_groups=mesh['mem'=64,'reg'=4] {'mem'}, dimensions={0} | all-to-all | bytes 1048576 | tf_op jit(solution)/shard_map/all_to_all | solution.py:354
  69.9 0.8 %shard_map.87 = bf16[4,64,8,128]{3,2,1,0:T(8,128)(2,1)} custom-call(bf16[64,4,8,128]{3,2,1,0:T(8,128)(2,1)S(1)} %all_to_all.11.source_ref), custom_call_target="tpu_custom_call" | custom-call | tf_op jit(solution)/shard_map/pallas_call | solution.py:355
Async XLA Ops:
  35.9 6.9 %collective-permute-start.1 = (bf16[2,136,256]{2,1,0:T(8,128)(2,1)S(1)}, bf16[2,136,256]{2,1,0:T(8,128)(2,1)S(1)}, u32[]{:S(2)}, u32[]{:S(2)}) collective-permute-start(bf16[2,136,256]{2,1,0:T(8,128)(2,1)S(1)} %get-tuple-element.39), channel_id=1, source_target_pairs={{1,0},{2,1},{3,2},{5,4},{6,5},{7,6},{9,8},{10,9},{11,10},{13,12},{... | collective-permute-start | bytes 417800 | tf_op jit(solution)/shard_map/ppermute | solution.py:336
  37.2 5.6 %collective-permute-start.2 = (bf16[2,136,256]{2,1,0:T(8,128)(2,1)S(1)}, bf16[2,136,256]{2,1,0:T(8,128)(2,1)S(1)}, u32[]{:S(2)}, u32[]{:S(2)}) collective-permute-start(bf16[2,136,256]{2,1,0:T(8,128)(2,1)S(1)} %get-tuple-element.40), channel_id=1, source_target_pairs={{4,0},{8,4},{12,8},{16,12},{20,16},{24,20},{28,24},{32,28},{36,32}... | collective-permute-start | bytes 417800 | tf_op jit(solution)/shard_map/ppermute | solution.py:338
  37.5 7.3 %collective-permute-start = (bf16[1,136,256]{2,1,0:T(8,128)(2,1)S(1)}, bf16[1,136,256]{2,1,0:T(8,128)(2,1)S(1)}, u32[]{:S(2)}, u32[]{:S(2)}) collective-permute-start(bf16[1,136,256]{2,1,0:T(8,128)(2,1)S(1)} %get-tuple-element.30), channel_id=1, source_target_pairs={{5,0},{6,1},{7,2},{9,4},{10,5},{11,6},{13,8},{14,9},{15,10},{17,12... | collective-permute-start | bytes 208904 | tf_op jit(solution)/shard_map/ppermute | solution.py:337
